TPU v7x, 512 devices: a whole 4x4x16 slice. The times are simulated.
512 devices in a mesh: wide: 64 (over x, y, z_hi, core), narrow: 8 (over z_lo).
Axes of the slice: x: 4, y: 4, z: 16 (z_hi: 2, z_lo: 8; z = z_hi * 8 + z_lo), core: 2. Of those that a mesh axis runs over, the one named last changes fastest.
Arguments:
- electric: float32 [3, 3, 512, 192, 128], P(None, None, 'wide', 'narrow'), may hold values from -6 to 6
- magnetic: float32 [3, 3, 512, 192, 128], P(None, None, 'wide', 'narrow'), may hold values from -6 to 6
- current: float32 [3, 512, 192, 128], P(None, 'wide', 'narrow'), may hold values from -6 to 6
- density_tiles: float32 [256, 96, 64], P('wide', 'narrow'), may hold values from 0 to 1
- tile_slabs: int32 [64], replicated, may hold values from 0 to 63, each once
- design_box: int32 [6], replicated, may hold values from 0 to 512, as said below
- material_mask: int32 [512, 192, 128], P('wide', 'narrow'), may hold values 0 or 1
- material_levels: float32 [2], replicated, may hold values from 2 to 12
Outputs:
- final_electric: float32 [3, 3, 512, 192, 128], P(None, None, 'wide', 'narrow')
- final_magnetic: float32 [3, 3, 512, 192, 128], P(None, None, 'wide', 'narrow')
Inputs may be any that keep to these rules, and one draw needn't show every extreme that they name: `tile_slabs`: each slab index appears exactly once. `design_box`: along each dimension of n cells the low bound is below n // 4; the high bound is 512 along the first dimension, at least 168 along the second, and at least n // 2 along the third.
All inputs are finite; a program needn't handle non-finite values. No bound on the sum of `material_mask` on one device may be relied on, other than what follows from the above.
Results may differ from a plain program's by a relative error of at most 0.00013.
Values sent between devices are 32-bit elements; how exact they have to be, the bound alone decides.
No kernel may reach another device: no remote copies, remote signals or barrier semaphores. Data moves between devices by JAX's collectives and lax.ppermute only.
A program may use at most 64 MiB of HBM per device.

v0:
```python
import jax
import jax.numpy as jnp
from jax import lax
from jax.sharding import PartitionSpec as P

STEPS = 4


sharpness = 8.0
thresholds = (0.7, 0.5, 0.3)
time_step = 0.5


def sent_to_all(x, axis):
    copies = jnp.broadcast_to(x, (lax.axis_size(axis), *x.shape))
    return lax.all_to_all(copies, axis, split_axis=0, concat_axis=0, tiled=True)


def in_order(pieces, dim):
    pieces = jnp.moveaxis(pieces, 0, dim)
    lengths = pieces.shape
    return pieces.reshape(*lengths[:dim], lengths[dim] * lengths[dim + 1], *lengths[dim + 2 :])


def gathered_copies(x, axis, dim):
    pieces = sent_to_all(x, axis)
    return in_order(pieces, dim)


def from_behind(value, axis, steps):
    count = lax.axis_size(axis)
    first, last = (max(0, -steps), min(count, count - steps))
    return lax.ppermute(value, axis, [(source, source + steps) for source in range(first, last)])


def project(filtered, threshold):
    numer = jnp.tanh(sharpness * threshold) + jnp.tanh(sharpness * (filtered - threshold))
    denom = jnp.tanh(sharpness * threshold) + jnp.tanh(sharpness * (1.0 - threshold))
    return numer / denom


def refine(extended, dimension):
    cells_in = extended.shape[dimension] - 1
    lower_cells = lax.slice_in_dim(extended, 0, cells_in, axis=dimension)
    higher_cells = lax.slice_in_dim(extended, 1, cells_in + 1, axis=dimension)
    middle = 0.5 * (lower_cells + higher_cells)
    paired = jnp.stack([lower_cells, middle], axis=dimension + 1)
    new_shape = list(extended.shape)
    new_shape[dimension] = 2 * cells_in
    return paired.reshape(new_shape)


def forward(component, upper_face, dimension):
    length = component.shape[dimension]
    shifted_up = jnp.concatenate(
        [lax.slice_in_dim(component, 1, length, axis=dimension), upper_face], axis=dimension
    )
    return shifted_up - component


def backward(component, lower_face, dimension):
    length = component.shape[dimension]
    behind = jnp.concatenate(
        [lower_face, lax.slice_in_dim(component, 0, length - 1, axis=dimension)], axis=dimension
    )
    return component - behind


def curl(components, faces, difference):

    def slope(member, dimension):
        return difference(components[member], faces[dimension, member], dimension + 1)

    return [slope(2, 1) - slope(1, 2), slope(0, 2) - slope(2, 0), slope(1, 0) - slope(0, 1)]


def select_rows(selected, flat_rows):
    return jnp.dot(
        selected.astype(jnp.float32),
        flat_rows,
        precision=lax.Precision.HIGHEST,
        preferred_element_type=jnp.float32,
    )


def body(
    electric,
    magnetic,
    current,
    density_tiles,
    tile_slabs,
    design_box,
    material_mask,
    material_levels,
):
    wide_count = lax.axis_size("wide")
    wide_place = lax.axis_index("wide")
    narrow_count = lax.axis_size("narrow")
    narrow_place = lax.axis_index("narrow")
    tile_rows, half_y, half_z = density_tiles.shape
    flat_width = half_y * half_z
    slab_ids = jnp.arange(wide_count, dtype=jnp.int32)
    row_ids = jnp.arange(tile_rows, dtype=jnp.int32)
    portion = gathered_copies(density_tiles, "wide", 0)
    row_total = portion.shape[0]
    global_rows = jnp.arange(row_total, dtype=jnp.int32)
    tile_of_row = global_rows // tile_rows
    within = global_rows % tile_rows
    matches = (tile_of_row[:, None] == slab_ids[None, :]).astype(jnp.int32)
    owners = jnp.sum(matches * tile_slabs[None, :], axis=1)
    owners, within, flat_rows = (owners, within, portion.reshape(row_total, flat_width))
    own_select = (owners[None, :] == wide_place) & (within[None, :] == row_ids[:, None])
    own_flat = select_rows(own_select, flat_rows)
    own_block = own_flat.reshape(tile_rows, half_y, half_z)
    next_plane = from_behind(own_block[:1], "wide", -1)
    next_plane = jnp.where(wide_place == wide_count - 1, own_block[-1:], next_plane)
    refined_x = refine(jnp.concatenate([own_block, next_plane], axis=0), 0)
    next_row = from_behind(refined_x[:, :1], "narrow", -1)
    next_row = jnp.where(narrow_place == narrow_count - 1, refined_x[:, -1:], next_row)
    refined_y = refine(jnp.concatenate([refined_x, next_row], axis=1), 1)
    density = refine(jnp.concatenate([refined_y, refined_y[:, :, -1:]], axis=2), 2)
    projected = jnp.stack([project(density, threshold) for threshold in thresholds])
    cells_x, cells_y, cells_z = material_mask.shape
    global_x = wide_place * cells_x + jnp.arange(cells_x, dtype=jnp.int32)
    global_y = narrow_place * cells_y + jnp.arange(cells_y, dtype=jnp.int32)
    global_z = jnp.arange(cells_z, dtype=jnp.int32)
    inside = (
        ((global_x >= design_box[0]) & (global_x < design_box[1]))[:, None, None]
        & ((global_y >= design_box[2]) & (global_y < design_box[3]))[None, :, None]
        & ((global_z >= design_box[4]) & (global_z < design_box[5]))[None, None, :]
    )
    background = jnp.where(material_mask == 1, material_levels[1], material_levels[0])
    design = material_levels[0] + projected * (material_levels[1] - material_levels[0])
    permittivity = jnp.where(inside[None], design, background[None])
    coefficient = time_step / permittivity
    realizations = electric.shape[0]
    depth_zero = jnp.zeros((realizations, cells_x, cells_y, 1), jnp.float32)
    for iteration in range(STEPS):
        e_plane = from_behind(electric[:, 1:3, :1], "wide", -1)
        e_row = from_behind(
            jnp.stack([electric[:, 2, :, :1], electric[:, 0, :, :1]], axis=1), "narrow", -1
        )
        uppers = {
            (0, 1): e_plane[:, 0],
            (0, 2): e_plane[:, 1],
            (1, 2): e_row[:, 0],
            (1, 0): e_row[:, 1],
        }
        uppers[2, 0] = depth_zero
        uppers[2, 1] = depth_zero
        curl_e = curl([electric[:, member] for member in range(3)], uppers, forward)
        magnetic = jnp.stack(
            [magnetic[:, member] - time_step * curl_e[member] for member in range(3)], axis=1
        )
        h_plane = from_behind(magnetic[:, 1:3, -1:], "wide", 1)
        h_row = from_behind(
            jnp.stack([magnetic[:, 2, :, -1:], magnetic[:, 0, :, -1:]], axis=1), "narrow", 1
        )
        lowers = {
            (0, 1): h_plane[:, 0],
            (0, 2): h_plane[:, 1],
            (1, 2): h_row[:, 0],
            (1, 0): h_row[:, 1],
        }
        lowers[2, 0] = depth_zero
        lowers[2, 1] = depth_zero
        curl_h = curl([magnetic[:, member] for member in range(3)], lowers, backward)
        electric = jnp.stack(
            [
                electric[:, member] + coefficient * (curl_h[member] - current[member])
                for member in range(3)
            ],
            axis=1,
        )
    return (electric, magnetic)


def solution(mesh):
    return jax.shard_map(
        body,
        mesh=mesh,
        in_specs=(
            P(None, None, "wide", "narrow", None),
            P(None, None, "wide", "narrow", None),
            P(None, "wide", "narrow", None),
            P("wide", "narrow", None),
            P(),
            P(),
            P("wide", "narrow", None),
            P(),
        ),
        out_specs=(P(None, None, "wide", "narrow", None), P(None, None, "wide", "narrow", None)),
        check_vma=False,
    )
```

profile of v0, /device:TPU:6, one launch (start us, length us, event | category | flops | bytes accessed | tf_op | source)
XLA Modules:
  0.0 216.4 jit_solution(16255631924651366672)
XLA Ops:
  0.6 0.7 copy-done
  1.6 2.3 %reshape.202 = f32[64,1,3072]{2,1,0:T(1,128)} reshape(f32[64,12,4,64]{3,2,1,0:T(4,128)S(1)} %broadcast_bitcast_fusion) | data formatting | bytes 1572864
  4.0 21.6 %all-to-all-start = ((f32[64,1,3072]{2,1,0:T(1,128)}), f32[64,1,3072]{2,1,0:T(1,128)S(1)}, u32[]{:S(2)}, u32[]{:S(2)}) async-start(f32[64,1,3072]{2,1,0:T(1,128)} %reshape.202), calls=%async_computation | async-start | bytes 1572864 | tf_op jit(solution)/shard_map/all_to_all | solution.py:16
  25.6 1.3 collective-permute-start.3
  26.9 14.2 %collective-permute-start.2 = (f32[3,2,1,24,128]{4,3,2,0,1:T(8,128)S(1)}, f32[3,2,1,24,128]{4,3,2,0,1:T(8,128)}, u32[]{:S(2)}, u32[]{:S(2)}) collective-permute-start(f32[3,2,1,24,128]{4,3,2,0,1:T(8,128)S(1)} %copy.593), channel_id=1, source_target_pairs={{8,0},{16,8},{24,16},{32,24},{40,32},{48,40},{56,48},{64,56},{72,6... | collective-permute-start | bytes 221192 | tf_op jit(solution)/shard_map/ppermute | solution.py:33
  41.2 0.7 fusion.115
  41.9 1.2 compare_and_fusion
  43.2 1.3 compare_and_fusion.2
  44.5 1.3 compare_and_fusion.1
  45.8 0.6 fusion.116
  46.6 1.8 compare_select_fusion
  48.4 0.7 slice_bitcast_fusion.4
  49.1 0.8 slice_bitcast_fusion.30
  50.0 0.7 slice_bitcast_fusion.31
  50.7 0.6 and_select_fusion
  51.5 0.9 slice.556
  52.3 0.8 slice.550
  53.1 0.7 slice.557
  55.0 9.0 %collective-permute-done.3 = f32[3,2,8,1,128]{4,2,3,1,0:T(8,128)S(1)} collective-permute-done((f32[3,2,8,1,128]{4,2,3,1,0:T(8,128)S(1)}, f32[3,2,8,1,128]{4,2,3,1,0:T(8,128)S(1)}, u32[]{:S(2)}, u32[]{:S(2)}) %collective-permute-start.3) | collective-permute-done | bytes 24608 | tf_op jit(solution)/shard_map/ppermute | solution.py:33
  64.0 0.8 slice_bitcast_fusion.20
  64.8 1.9 fusion.18
  66.7 1.1 fusion.8
  67.9 2.2 %collective-permute-start.4 = (f32[3,2,8,1,128]{4,2,3,1,0:T(8,128)S(1)}, f32[3,2,8,1,128]{4,2,3,1,0:T(8,128)S(1)}, u32[]{:S(2)}, u32[]{:S(2)}) collective-permute-start(f32[3,2,8,1,128]{4,2,3,1,0:T(8,128)S(1)} %pad_maximum_fusion.16), channel_id=1, source_target_pairs={{0,1},{1,2},{2,3},{3,4},{4,5},{5,6},{6,7},{8,9},{9,10},{10,11},{11... | collective-permute-start | bytes 73736 | tf_op jit(solution)/shard_map/ppermute | solution.py:33
  70.1 0.7 slice.565
  70.8 0.6 pad_maximum_fusion.11
  71.4 12.2 %collective-permute-start.5 = (f32[3,2,1,24,128]{4,3,2,0,1:T(8,128)}, f32[3,2,1,24,128]{4,3,2,0,1:T(8,128)}, u32[]{:S(2)}, u32[]{:S(2)}) collective-permute-start(f32[3,2,1,24,128]{4,3,2,0,1:T(8,128)} %pad_maximum_fusion.11), channel_id=1, source_target_pairs={{0,8},{8,16},{16,24},{24,32},{32,40},{40,48},{48,56},{56,64},{64,7... | collective-permute-start | bytes 221192 | tf_op jit(solution)/shard_map/ppermute | solution.py:33
  83.6 0.7 slice.562
  84.3 0.6 broadcast.322
  84.9 3.6 %reduce.4 = f32[64,3072]{1,0:T(8,128)} reduce(f32[64,1,3072]{2,1,0:T(1,128)S(1)} %all-to-all-done, f32[]{:T(128)} %broadcast.322), dimensions={1}, to_apply=%all_to_all.3.reduce_sub_computation | reduce | bytes 1572868 | tf_op jit(solution)/shard_map/all_to_all | solution.py:16
  88.5 2.2 %reshape.203 = f32[64,12,4,64]{3,2,1,0:T(4,128)S(1)} reshape(f32[64,3072]{1,0:T(8,128)} %reduce.4) | data formatting | bytes 1572864
  90.7 1.6 copy.513
  92.3 2.0 reshape_reshape.3
  94.3 0.4 fusion.103
  94.8 5.2 %collective-permute-start = (f32[1,12,64]{2,1,0:T(8,128)S(1)}, f32[1,12,64]{2,1,0:T(8,128)S(1)}, u32[]{:S(2)}, u32[]{:S(2)}) collective-permute-start(f32[1,12,64]{2,1,0:T(8,128)S(1)} %slice.420), channel_id=1, source_target_pairs={{8,0},{16,8},{24,16},{32,24},{40,32},{48,40},{56,48},{64,56},{72,6... | collective-permute-start | bytes 9224 | tf_op jit(solution)/shard_map/ppermute | solution.py:33
  100.3 1.1 collective-permute-done
  101.5 1.3 collective-permute-start.1
  102.8 0.8 slice_bitcast_fusion.19
  103.6 3.4 %collective-permute-done.1 = f32[8,1,64]{2,0,1:T(8,128)S(1)} collective-permute-done((f32[8,1,64]{2,0,1:T(8,128)S(1)}, f32[8,1,64]{2,0,1:T(8,128)S(1)}, u32[]{:S(2)}, u32[]{:S(2)}) %collective-permute-start.1) | collective-permute-done | bytes 2080 | tf_op jit(solution)/shard_map/ppermute | solution.py:33
  107.9 0.3 copy.521
  108.4 0.3 copy.522
  108.9 1.7 fusion.15
  111.0 1.3 collective-permute-start.7
  112.7 14.2 %collective-permute-start.6 = (f32[3,2,1,24,128]{4,3,2,0,1:T(8,128)S(1)}, f32[3,2,1,24,128]{4,3,2,0,1:T(8,128)S(1)}, u32[]{:S(2)}, u32[]{:S(2)}) collective-permute-start(f32[3,2,1,24,128]{4,3,2,0,1:T(8,128)S(1)} %pad_maximum_fusion.10), channel_id=1, source_target_pairs={{8,0},{16,8},{24,16},{32,24},{40,32},{48,40},{56,48},{64,56},{72,6... | collective-permute-start | bytes 221192 | tf_op jit(solution)/shard_map/ppermute | solution.py:33
  126.9 1.9 collective-permute-done.6
  129.2 4.3 %collective-permute-start.8 = (f32[3,2,8,1,128]{4,2,3,1,0:T(8,128)S(1)}, f32[3,2,8,1,128]{4,2,3,1,0:T(8,128)S(1)}, u32[]{:S(2)}, u32[]{:S(2)}) collective-permute-start(f32[3,2,8,1,128]{4,2,3,1,0:T(8,128)S(1)} %pad_maximum_fusion.18), channel_id=1, source_target_pairs={{0,1},{1,2},{2,3},{3,4},{4,5},{5,6},{6,7},{8,9},{9,10},{10,11},{11... | collective-permute-start | bytes 73736 | tf_op jit(solution)/shard_map/ppermute | solution.py:33
  133.6 6.0 %collective-permute-start.9 = (f32[3,2,1,24,128]{4,3,2,0,1:T(8,128)S(1)}, f32[3,2,1,24,128]{4,3,2,0,1:T(8,128)S(1)}, u32[]{:S(2)}, u32[]{:S(2)}) collective-permute-start(f32[3,2,1,24,128]{4,3,2,0,1:T(8,128)S(1)} %pad_maximum_fusion.9), channel_id=1, source_target_pairs={{0,8},{8,16},{16,24},{24,32},{32,40},{40,48},{48,56},{56,64},{64,7... | collective-permute-start | bytes 221192 | tf_op jit(solution)/shard_map/ppermute | solution.py:33
  139.7 13.4 %collective-permute-done.9 = f32[3,2,1,24,128]{4,3,2,0,1:T(8,128)S(1)} collective-permute-done((f32[3,2,1,24,128]{4,3,2,0,1:T(8,128)S(1)}, f32[3,2,1,24,128]{4,3,2,0,1:T(8,128)S(1)}, u32[]{:S(2)}, u32[]{:S(2)}) %collective-permute-start.9) | collective-permute-done | bytes 73760 | tf_op jit(solution)/shard_map/ppermute | solution.py:33
  153.5 1.3 collective-permute-start.11
  155.4 1.9 collective-permute-start.10
  157.3 1.9 collective-permute-done.11
  159.3 0.3 fusion.53
  159.6 6.5 %collective-permute-start.12 = (f32[3,2,8,1,128]{4,3,2,0,1:T(1,128)S(1)}, f32[3,2,8,1,128]{4,3,2,0,1:T(1,128)S(1)}, u32[]{:S(2)}, u32[]{:S(2)}) collective-permute-start(f32[3,2,8,1,128]{4,3,2,0,1:T(1,128)S(1)} %pad_maximum_fusion.20), channel_id=1, source_target_pairs={{0,1},{1,2},{2,3},{3,4},{4,5},{5,6},{6,7},{8,9},{9,10},{10,11},{11... | collective-permute-start | bytes 73736 | tf_op jit(solution)/shard_map/ppermute | solution.py:33
  166.2 1.9 collective-permute-start.13
  168.2 15.4 %collective-permute-done.13 = f32[3,2,1,24,128]{4,3,2,0,1:T(8,128)S(1)} collective-permute-done((f32[3,2,1,24,128]{4,3,2,0,1:T(8,128)S(1)}, f32[3,2,1,24,128]{4,3,2,0,1:T(8,128)S(1)}, u32[]{:S(2)}, u32[]{:S(2)}) %collective-permute-start.13) | collective-permute-done | bytes 73760 | tf_op jit(solution)/shard_map/ppermute | solution.py:33
  184.0 1.3 collective-permute-start.15
  185.9 1.9 collective-permute-start.14
  187.8 1.9 collective-permute-done.15
  189.8 0.3 fusion.74
  190.2 6.3 %collective-permute-start.16 = (f32[3,2,8,1,128]{4,2,3,1,0:T(8,128)S(1)}, f32[3,2,8,1,128]{4,2,3,1,0:T(8,128)S(1)}, u32[]{:S(2)}, u32[]{:S(2)}) collective-permute-start(f32[3,2,8,1,128]{4,2,3,1,0:T(8,128)S(1)} %pad_maximum_fusion.22), channel_id=1, source_target_pairs={{0,1},{1,2},{2,3},{3,4},{4,5},{5,6},{6,7},{8,9},{9,10},{10,11},{11... | collective-permute-start | bytes 73736 | tf_op jit(solution)/shard_map/ppermute | solution.py:33
  196.5 1.0 pad_maximum_fusion.1
  197.5 1.9 collective-permute-start.17
  199.5 15.4 %collective-permute-done.17 = f32[3,2,1,24,128]{4,3,2,1,0:T(8,128)S(1)} collective-permute-done((f32[3,2,1,24,128]{4,3,2,1,0:T(8,128)S(1)}, f32[3,2,1,24,128]{4,3,2,1,0:T(8,128)S(1)}, u32[]{:S(2)}, u32[]{:S(2)}) %collective-permute-start.17) | collective-permute-done | bytes 73760 | tf_op jit(solution)/shard_map/ppermute | solution.py:33
  215.1 0.4 fusion.79
  215.4 1.0 pad_maximum_fusion
  (142 shorter events, 5.7 us)
Async XLA Ops:
  0.6 0.7 copy-start
  1.6 24.0 %copy-start.1 = (f32[3,3,8,24,128]{4,3,2,1,0:T(8,128)S(1)}, f32[3,3,8,24,128]{4,3,2,1,0:T(8,128)}, u32[]{:S(2)}) copy-start(f32[3,3,8,24,128]{4,3,2,1,0:T(8,128)} %param.8) | copy-start | bytes 2654212
  3.9 37.2 %copy-start.10 = (s32[6]{0:T(128)S(1)}, s32[6]{0:T(128)}, u32[]{:S(2)}) copy-start(s32[6]{0:T(128)} %param.13) | copy-start | bytes 76
  3.9 37.9 %copy-start.13 = (s32[64]{0:T(128)S(1)}, s32[64]{0:T(128)}, u32[]{:S(2)}) copy-start(s32[64]{0:T(128)} %param.12) | copy-start | bytes 772
  3.9 41.8 %copy-start.11 = (f32[2]{0:T(128)S(1)}, f32[2]{0:T(128)}, u32[]{:S(2)}) copy-start(f32[2]{0:T(128)} %param.15) | copy-start | bytes 28
  3.9 42.6 %copy-start.9 = (s32[8,24,128]{2,1,0:T(8,128)S(1)}, s32[8,24,128]{2,1,0:T(8,128)}, u32[]{:S(2)}) copy-start(s32[8,24,128]{2,1,0:T(8,128)} %param.14) | copy-start | bytes 294916
  3.9 44.4 %copy-start.8 = (f32[3,8,24,128]{3,2,1,0:T(8,128)S(1)}, f32[3,8,24,128]{3,2,1,0:T(8,128)}, u32[]{:S(2)}) copy-start(f32[3,8,24,128]{3,2,1,0:T(8,128)} %param.10) | copy-start | bytes 884740
  4.0 80.4 %all-to-all-start = ((f32[64,1,3072]{2,1,0:T(1,128)}), f32[64,1,3072]{2,1,0:T(1,128)S(1)}, u32[]{:S(2)}, u32[]{:S(2)}) async-start(f32[64,1,3072]{2,1,0:T(1,128)} %reshape.202), calls=%async_computation | async-start | bytes 1572864 | tf_op jit(solution)/shard_map/all_to_all | solution.py:16
  25.6 38.4 %collective-permute-start.3 = (f32[3,2,8,1,128]{4,2,3,1,0:T(8,128)S(1)}, f32[3,2,8,1,128]{4,2,3,1,0:T(8,128)S(1)}, u32[]{:S(2)}, u32[]{:S(2)}) collective-permute-start(f32[3,2,8,1,128]{4,2,3,1,0:T(8,128)S(1)} %pad_maximum_fusion.15), channel_id=1, source_target_pairs={{1,0},{2,1},{3,2},{4,3},{5,4},{6,5},{7,6},{9,8},{10,9},{11,10},{12... | collective-permute-start | bytes 73736 | tf_op jit(solution)/shard_map/ppermute | solution.py:33
  26.9 37.1 %collective-permute-start.2 = (f32[3,2,1,24,128]{4,3,2,0,1:T(8,128)S(1)}, f32[3,2,1,24,128]{4,3,2,0,1:T(8,128)}, u32[]{:S(2)}, u32[]{:S(2)}) collective-permute-start(f32[3,2,1,24,128]{4,3,2,0,1:T(8,128)S(1)} %copy.593), channel_id=1, source_target_pairs={{8,0},{16,8},{24,16},{32,24},{40,32},{48,40},{56,48},{64,56},{72,6... | collective-permute-start | bytes 221192 | tf_op jit(solution)/shard_map/ppermute | solution.py:33
  64.8 1.9 copy-start.4
  64.8 1.9 copy-start.5
  67.9 32.2 %collective-permute-start.4 = (f32[3,2,8,1,128]{4,2,3,1,0:T(8,128)S(1)}, f32[3,2,8,1,128]{4,2,3,1,0:T(8,128)S(1)}, u32[]{:S(2)}, u32[]{:S(2)}) collective-permute-start(f32[3,2,8,1,128]{4,2,3,1,0:T(8,128)S(1)} %pad_maximum_fusion.16), channel_id=1, source_target_pairs={{0,1},{1,2},{2,3},{3,4},{4,5},{5,6},{6,7},{8,9},{9,10},{10,11},{11... | collective-permute-start | bytes 73736 | tf_op jit(solution)/shard_map/ppermute | solution.py:33
  71.4 31.3 %collective-permute-start.5 = (f32[3,2,1,24,128]{4,3,2,0,1:T(8,128)}, f32[3,2,1,24,128]{4,3,2,0,1:T(8,128)}, u32[]{:S(2)}, u32[]{:S(2)}) collective-permute-start(f32[3,2,1,24,128]{4,3,2,0,1:T(8,128)} %pad_maximum_fusion.11), channel_id=1, source_target_pairs={{0,8},{8,16},{16,24},{24,32},{32,40},{40,48},{48,56},{56,64},{64,7... | collective-permute-start | bytes 221192 | tf_op jit(solution)/shard_map/ppermute | solution.py:33
  92.3 2.0 copy-start.12
  94.8 6.6 %collective-permute-start = (f32[1,12,64]{2,1,0:T(8,128)S(1)}, f32[1,12,64]{2,1,0:T(8,128)S(1)}, u32[]{:S(2)}, u32[]{:S(2)}) collective-permute-start(f32[1,12,64]{2,1,0:T(8,128)S(1)} %slice.420), channel_id=1, source_target_pairs={{8,0},{16,8},{24,16},{32,24},{40,32},{48,40},{56,48},{64,56},{72,6... | collective-permute-start | bytes 9224 | tf_op jit(solution)/shard_map/ppermute | solution.py:33
  101.5 5.5 %collective-permute-start.1 = (f32[8,1,64]{2,0,1:T(8,128)S(1)}, f32[8,1,64]{2,0,1:T(8,128)S(1)}, u32[]{:S(2)}, u32[]{:S(2)}) collective-permute-start(f32[8,1,64]{2,0,1:T(8,128)S(1)} %slice.543), channel_id=1, source_target_pairs={{1,0},{2,1},{3,2},{4,3},{5,4},{6,5},{7,6},{9,8},{10,9},{11,10},{12... | collective-permute-start | bytes 6152 | tf_op jit(solution)/shard_map/ppermute | solution.py:33
  107.7 1.2 copy-start.2
  108.7 2.0 copy-start.3
  108.7 2.0 copy-start.6
  108.7 2.0 copy-start.7
  111.0 15.9 %collective-permute-start.7 = (f32[3,2,8,1,128]{4,3,2,0,1:T(1,128)S(1)}, f32[3,2,8,1,128]{4,3,2,0,1:T(1,128)S(1)}, u32[]{:S(2)}, u32[]{:S(2)}) collective-permute-start(f32[3,2,8,1,128]{4,3,2,0,1:T(1,128)S(1)} %pad_maximum_fusion.17), channel_id=1, source_target_pairs={{1,0},{2,1},{3,2},{4,3},{5,4},{6,5},{7,6},{9,8},{10,9},{11,10},{12... | collective-permute-start | bytes 73736 | tf_op jit(solution)/shard_map/ppermute | solution.py:33
  112.7 16.2 %collective-permute-start.6 = (f32[3,2,1,24,128]{4,3,2,0,1:T(8,128)S(1)}, f32[3,2,1,24,128]{4,3,2,0,1:T(8,128)S(1)}, u32[]{:S(2)}, u32[]{:S(2)}) collective-permute-start(f32[3,2,1,24,128]{4,3,2,0,1:T(8,128)S(1)} %pad_maximum_fusion.10), channel_id=1, source_target_pairs={{8,0},{16,8},{24,16},{32,24},{40,32},{48,40},{56,48},{64,56},{72,6... | collective-permute-start | bytes 221192 | tf_op jit(solution)/shard_map/ppermute | solution.py:33
  129.2 10.5 %collective-permute-start.8 = (f32[3,2,8,1,128]{4,2,3,1,0:T(8,128)S(1)}, f32[3,2,8,1,128]{4,2,3,1,0:T(8,128)S(1)}, u32[]{:S(2)}, u32[]{:S(2)}) collective-permute-start(f32[3,2,8,1,128]{4,2,3,1,0:T(8,128)S(1)} %pad_maximum_fusion.18), channel_id=1, source_target_pairs={{0,1},{1,2},{2,3},{3,4},{4,5},{5,6},{6,7},{8,9},{9,10},{10,11},{11... | collective-permute-start | bytes 73736 | tf_op jit(solution)/shard_map/ppermute | solution.py:33
  133.6 19.5 %collective-permute-start.9 = (f32[3,2,1,24,128]{4,3,2,0,1:T(8,128)S(1)}, f32[3,2,1,24,128]{4,3,2,0,1:T(8,128)S(1)}, u32[]{:S(2)}, u32[]{:S(2)}) collective-permute-start(f32[3,2,1,24,128]{4,3,2,0,1:T(8,128)S(1)} %pad_maximum_fusion.9), channel_id=1, source_target_pairs={{0,8},{8,16},{16,24},{24,32},{32,40},{40,48},{48,56},{56,64},{64,7... | collective-permute-start | bytes 221192 | tf_op jit(solution)/shard_map/ppermute | solution.py:33
  153.5 5.7 %collective-permute-start.11 = (f32[3,2,8,1,128]{4,3,2,0,1:T(1,128)S(1)}, f32[3,2,8,1,128]{4,3,2,0,1:T(1,128)S(1)}, u32[]{:S(2)}, u32[]{:S(2)}) collective-permute-start(f32[3,2,8,1,128]{4,3,2,0,1:T(1,128)S(1)} %pad_maximum_fusion.19), channel_id=1, source_target_pairs={{1,0},{2,1},{3,2},{4,3},{5,4},{6,5},{7,6},{9,8},{10,9},{11,10},{12... | collective-permute-start | bytes 73736 | tf_op jit(solution)/shard_map/ppermute | solution.py:33
  155.4 3.9 %collective-permute-start.10 = (f32[3,2,1,24,128]{4,3,2,0,1:T(8,128)S(1)}, f32[3,2,1,24,128]{4,3,2,0,1:T(8,128)S(1)}, u32[]{:S(2)}, u32[]{:S(2)}) collective-permute-start(f32[3,2,1,24,128]{4,3,2,0,1:T(8,128)S(1)} %pad_maximum_fusion.8), channel_id=1, source_target_pairs={{8,0},{16,8},{24,16},{32,24},{40,32},{48,40},{56,48},{64,56},{72,6... | collective-permute-start | bytes 221192 | tf_op jit(solution)/shard_map/ppermute | solution.py:33
  159.6 8.5 %collective-permute-start.12 = (f32[3,2,8,1,128]{4,3,2,0,1:T(1,128)S(1)}, f32[3,2,8,1,128]{4,3,2,0,1:T(1,128)S(1)}, u32[]{:S(2)}, u32[]{:S(2)}) collective-permute-start(f32[3,2,8,1,128]{4,3,2,0,1:T(1,128)S(1)} %pad_maximum_fusion.20), channel_id=1, source_target_pairs={{0,1},{1,2},{2,3},{3,4},{4,5},{5,6},{6,7},{8,9},{9,10},{10,11},{11... | collective-permute-start | bytes 73736 | tf_op jit(solution)/shard_map/ppermute | solution.py:33
  166.2 17.4 %collective-permute-start.13 = (f32[3,2,1,24,128]{4,3,2,0,1:T(8,128)S(1)}, f32[3,2,1,24,128]{4,3,2,0,1:T(8,128)S(1)}, u32[]{:S(2)}, u32[]{:S(2)}) collective-permute-start(f32[3,2,1,24,128]{4,3,2,0,1:T(8,128)S(1)} %pad_maximum_fusion.7), channel_id=1, source_target_pairs={{0,8},{8,16},{16,24},{24,32},{32,40},{40,48},{48,56},{56,64},{64,7... | collective-permute-start | bytes 221192 | tf_op jit(solution)/shard_map/ppermute | solution.py:33
  184.0 5.7 %collective-permute-start.15 = (f32[3,2,8,1,128]{4,3,2,0,1:T(1,128)S(1)}, f32[3,2,8,1,128]{4,3,2,0,1:T(1,128)S(1)}, u32[]{:S(2)}, u32[]{:S(2)}) collective-permute-start(f32[3,2,8,1,128]{4,3,2,0,1:T(1,128)S(1)} %pad_maximum_fusion.21), channel_id=1, source_target_pairs={{1,0},{2,1},{3,2},{4,3},{5,4},{6,5},{7,6},{9,8},{10,9},{11,10},{12... | collective-permute-start | bytes 73736 | tf_op jit(solution)/shard_map/ppermute | solution.py:33
  185.9 3.9 %collective-permute-start.14 = (f32[3,2,1,24,128]{4,3,2,0,1:T(8,128)S(1)}, f32[3,2,1,24,128]{4,3,2,0,1:T(8,128)S(1)}, u32[]{:S(2)}, u32[]{:S(2)}) collective-permute-start(f32[3,2,1,24,128]{4,3,2,0,1:T(8,128)S(1)} %pad_maximum_fusion.6), channel_id=1, source_target_pairs={{8,0},{16,8},{24,16},{32,24},{40,32},{48,40},{56,48},{64,56},{72,6... | collective-permute-start | bytes 221192 | tf_op jit(solution)/shard_map/ppermute | solution.py:33
  190.2 9.3 %collective-permute-start.16 = (f32[3,2,8,1,128]{4,2,3,1,0:T(8,128)S(1)}, f32[3,2,8,1,128]{4,2,3,1,0:T(8,128)S(1)}, u32[]{:S(2)}, u32[]{:S(2)}) collective-permute-start(f32[3,2,8,1,128]{4,2,3,1,0:T(8,128)S(1)} %pad_maximum_fusion.22), channel_id=1, source_target_pairs={{0,1},{1,2},{2,3},{3,4},{4,5},{5,6},{6,7},{8,9},{9,10},{10,11},{11... | collective-permute-start | bytes 73736 | tf_op jit(solution)/shard_map/ppermute | solution.py:33
  197.5 17.4 %collective-permute-start.17 = (f32[3,2,1,24,128]{4,3,2,1,0:T(8,128)S(1)}, f32[3,2,1,24,128]{4,3,2,1,0:T(8,128)S(1)}, u32[]{:S(2)}, u32[]{:S(2)}) collective-permute-start(f32[3,2,1,24,128]{4,3,2,1,0:T(8,128)S(1)} %pad_maximum_fusion.5), channel_id=1, source_target_pairs={{0,8},{8,16},{16,24},{24,32},{32,40},{40,48},{48,56},{56,64},{64,7... | collective-permute-start | bytes 221192 | tf_op jit(solution)/shard_map/ppermute | solution.py:33
where the time goes:
time: 218 us; the launch traced here: 216 us
  starting transfers between devices  107 us (49%)
  waiting for transfers between devices  63.6 us (29%)
  local copies, waits for them, and re-layouts  22.2 us (10%)
  other arithmetic  20.4 us (9%)
  between operations  2.87 us (1%)
    ppermute x18, starting transfers between devices, from_behind(): lax.ppermute(value, axis, [(source, source + steps) for source in range(f...  85.4 us
    ppermute x18, waiting for transfers between devices, from_behind(): lax.ppermute(value, axis, [(source, source + steps) for source in range(f...  63.6 us
    all_to_all x1, starting transfers between devices, sent_to_all(): return lax.all_to_all(copies, axis, split_axis=0, concat_axis=0, tiled=True)  21.6 us
    unnamed x32, local copies, waits for them, and re-layouts  5.52 us
  transfers between devices with their start and end apart: 19, of which 11 were waited for; matrix products, arithmetic and copies ran while one was open for 15% of the time, Pallas kernels for 0%

commit v1 on v0

v1 whole, which is shorter than its diff:
```python
import jax
import jax.numpy as jnp
import numpy as np
from jax import lax
from jax.experimental import pallas as pl
from jax.experimental.pallas import tpu as pltpu
from jax.sharding import PartitionSpec as P

STEPS = 4
PLANES = 8
OWN = 24
ROWS = 32
HALO = 4
LANES = 128
TILES = 28

sharpness = 8.0
thresholds = (0.7, 0.5, 0.3)
time_step = 0.5

INTERPRET = False


def lane_ids():
    return lax.broadcasted_iota(jnp.int32, (ROWS, LANES), 1)


def row_ids():
    rows = lax.broadcasted_iota(jnp.int32, (ROWS, LANES), 0)
    return jnp.where(rows < OWN + HALO, rows, rows - ROWS)


def y_forward(a):
    return pltpu.roll(a, ROWS - 1, 0) - a


def y_backward(a):
    return a - pltpu.roll(a, 1, 0)


def z_forward(a, lanes):
    return jnp.where(lanes == LANES - 1, 0.0, pltpu.roll(a, LANES - 1, 1)) - a


def z_backward(a, lanes):
    return a - jnp.where(lanes == 0, 0.0, pltpu.roll(a, 1, 1))


def next_magnetic(h, e, e_up, step, lanes):
    up_y, up_z = e_up
    curl_x = y_forward(e[2]) - z_forward(e[1], lanes)
    curl_y = z_forward(e[0], lanes) - (up_z - e[2])
    curl_z = (up_y - e[1]) - y_forward(e[0])
    return [h[0] - step * curl_x, h[1] - step * curl_y, h[2] - step * curl_z]


def next_electric(e, h, h_down, coefficient, current, lanes):
    down_y, down_z = h_down
    curls = [
        y_backward(h[2]) - z_backward(h[1], lanes),
        z_backward(h[0], lanes) - (h[2] - down_z),
        (h[1] - down_y) - y_backward(h[0]),
    ]
    if current is not None:
        curls = [curls[c] - current[c] for c in range(3)]
    return [e[c] + coefficient * curls[c] for c in range(3)]


def step_of_rows(narrow_place):
    return jnp.where((row_ids() < 0) & (narrow_place == 0), 0.0, time_step)


WIDE, NARROW, CORE, WIDE_COUNT, NARROW_COUNT, OWN_AT, BEFORE_AT, AFTER_AT, BOX = 0, 1, 2, 3, 4, 5, 6, 7, 8


def extend_kernel(table, e_ref, h_ref, j_ref, m_ref, lo_ref, hi_ref, ee_ref, h1_ref, jj_ref, mm_ref):
    lanes = lane_ids()
    step = step_of_rows(table[NARROW])

    def extended(own, at):
        return jnp.concatenate([own, hi_ref[at], lo_ref[at]], axis=0)

    def per_real(r, carry):
        def fields(p):
            return [extended(e_ref[r, c, p], (r * 3 + c) * PLANES + p) for c in range(3)]

        up = fields(PLANES - 1)
        for p in range(PLANES - 1, -1, -1):
            e = up if p == PLANES - 1 else fields(p)
            h = [extended(h_ref[r, c, p], 72 + (r * 3 + c) * PLANES + p) for c in range(3)]
            zero = jnp.zeros((ROWS, LANES), jnp.float32)
            e_up = (zero, zero) if p == PLANES - 1 else (up[1], up[2])
            new = next_magnetic(h, e, e_up, step, lanes)
            for c in range(3):
                ee_ref[r, c, p] = e[c]
                h1_ref[r, c, p] = new[c]
            up = e
        return carry

    lax.fori_loop(0, 3, per_real, 0)

    def per_plane(p, carry):
        for c in range(3):
            jj_ref[c, p] = extended(j_ref[c, p], 144 + c * PLANES + p)
        mm_ref[p] = extended(m_ref[p].astype(jnp.float32), 168 + p)
        return carry

    lax.fori_loop(0, PLANES, per_plane, 0)


def coefficients_of(density, mask, global_x, table, levels, lanes):
    m0, m1 = levels[0], levels[1]
    global_y = table[NARROW] * OWN + row_ids()
    inside = (
        (global_x >= table[BOX])
        & (global_x < table[BOX + 1])
        & (global_y >= table[BOX + 2])
        & (global_y < table[BOX + 3])
        & (lanes >= table[BOX + 4])
        & (lanes < table[BOX + 5])
    )
    in_grid = (
        (global_x >= 0)
        & (global_x < table[WIDE_COUNT] * PLANES)
        & (global_y >= 0)
        & (global_y < table[NARROW_COUNT] * OWN)
    )
    background = jnp.where(mask > 0.5, m1, m0)
    out = []
    for threshold in thresholds:
        base = float(np.tanh(sharpness * threshold))
        scale = 1.0 / (base + float(np.tanh(sharpness * (1.0 - threshold))))
        projected = (base + jnp.tanh(sharpness * (density - threshold))) * scale
        permittivity = jnp.where(inside, m0 + projected * (m1 - m0), background)
        out.append(jnp.where(in_grid, time_step / permittivity, 0.0))
    return out


def packed_halo(traces):
    rows = lax.broadcasted_iota(jnp.int32, (8, LANES), 0)
    tiles = []
    for c in range(2):
        halo = [traces[n][c][OWN:] for n in range(STEPS)]
        tiles.append(jnp.where(rows == 3, pltpu.roll(halo[3], 4, 0), halo[0]))
        tiles.append(jnp.where((rows > 1) & (rows < 5), pltpu.roll(halo[2], 4, 0), halo[1]))
    return tiles


def as_message(traces):
    tiles = []
    for n in range(STEPS):
        for c in range(2):
            tiles += [traces[n][c][8 * i : 8 * i + 8] for i in range(3)]
    return tiles + packed_halo(traces)


def from_message(tile):
    traces = []
    for n in range(STEPS):
        step = []
        for c in range(2):
            halo = tile(24 + 2 * c + (0 if n in (0, 3) else 1))
            halo = pltpu.roll(halo, 4, 0) if n > 1 else halo
            step.append(jnp.concatenate([tile((n * 2 + c) * 3 + i) for i in range(3)] + [halo], axis=0))
        traces.append(step)
    return traces


def trace_kernel(table, levels, g_ref, wz_ref, wy_ref, mm_ref, ee_ref, h1_ref, jj_ref, far_ref, near_ref, c_ref, d_ref):
    lanes = lane_ids()
    step = step_of_rows(table[NARROW])
    own, before, after = table[OWN_AT], table[BEFORE_AT], table[AFTER_AT]
    last = table[WIDE] == table[WIDE_COUNT] - 1
    coarse = [g_ref[before * 4 + 3]] + [g_ref[own * 4 + q] for q in range(4)]
    coarse.append(jnp.where(last, coarse[4], g_ref[after * 4]))
    coarse.append(g_ref[after * 4 + 1])
    along_z = jnp.dot(
        jnp.concatenate(coarse, axis=0),
        wz_ref[...],
        precision=lax.Precision.HIGHEST,
        preferred_element_type=jnp.float32,
    )
    strips = [
        jnp.concatenate([along_z[8 * q : 8 * q + 8, :LANES], along_z[8 * q : 8 * q + 8, LANES:]], axis=0)
        for q in range(7)
    ]
    along_y = jnp.dot(
        wy_ref[...],
        jnp.concatenate(strips, axis=1),
        precision=lax.Precision.HIGHEST,
        preferred_element_type=jnp.float32,
    )
    for q in range(7):
        d_ref[q] = along_y[:, LANES * q : LANES * (q + 1)]

    def own_plane(p, carry):
        q = 1 + lax.div(p, 2)
        lower = d_ref[q]
        upper = d_ref[q + lax.rem(p, 2)]
        values = coefficients_of(
            0.5 * (lower + upper), mm_ref[p], table[WIDE] * PLANES + p, table, levels, lanes
        )
        for r in range(3):
            c_ref[r, p] = values[r]
        return carry

    lax.fori_loop(0, PLANES, own_plane, 0)
    core = table[CORE]
    zero = jnp.zeros((ROWS, LANES), jnp.float32)

    def per_real(r, carry):
        def j(p):
            return [jj_ref[c, p] for c in range(3)]

        e = {p: [ee_ref[r, c, p] for c in range(3)] for p in (5, 6, 7)}
        h = {p: [h1_ref[r, c, p] for c in range(3)] for p in (4, 5, 6, 7)}
        up = [(h[7][1], h[7][2])]
        for first in (5, 6, 7):
            for p in range(first, 8):
                e[p] = next_electric(e[p], h[p], (h[p - 1][1], h[p - 1][2]), c_ref[r, p], j(p), lanes)
            e[8] = [zero] * 3
            for p in range(first, 8):
                h[p] = next_magnetic(h[p], e[p], (e[p + 1][1], e[p + 1][2]), step, lanes)
            up.append((h[7][1], h[7][2]))
        e = {p: [ee_ref[r, c, p] for c in range(3)] for p in (0, 1, 2)}
        h = {p: [h1_ref[r, c, p] for c in range(3)] for p in (0, 1, 2)}
        h[-1] = [zero] * 3
        down = [(e[0][1], e[0][2])]
        for last_plane in (2, 1, 0):
            for p in range(last_plane + 1):
                e[p] = next_electric(e[p], h[p], (h[p - 1][1], h[p - 1][2]), c_ref[r, p], j(p), lanes)
            down.append((e[0][1], e[0][2]))
            for p in range(last_plane):
                h[p] = next_magnetic(h[p], e[p], (e[p + 1][1], e[p + 1][2]), step, lanes)
        for i, (a, b) in enumerate(zip(as_message(up), as_message(down), strict=True)):
            far_ref[r * TILES + i] = jnp.where(core == 1, a, b)
            near_ref[r * TILES + i] = jnp.where(core == 1, b, a)
        return carry

    lax.fori_loop(0, 3, per_real, 0)


def ghost_kernel(table, levels, d_ref, far_ref, near_ref, c_ref):
    lanes = lane_ids()
    core = table[CORE]
    for i, (p, lower, upper) in enumerate(((-2, 0, 0), (-1, 0, 1), (8, 5, 5), (9, 5, 6))):
        far, near = far_ref[i % 2], near_ref[i % 2]
        mask = jnp.where(core == 0, far, near) if p < 0 else jnp.where(core == 1, far, near)
        values = coefficients_of(
            0.5 * (d_ref[lower] + d_ref[upper]), mask, table[WIDE] * PLANES + p, table, levels, lanes
        )
        for r in range(3):
            c_ref[r, i] = values[r]


def window_kernel(table, far_ref, near_ref, c_ref, g_ref, ee_ref, h1_ref, jj_ref, eo_ref, ho_ref):
    lanes = lane_ids()
    core = table[CORE]
    step = step_of_rows(table[NARROW])
    below = jnp.where(table[WIDE] == 0, 0.0, step)
    zero = jnp.zeros((ROWS, LANES), jnp.float32)

    def per_real(r, carry):
        def tile_from_below(i):
            return jnp.where(core == 0, far_ref[r * TILES + i], near_ref[r * TILES + i])

        def tile_from_above(i):
            return jnp.where(core == 1, far_ref[r * TILES + i], near_ref[r * TILES + i])

        trace_h = from_message(tile_from_below)
        trace_e = from_message(tile_from_above)

        def coefficient(p):
            if p < 0:
                return g_ref[r, p + 2]
            return g_ref[r, p - 6] if p >= PLANES else c_ref[r, p]

        def current(p):
            return [jj_ref[c, p] for c in range(3)] if 0 <= p < PLANES else None

        e = {p: [zero] * 3 for p in (-2, -1, 8, 9)}
        h = {p: [zero] * 3 for p in (-3, -2, -1, 8, 9)}
        for p in range(PLANES):
            e[p] = [ee_ref[r, c, p] for c in range(3)]
            h[p] = [h1_ref[r, c, p] for c in range(3)]
        h[7] = [h[7][0], h[7][1] + step * trace_e[0][1], h[7][2] - step * trace_e[0][0]]
        h[-1] = next_magnetic(h[-1], e[-1], (e[0][1], e[0][2]), below, lanes)

        def magnetic(planes, n):
            new = {}
            for p in planes:
                up = [e[p + 1][1], e[p + 1][2]]
                if p == 7:
                    up = [up[0] + trace_e[n - 1][0], up[1] + trace_e[n - 1][1]]
                new[p] = next_magnetic(h[p], e[p], up, below if p < 0 else step, lanes)
            h.update(new)

        def electric(planes, n):
            new = {}
            for p in planes:
                down = [h[p - 1][1], h[p - 1][2]]
                if p == 0:
                    down = [down[0] + trace_h[n - 1][0], down[1] + trace_h[n - 1][1]]
                new[p] = next_electric(e[p], h[p], down, coefficient(p), current(p), lanes)
            e.update(new)

        electric(range(-1, 9), 1)
        magnetic(range(-2, 9), 2)
        electric(range(-2, 10), 2)
        magnetic(range(-2, 9), 3)
        electric(range(-1, 9), 3)
        magnetic(range(-1, 8), 4)
        electric(range(8), 4)
        for p in range(PLANES):
            for c in range(3):
                eo_ref[r, c, p] = e[p][c][:OWN]
                ho_ref[r, c, p] = h[p][c][:OWN]
        return carry

    lax.fori_loop(0, 3, per_real, 0)


def refine_weights():
    along_z = np.zeros((64, LANES), np.float32)
    for cell in range(LANES):
        along_z[cell // 2, cell] += 0.5
        along_z[min((cell + 1) // 2, 63), cell] += 0.5
    both = np.zeros((LANES, 2 * LANES), np.float32)
    both[:64, :LANES] = along_z
    both[64:, LANES:] = along_z
    along_y = np.zeros((ROWS, 16), np.float32)
    for row in range(ROWS):
        y = row if row < OWN + HALO else row - ROWS
        along_y[row, y // 2 + 2] += 0.5
        along_y[row, min((y + 1) // 2 + 2, 15)] += 0.5
    return both, along_y


def call(kernel, outs, cost=None):
    return dict(
        out_shape=[jax.ShapeDtypeStruct(shape, jnp.float32) for shape in outs],
        out_specs=[pl.BlockSpec(memory_space=pltpu.VMEM) for _ in outs],
        compiler_params=pltpu.CompilerParams(vmem_limit_bytes=40 * 1024 * 1024),
        cost_estimate=cost,
        interpret=INTERPRET,
        name=kernel.__name__,
    )


def specs(smem, vmem):
    return [pl.BlockSpec(memory_space=pltpu.SMEM)] * smem + [pl.BlockSpec(memory_space=pltpu.VMEM)] * vmem


def body(
    electric,
    magnetic,
    current,
    density_tiles,
    tile_slabs,
    design_box,
    material_mask,
    material_levels,
):
    wide_count = lax.axis_size("wide")
    wide_place = lax.axis_index("wide")
    narrow_count = lax.axis_size("narrow")
    narrow_place = lax.axis_index("narrow")
    core = wide_place % 2
    half = wide_count // 2
    f32 = jnp.float32

    near_pairs = [(w, w ^ 1) for w in range(wide_count)]
    partner = [(w + 1) % wide_count if w % 2 else (w - 1) % wide_count for w in range(wide_count)]
    far_ring = [(w, partner[w]) for w in range(wide_count)]
    far_pairs = [(w, partner[w]) for w in range(1, wide_count - 1)]
    up = [(n, n + 1) for n in range(narrow_count - 1)]
    down = [(n + 1, n) for n in range(narrow_count - 1)]
    groups = [[w for w in range(wide_count) if (w // 2) % 2 == side] for side in range(2)]

    tile = density_tiles
    tile_lo = lax.ppermute(tile[:, 10:].reshape(4, 128), "narrow", up).reshape(4, 2, 64)
    tile_hi = lax.ppermute(tile[:, :2].reshape(4, 128), "narrow", down).reshape(4, 2, 64)
    tile_hi = jnp.where(narrow_place == narrow_count - 1, tile[:, 11:], tile_hi)
    rows = jnp.concatenate([tile_lo, tile, tile_hi], axis=1)
    packed = jnp.concatenate([rows[:, :8], rows[:, 8:]], axis=2)

    stack = [
        electric.reshape(72, OWN, LANES),
        magnetic.reshape(72, OWN, LANES),
        current.reshape(24, OWN, LANES),
        material_mask.astype(f32),
    ]
    first_rows = jnp.concatenate([x[:, :HALO] for x in stack], axis=0)
    last_rows = jnp.concatenate([x[:, OWN - HALO :] for x in stack], axis=0)
    low = lax.ppermute(last_rows, "narrow", up)
    high = lax.ppermute(first_rows, "narrow", down)

    other = lax.ppermute(packed, "wide", far_ring)
    held = jnp.concatenate([packed, other], axis=0)
    spread = jnp.broadcast_to(held, (half, 8, 8, LANES))
    gathered = lax.all_to_all(spread, "wide", 0, 0, axis_index_groups=groups, tiled=True)
    gathered = gathered.reshape(half * 8, 8, LANES)

    wanted = jnp.clip(wide_place + jnp.arange(-1, 2, dtype=jnp.int32), 0, wide_count - 1)
    ids = jnp.arange(wide_count, dtype=jnp.int32)
    at = jnp.sum(jnp.where(tile_slabs[None, :] == wanted[:, None], ids[None, :], 0), axis=1)
    mate = jnp.where(at % 2 == 1, at + 1, at - 1 + wide_count) % wide_count
    same_side = (at // 2) % 2 == (wide_place // 2) % 2
    holder = jnp.where(same_side, at, mate)
    place = ((holder // 4) * 2 + holder % 2) * 2 + jnp.where(same_side, 0, 1)
    table = jnp.concatenate(
        [
            jnp.stack([wide_place, narrow_place, core, jnp.int32(wide_count), jnp.int32(narrow_count)]),
            place[1:2],
            place[0:1],
            place[2:3],
            design_box,
        ]
    ).astype(jnp.int32)

    extended = (3, 3, PLANES, ROWS, LANES)
    planes = (PLANES, ROWS, LANES)
    e_ext, h_one, j_ext, m_ext = pl.pallas_call(
        extend_kernel,
        in_specs=specs(1, 6),
        **call(extend_kernel, [extended, extended, (3, *planes), planes]),
    )(table, electric, magnetic, current, material_mask, low, high)

    mask_up, mask_down = m_ext[6:], m_ext[:2]
    mask_far = lax.ppermute(jnp.where(core == 1, mask_up, mask_down), "wide", far_pairs)
    mask_near = lax.ppermute(jnp.where(core == 1, mask_down, mask_up), "wide", near_pairs)

    weights_z, weights_y = refine_weights()
    message = (3 * TILES, 8, LANES)
    far, near, own_c, dens = pl.pallas_call(
        trace_kernel,
        in_specs=specs(2, 7),
        **call(trace_kernel, [message, message, (3, *planes), (7, ROWS, LANES)]),
    )(table, material_levels, gathered, weights_z, weights_y, m_ext, e_ext, h_one, j_ext)

    near = lax.ppermute(near, "wide", near_pairs)
    far = lax.ppermute(far, "wide", far_pairs)

    (ghost_c,) = pl.pallas_call(
        ghost_kernel,
        in_specs=specs(2, 3),
        **call(ghost_kernel, [(3, 4, ROWS, LANES)]),
    )(table, material_levels, dens, mask_far, mask_near)

    own = (3, 3, PLANES, OWN, LANES)
    return tuple(
        pl.pallas_call(
            window_kernel,
            in_specs=specs(1, 7),
            **call(window_kernel, [own, own]),
        )(table, far, near, own_c, ghost_c, e_ext, h_one, j_ext)
    )


def solution(mesh):
    return jax.shard_map(
        body,
        mesh=mesh,
        in_specs=(
            P(None, None, "wide", "narrow", None),
            P(None, None, "wide", "narrow", None),
            P(None, "wide", "narrow", None),
            P("wide", "narrow", None),
            P(),
            P(),
            P("wide", "narrow", None),
            P(),
        ),
        out_specs=(P(None, None, "wide", "narrow", None), P(None, None, "wide", "narrow", None)),
        check_vma=False,
    )
```

time: 218 us -> 129 us (0.59)
  the two profiles are of different devices: /device:TPU:6 before, /device:TPU:102 now
where the time goes in v1:
time: 129 us; the launch traced here: 128 us
  starting transfers between devices  56.4 us (44%)
  waiting for transfers between devices  34.8 us (27%)
  local copies, waits for them, and re-layouts  25.6 us (20%)
  Pallas kernels  9.93 us (8%)
    ppermute x1, waiting for transfers between devices, body(): lax.ppermute(jnp.where(core == 1, mask_up, mask_down), 'wide', far_pairs)  25.8 us
    unnamed x56, local copies, waits for them, and re-layouts  18.5 us
    ppermute x1, starting transfers between devices, body(): far = lax.ppermute(far, 'wide', far_pairs)  14.8 us
    ppermute x1, starting transfers between devices, body(): other = lax.ppermute(packed, 'wide', far_ring)  14.6 us
    all_to_all x1, starting transfers between devices, body(): lax.all_to_all(spread, 'wide', 0, 0, axis_index_groups=groups, tiled=True)  5.65 us
    ppermute x1, starting transfers between devices, body(): low = lax.ppermute(last_rows, 'narrow', up)  5.17 us
    ppermute x1, starting transfers between devices, body(): lax.ppermute(tile[:, 10:].reshape(4, 128), 'narrow', up).reshape(4, 2, 64)  5.02 us
    ppermute x1, waiting for transfers between devices, body(): high = lax.ppermute(first_rows, 'narrow', down)  4.68 us
  transfers between devices with their start and end apart: 10, of which 4 were waited for; matrix products, arithmetic and copies ran while one was open for 4% of the time, Pallas kernels for 1%

profile of v1, /device:TPU:102, one launch (start us, length us, event | category | flops | bytes accessed | tf_op | source)
XLA Modules:
  0.0 128.2 jit_solution(1921793293271379732)
XLA Ops:
  0.6 0.7 fusion.8
  1.4 0.1 reshape.37
  1.5 2.0 %collective-permute-start.1 = (f32[4,128]{1,0:T(4,128)S(1)}, f32[4,128]{1,0:T(4,128)S(1)}, u32[]{:S(2)}, u32[]{:S(2)}) collective-permute-start(f32[4,128]{1,0:T(4,128)S(1)} %reshape.37), channel_id=1, source_target_pairs={{1,0},{2,1},{3,2},{4,3},{5,4},{6,5},{7,6},{9,8},{10,9},{11,10},{12... | collective-permute-start | bytes 6152 | tf_op jit(solution)/shard_map/ppermute | solution.py:382
  3.5 0.1 reshape.35
  3.6 5.0 %collective-permute-start = (f32[4,128]{1,0:T(4,128)S(1)}, f32[4,128]{1,0:T(4,128)S(1)}, u32[]{:S(2)}, u32[]{:S(2)}) collective-permute-start(f32[4,128]{1,0:T(4,128)S(1)} %reshape.35), channel_id=1, source_target_pairs={{0,1},{1,2},{2,3},{3,4},{4,5},{5,6},{6,7},{8,9},{9,10},{10,11},{11... | collective-permute-start | bytes 6152 | tf_op jit(solution)/shard_map/ppermute | solution.py:381
  8.6 1.4 %fusion.4 = (f32[72,4,128]{2,1,0:T(4,128)S(1)}, f32[72,4,128]{2,1,0:T(4,128)S(1)}, f32[72,4,128]{2,1,0:T(4,128)S(1)}, f32[72,4,128]{2,1,0:T(4,128)S(1)}) fusion(f32[72,24,128]{2,1,0:T(8,128)} %bitcast.10, f32[72,24,128]{2,1,0:T(8,128)} %bitcast.11), kind=kLoop, calls=%fused_computation.36 | loop fusion | bytes 1179648 | tf_op jit(solution)/shard_map/slice | solution.py:393
  10.0 0.0 collective-permute-done.1
  10.0 0.1 reshape.38
  10.1 0.0 collective-permute-done
  10.1 0.1 reshape.36
  10.2 0.1 pad_maximum_fusion.5
  10.3 14.6 %collective-permute-start.2 = (f32[4,8,128]{2,0,1:T(4,128)S(1)}, f32[4,8,128]{2,0,1:T(4,128)S(1)}, u32[]{:S(2)}, u32[]{:S(2)}) collective-permute-start(f32[4,8,128]{2,0,1:T(4,128)S(1)} %pad_maximum_fusion.5), channel_id=1, source_target_pairs={{0,504},{8,16},{16,8},{24,32},{32,24},{40,48},{48,40},{56,64},{64,... | collective-permute-start | bytes 49160 | tf_op jit(solution)/shard_map/ppermute | solution.py:398
  24.9 1.0 fusion.6
  25.9 1.2 collective-permute-done.2
  27.1 0.1 pad_maximum_fusion.2
  27.2 1.1 broadcast_in_dim.36
  28.3 5.6 %all-to-all-start = ((f32[32,8,8,128]{3,2,1,0:T(8,128)}), f32[32,8,8,128]{3,2,1,0:T(8,128)S(1)}, u32[]{:S(2)}, u32[]{:S(2)}) async-start(f32[32,8,8,128]{3,2,1,0:T(8,128)} %broadcast_in_dim.36), calls=%async_computation | async-start | bytes 2097152 | tf_op jit(solution)/shard_map/all_to_all | solution.py:401
  33.9 0.0 copy-start.27
  34.0 0.0 copy-start.26
  34.0 0.1 pad_maximum_fusion
  34.1 5.2 %collective-permute-start.3 = (f32[176,4,128]{2,1,0:T(4,128)S(1)}, f32[176,4,128]{2,1,0:T(4,128)S(1)}, u32[]{:S(2)}, u32[]{:S(2)}) collective-permute-start(f32[176,4,128]{2,1,0:T(4,128)S(1)} %pad_maximum_fusion), channel_id=1, source_target_pairs={{0,1},{1,2},{2,3},{3,4},{4,5},{5,6},{6,7},{8,9},{9,10},{10,11},{11... | collective-permute-start | bytes 1081352 | tf_op jit(solution)/shard_map/ppermute | solution.py:395
  39.2 0.1 pad_maximum_fusion.1
  39.3 1.9 %collective-permute-start.4 = (f32[176,4,128]{2,1,0:T(4,128)S(1)}, f32[176,4,128]{2,1,0:T(4,128)S(1)}, u32[]{:S(2)}, u32[]{:S(2)}) collective-permute-start(f32[176,4,128]{2,1,0:T(4,128)S(1)} %pad_maximum_fusion.1), channel_id=1, source_target_pairs={{1,0},{2,1},{3,2},{4,3},{5,4},{6,5},{7,6},{9,8},{10,9},{11,10},{12... | collective-permute-start | bytes 1081352 | tf_op jit(solution)/shard_map/ppermute | solution.py:396
  41.3 0.2 select_reduce_fusion
  41.5 0.7 fusion.9
  42.2 1.9 %concatenate.22.table = s32[14]{0:T(128)S(1)} concatenate(s32[1]{0:T(128)} %bitcast, s32[1]{0:T(128)} %bitcast.1, s32[1]{0:T(128)} %bitcast.2, s32[1]{0:T(128)} %constant.97.clone.1, s32[1]{0:T(128)} %constant.98.clone.1, s32[1]{0:T(128)} %get-tuple-element.34, s32[1]{0:T(128)} %get-tuple-element.33, s32[1]{0:T(128)} %get-tuple-element.32, s32[6]{0:T(128)S(1)} %copy-done.26), dimensions={0} | concatenate | bytes 112 | tf_op jit(solution)/shard_map/concatenate | solution.py:411
  44.1 3.1 %collective-permute-done.3.lo_ref = f32[176,4,128]{2,1,0:T(4,128)S(1)} collective-permute-done((f32[176,4,128]{2,1,0:T(4,128)S(1)}, f32[176,4,128]{2,1,0:T(4,128)S(1)}, u32[]{:S(2)}, u32[]{:S(2)}) %collective-permute-start.3) | collective-permute-done | bytes 360480 | tf_op jit(solution)/shard_map/ppermute | solution.py:395
  47.2 0.7 copy-done.9
  47.9 4.7 %collective-permute-done.4.hi_ref = f32[176,4,128]{2,1,0:T(4,128)S(1)} collective-permute-done((f32[176,4,128]{2,1,0:T(4,128)S(1)}, f32[176,4,128]{2,1,0:T(4,128)S(1)}, u32[]{:S(2)}, u32[]{:S(2)}) %collective-permute-start.4) | collective-permute-done | bytes 360480 | tf_op jit(solution)/shard_map/ppermute | solution.py:396
  52.6 0.7 copy-done.11
  53.4 1.2 copy-done.3
  54.5 1.2 copy-done.4
  55.7 1.0 copy-done.5
  56.7 1.0 copy-done.10
  57.6 1.0 copy-done.12
  58.6 1.1 extend_kernel.1
  59.7 0.0 copy-start
  59.7 0.7 copy-done
  60.5 0.6 copy-done.13
  61.1 0.6 copy-done.20
  61.7 0.0 all-to-all-done
  61.7 1.0 copy-done.1
  62.7 0.9 copy-done.14
  63.6 0.9 copy-done.16
  64.5 0.7 copy-done.21
  65.2 0.7 copy-done.23
  65.8 3.6 %trace_kernel.1 = (f32[84,8,128]{2,1,0:T(8,128)}, f32[84,8,128]{2,1,0:T(8,128)}, f32[3,8,32,128]{3,2,1,0:T(8,128)S(1)}, f32[7,32,128]{2,1,0:T(8,128)S(1)}) custom-call(s32[14]{0:T(128)S(1)} %copy-done.21, f32[2]{0:T(128)S(1)} %copy-done.23, f32[256,8,128]{2,1,0:T(8,128)S(1)} %bitcast.9, f32[128,256]{1,0:T(8,128)S(1)} %copy-done.16, f32[32,16]{1,0:T(8,128)S(1)} %copy-done.19, ...), custom_call_target="tpu_custom_call" | custom-call | tf_op jit(solution)/shard_map/trace_kernel/pallas_call | solution.py:435
  69.4 0.7 copy-done.7
  70.2 0.6 copy-done.17
  70.8 14.8 %collective-permute-start.5 = (f32[84,8,128]{2,1,0:T(8,128)}, f32[84,8,128]{2,1,0:T(8,128)S(1)}, u32[]{:S(2)}, u32[]{:S(2)}) collective-permute-start(f32[84,8,128]{2,1,0:T(8,128)} %get-tuple-element.14), channel_id=1, source_target_pairs={{8,16},{16,8},{24,32},{32,24},{40,48},{48,40},{56,64},{64,56},{72,... | collective-permute-start | bytes 1032200 | tf_op jit(solution)/shard_map/ppermute | solution.py:442
  85.6 1.9 %collective-permute-start.6 = (f32[84,8,128]{2,1,0:T(8,128)}, f32[84,8,128]{2,1,0:T(8,128)S(1)}, u32[]{:S(2)}, u32[]{:S(2)}) collective-permute-start(f32[84,8,128]{2,1,0:T(8,128)} %get-tuple-element.15), channel_id=1, source_target_pairs={{0,8},{8,0},{16,24},{24,16},{32,40},{40,32},{48,56},{56,48},{64,72... | collective-permute-start | bytes 1032200 | tf_op jit(solution)/shard_map/ppermute | solution.py:441
  87.6 2.4 %collective-permute-start.8 = (f32[2,32,128]{2,1,0:T(8,128)S(1)}, f32[2,32,128]{2,1,0:T(8,128)S(1)}, u32[]{:S(2)}, u32[]{:S(2)}) collective-permute-start(f32[2,32,128]{2,1,0:T(8,128)S(1)} %get-tuple-element.24), channel_id=1, source_target_pairs={{0,8},{8,0},{16,24},{24,16},{32,40},{40,32},{48,56},{56,48},{64,72... | collective-permute-start | bytes 98312 | tf_op jit(solution)/shard_map/ppermute | solution.py:431
  90.0 2.9 %collective-permute-start.7 = (f32[2,32,128]{2,1,0:T(8,128)S(1)}, f32[2,32,128]{2,1,0:T(8,128)S(1)}, u32[]{:S(2)}, u32[]{:S(2)}) collective-permute-start(f32[2,32,128]{2,1,0:T(8,128)S(1)} %get-tuple-element.25), channel_id=1, source_target_pairs={{8,16},{16,8},{24,32},{32,24},{40,48},{48,40},{56,64},{64,56},{72,... | collective-permute-start | bytes 98312 | tf_op jit(solution)/shard_map/ppermute | solution.py:430
  92.9 25.8 %collective-permute-done.7.far_ref = f32[2,32,128]{2,1,0:T(8,128)S(1)} collective-permute-done((f32[2,32,128]{2,1,0:T(8,128)S(1)}, f32[2,32,128]{2,1,0:T(8,128)S(1)}, u32[]{:S(2)}, u32[]{:S(2)}) %collective-permute-start.7) | collective-permute-done | bytes 32800 | tf_op jit(solution)/shard_map/ppermute | solution.py:430
  118.7 0.9 copy-done.18
  119.6 0.7 copy-done.22
  120.3 0.7 copy-done.24
  121.0 0.6 ghost_kernel.1.g_ref
  121.6 0.0 collective-permute-done.5.far_ref
  121.6 0.0 collective-permute-done.6.near_ref
  121.6 0.0 copy-start.2
  121.7 1.0 copy-done.2
  122.6 1.0 copy-done.8
  123.6 4.6 %window_kernel.1 = (f32[3,3,8,24,128]{4,3,2,1,0:T(8,128)}, f32[3,3,8,24,128]{4,3,2,1,0:T(8,128)}) custom-call(s32[14]{0:T(128)S(1)} %copy-done.22, f32[84,8,128]{2,1,0:T(8,128)S(1)} %collective-permute-done.5.far_ref, f32[84,8,128]{2,1,0:T(8,128)S(1)} %collective-permute-done.6.near_ref, f32[3,8,32,128]{3,2,1,0:T(8,128)S(1)} %copy-done.8, ...), custom_call_target="tpu_custom_call" | custom-call | tf_op jit(solution)/shard_map/window_kernel/pallas_call | solution.py:452
  (44 shorter events, 0.2 us)
Async XLA Ops:
  0.6 9.4 %copy-start.25 = (f32[4,12,64]{2,0,1:T(4,128)S(1)}, f32[4,12,64]{2,0,1:T(4,128)}, u32[]{:S(2)}) copy-start(f32[4,12,64]{2,0,1:T(4,128)} %param.13) | copy-start | bytes 36868
  0.6 25.2 %copy-start.6 = (s32[8,24,128]{2,1,0:T(8,128)S(1)}, s32[8,24,128]{2,1,0:T(8,128)}, u32[]{:S(2)}) copy-start(s32[8,24,128]{2,1,0:T(8,128)} %m_ref.1) | copy-start | bytes 294916
  1.5 8.5 %collective-permute-start.1 = (f32[4,128]{1,0:T(4,128)S(1)}, f32[4,128]{1,0:T(4,128)S(1)}, u32[]{:S(2)}, u32[]{:S(2)}) collective-permute-start(f32[4,128]{1,0:T(4,128)S(1)} %reshape.37), channel_id=1, source_target_pairs={{1,0},{2,1},{3,2},{4,3},{5,4},{6,5},{7,6},{9,8},{10,9},{11,10},{12... | collective-permute-start | bytes 6152 | tf_op jit(solution)/shard_map/ppermute | solution.py:382
  3.6 6.5 %collective-permute-start = (f32[4,128]{1,0:T(4,128)S(1)}, f32[4,128]{1,0:T(4,128)S(1)}, u32[]{:S(2)}, u32[]{:S(2)}) collective-permute-start(f32[4,128]{1,0:T(4,128)S(1)} %reshape.35), channel_id=1, source_target_pairs={{0,1},{1,2},{2,3},{3,4},{4,5},{5,6},{6,7},{8,9},{9,10},{10,11},{11... | collective-permute-start | bytes 6152 | tf_op jit(solution)/shard_map/ppermute | solution.py:381
  10.3 16.8 %collective-permute-start.2 = (f32[4,8,128]{2,0,1:T(4,128)S(1)}, f32[4,8,128]{2,0,1:T(4,128)S(1)}, u32[]{:S(2)}, u32[]{:S(2)}) collective-permute-start(f32[4,8,128]{2,0,1:T(4,128)S(1)} %pad_maximum_fusion.5), channel_id=1, source_target_pairs={{0,504},{8,16},{16,8},{24,32},{32,24},{40,48},{48,40},{56,64},{64,... | collective-permute-start | bytes 49160 | tf_op jit(solution)/shard_map/ppermute | solution.py:398
  28.3 33.4 %all-to-all-start = ((f32[32,8,8,128]{3,2,1,0:T(8,128)}), f32[32,8,8,128]{3,2,1,0:T(8,128)S(1)}, u32[]{:S(2)}, u32[]{:S(2)}) async-start(f32[32,8,8,128]{3,2,1,0:T(8,128)} %broadcast_in_dim.36), calls=%async_computation | async-start | bytes 2097152 | tf_op jit(solution)/shard_map/all_to_all | solution.py:401
  33.9 7.3 %copy-start.27 = (s32[64]{0:T(128)S(1)}, s32[64]{0:T(128)}, u32[]{:S(2)}) copy-start(s32[64]{0:T(128)} %param.14) | copy-start | bytes 772
  34.0 8.3 %copy-start.26 = (s32[6]{0:T(128)S(1)}, s32[6]{0:T(128)}, u32[]{:S(2)}) copy-start(s32[6]{0:T(128)} %param.15) | copy-start | bytes 76
  34.1 13.1 %collective-permute-start.3 = (f32[176,4,128]{2,1,0:T(4,128)S(1)}, f32[176,4,128]{2,1,0:T(4,128)S(1)}, u32[]{:S(2)}, u32[]{:S(2)}) collective-permute-start(f32[176,4,128]{2,1,0:T(4,128)S(1)} %pad_maximum_fusion), channel_id=1, source_target_pairs={{0,1},{1,2},{2,3},{3,4},{4,5},{5,6},{6,7},{8,9},{9,10},{10,11},{11... | collective-permute-start | bytes 1081352 | tf_op jit(solution)/shard_map/ppermute | solution.py:395
  39.3 13.3 %collective-permute-start.4 = (f32[176,4,128]{2,1,0:T(4,128)S(1)}, f32[176,4,128]{2,1,0:T(4,128)S(1)}, u32[]{:S(2)}, u32[]{:S(2)}) collective-permute-start(f32[176,4,128]{2,1,0:T(4,128)S(1)} %pad_maximum_fusion.1), channel_id=1, source_target_pairs={{1,0},{2,1},{3,2},{4,3},{5,4},{6,5},{7,6},{9,8},{10,9},{11,10},{12... | collective-permute-start | bytes 1081352 | tf_op jit(solution)/shard_map/ppermute | solution.py:396
  47.2 0.7 copy-start.9
  52.6 0.7 copy-start.11
  53.4 1.2 copy-start.3
  54.5 1.2 copy-start.4
  55.7 1.0 copy-start.5
  56.7 1.0 copy-start.10
  57.6 1.0 copy-start.12
  58.6 3.0 %copy-start.19 = (f32[32,16]{1,0:T(8,128)S(1)}, f32[32,16]{1,0:T(8,128)}, u32[]{:S(2)}) copy-start(f32[32,16]{1,0:T(8,128)} %constant.105.clone.wy_ref) | copy-start | bytes 6148
  59.7 0.7 copy-start
  60.5 0.6 copy-start.13
  61.1 0.6 copy-start.20
  61.7 1.0 copy-start.1
  62.7 0.9 copy-start.14
  63.6 0.9 copy-start.16
  64.5 0.7 copy-start.21
  65.2 0.7 copy-start.23
  65.8 21.7 %copy-start.15 = (f32[8,32,128]{2,1,0:T(8,128)S(1)}, f32[8,32,128]{2,1,0:T(8,128)}, u32[]{:S(2)}) copy-start(f32[8,32,128]{2,1,0:T(8,128)} %copy-done.13) | copy-start | bytes 393220
  69.4 0.7 copy-start.7
  70.2 0.6 copy-start.17
  70.8 50.8 %collective-permute-start.5 = (f32[84,8,128]{2,1,0:T(8,128)}, f32[84,8,128]{2,1,0:T(8,128)S(1)}, u32[]{:S(2)}, u32[]{:S(2)}) collective-permute-start(f32[84,8,128]{2,1,0:T(8,128)} %get-tuple-element.14), channel_id=1, source_target_pairs={{8,16},{16,8},{24,32},{32,24},{40,48},{48,40},{56,64},{64,56},{72,... | collective-permute-start | bytes 1032200 | tf_op jit(solution)/shard_map/ppermute | solution.py:442
  85.6 36.0 %collective-permute-start.6 = (f32[84,8,128]{2,1,0:T(8,128)}, f32[84,8,128]{2,1,0:T(8,128)S(1)}, u32[]{:S(2)}, u32[]{:S(2)}) collective-permute-start(f32[84,8,128]{2,1,0:T(8,128)} %get-tuple-element.15), channel_id=1, source_target_pairs={{0,8},{8,0},{16,24},{24,16},{32,40},{40,32},{48,56},{56,48},{64,72... | collective-permute-start | bytes 1032200 | tf_op jit(solution)/shard_map/ppermute | solution.py:441
  87.6 5.4 %collective-permute-start.8 = (f32[2,32,128]{2,1,0:T(8,128)S(1)}, f32[2,32,128]{2,1,0:T(8,128)S(1)}, u32[]{:S(2)}, u32[]{:S(2)}) collective-permute-start(f32[2,32,128]{2,1,0:T(8,128)S(1)} %get-tuple-element.24), channel_id=1, source_target_pairs={{0,8},{8,0},{16,24},{24,16},{32,40},{40,32},{48,56},{56,48},{64,72... | collective-permute-start | bytes 98312 | tf_op jit(solution)/shard_map/ppermute | solution.py:431
  90.0 28.8 %collective-permute-start.7 = (f32[2,32,128]{2,1,0:T(8,128)S(1)}, f32[2,32,128]{2,1,0:T(8,128)S(1)}, u32[]{:S(2)}, u32[]{:S(2)}) collective-permute-start(f32[2,32,128]{2,1,0:T(8,128)S(1)} %get-tuple-element.25), channel_id=1, source_target_pairs={{8,16},{16,8},{24,32},{32,24},{40,48},{48,40},{56,64},{64,56},{72,... | collective-permute-start | bytes 98312 | tf_op jit(solution)/shard_map/ppermute | solution.py:430
  118.7 0.9 copy-start.18
  119.6 0.7 copy-start.22
  120.3 0.7 copy-start.24
  121.6 1.0 copy-start.2
  122.6 1.0 copy-start.8

commit v2 on v1

v2 whole, which is shorter than its diff:
```python
import jax
import jax.numpy as jnp
import numpy as np
from jax import lax
from jax.experimental import pallas as pl
from jax.experimental.pallas import tpu as pltpu
from jax.sharding import PartitionSpec as P

STEPS = 4
PLANES = 8
OWN = 24
ROWS = 32
HALO = 4
LANES = 128
FIRST_TILES = 8
COARSE = 6
TILES = 21

sharpness = 8.0
thresholds = (0.7, 0.5, 0.3)
time_step = 0.5

INTERPRET = False


def lane_ids():
    return lax.broadcasted_iota(jnp.int32, (ROWS, LANES), 1)


def row_ids():
    rows = lax.broadcasted_iota(jnp.int32, (ROWS, LANES), 0)
    return jnp.where(rows < OWN + HALO, rows, rows - ROWS)


def y_forward(a):
    return pltpu.roll(a, ROWS - 1, 0) - a


def y_backward(a):
    return a - pltpu.roll(a, 1, 0)


def z_forward(a, lanes):
    return jnp.where(lanes == LANES - 1, 0.0, pltpu.roll(a, LANES - 1, 1)) - a


def z_backward(a, lanes):
    return a - jnp.where(lanes == 0, 0.0, pltpu.roll(a, 1, 1))


def next_magnetic(h, e, e_up, step, lanes):
    up_y, up_z = e_up
    curl_x = y_forward(e[2]) - z_forward(e[1], lanes)
    curl_y = z_forward(e[0], lanes) - (up_z - e[2])
    curl_z = (up_y - e[1]) - y_forward(e[0])
    return [h[0] - step * curl_x, h[1] - step * curl_y, h[2] - step * curl_z]


def next_electric(e, h, h_down, coefficient, current, lanes):
    down_y, down_z = h_down
    curls = [
        y_backward(h[2]) - z_backward(h[1], lanes),
        z_backward(h[0], lanes) - (h[2] - down_z),
        (h[1] - down_y) - y_backward(h[0]),
    ]
    if current is not None:
        curls = [curls[c] - current[c] for c in range(3)]
    return [e[c] + coefficient * curls[c] for c in range(3)]


def step_of_rows(narrow_place):
    return jnp.where((row_ids() < 0) & (narrow_place == 0), 0.0, time_step)


WIDE, NARROW, CORE, WIDE_COUNT, NARROW_COUNT, BOX, MINE, THEIRS = 0, 1, 2, 3, 4, 5, 11, 17
E_AT, H_AT, J_AT, MASK_AT, HALO_PLANES = 0, 72, 144, 168, 176


def tiles_of(plane, count=4):
    return [plane[8 * i : 8 * i + 8] for i in range(count)]


def select(condition, yes, no):
    return [jnp.where(condition, a, b) for a, b in zip(yes, no, strict=True)]


def tile_rows_kernel(tile_ref, first_ref, last_ref):
    first_ref[...] = jnp.concatenate([tile_ref[0], tile_ref[1]], axis=1)
    last_ref[...] = jnp.concatenate([tile_ref[10], tile_ref[11]], axis=1)


def pack_kernel(e_first, e_last, h_first, h_last, j_first, j_last, m_first, m_last, first_ref, last_ref):
    for at, count, first, last in (
        (E_AT, 72, e_first, e_last),
        (H_AT, 72, h_first, h_last),
        (J_AT, 24, j_first, j_last),
        (MASK_AT, PLANES, m_first, m_last),
    ):
        first_ref[at : at + count] = first[:, :HALO].astype(jnp.float32)
        last_ref[at : at + count] = last[:, 8 - HALO :].astype(jnp.float32)


def tile_kernel(table, tile_ref, lo_ref, hi_ref, spread_ref):
    top = table[NARROW] == table[NARROW_COUNT] - 1
    for q in range(4):
        tile = jnp.concatenate([tile_ref[row, q : q + 1] for row in range(12)], axis=0)
        lo, hi = lo_ref[q : q + 1], hi_ref[q : q + 1]
        above = jnp.concatenate([hi[:, :64], hi[:, 64:]], axis=0)
        above = jnp.where(top, jnp.broadcast_to(tile[11:12], (2, 64)), above)
        first = jnp.concatenate([lo[:, :64], lo[:, 64:], tile[:6]], axis=0)
        second = jnp.concatenate([tile[6:], above], axis=0)
        packed = jnp.concatenate([first, second], axis=1)
        for i in range(spread_ref.shape[0]):
            spread_ref[i, q] = packed


def select_kernel(table, g_ref, message_ref, mine_ref, far_ref):
    for at, ref in ((MINE, mine_ref), (THEIRS, far_ref)):
        for i, (which, q) in enumerate(((0, 3), (1, 0), (1, 1), (1, 2), (1, 3), (2, 0))):
            held = g_ref[table[at + which] * 4 + q]
            ref[i] = jnp.where(table[at + 3 + which] == 1, held, 0.0)
    for i in range(3 * FIRST_TILES + 4):
        far_ref[COARSE + i] = message_ref[i]


def extend_kernel(
    table, e_ref, h_ref, j_ref, m_ref, lo_ref, hi_ref, ee_ref, h1_ref, jj_ref, mm_ref, far_ref, near_ref
):
    r = pl.program_id(0)
    lanes = lane_ids()
    step = step_of_rows(table[NARROW])
    core = table[CORE]
    zero = jnp.zeros((ROWS, LANES), jnp.float32)

    def extended(own, at):
        return jnp.concatenate([own, hi_ref[at], lo_ref[at]], axis=0)

    up = [zero] * 3
    upward = downward = None
    for p in range(PLANES - 1, -1, -1):
        at = r * 24 + p
        e = [extended(e_ref[0, c, p], E_AT + at + c * PLANES) for c in range(3)]
        h = [extended(h_ref[0, c, p], H_AT + at + c * PLANES) for c in range(3)]
        new = next_magnetic(h, e, (up[1], up[2]), step, lanes)
        for c in range(3):
            ee_ref[0, c, p] = e[c]
            h1_ref[0, c, p] = new[c]
        if p == PLANES - 1:
            upward = tiles_of(new[1]) + tiles_of(new[2])
        if p == 0:
            downward = tiles_of(e[1]) + tiles_of(e[2])
        up = e
    far, near = select(core == 1, upward, downward), select(core == 1, downward, upward)
    for i in range(FIRST_TILES):
        far_ref[r * FIRST_TILES + i] = far[i]
        near_ref[r * FIRST_TILES + i] = near[i]

    @pl.when(r == 0)
    def _():
        for p in range(PLANES):
            for c in range(3):
                jj_ref[c, p] = extended(j_ref[c, p], J_AT + c * PLANES + p)
            mm_ref[p] = extended(m_ref[p].astype(jnp.float32), MASK_AT + p)
        above, below = tiles_of(mm_ref[PLANES - 1]), tiles_of(mm_ref[0])
        far, near = select(core == 1, above, below), select(core == 1, below, above)
        for i in range(4):
            far_ref[3 * FIRST_TILES + i] = far[i]
            near_ref[3 * FIRST_TILES + i] = near[i]


def coefficients_of(density, mask, global_x, table, levels, lanes):
    m0, m1 = levels[0], levels[1]
    global_y = table[NARROW] * OWN + row_ids()
    inside = (
        (global_x >= table[BOX])
        & (global_x < table[BOX + 1])
        & (global_y >= table[BOX + 2])
        & (global_y < table[BOX + 3])
        & (lanes >= table[BOX + 4])
        & (lanes < table[BOX + 5])
    )
    in_grid = (
        (global_x >= 0)
        & (global_x < table[WIDE_COUNT] * PLANES)
        & (global_y >= 0)
        & (global_y < table[NARROW_COUNT] * OWN)
    )
    background = jnp.where(mask > 0.5, m1, m0)
    out = []
    for threshold in thresholds:
        base = float(np.tanh(sharpness * threshold))
        scale = 1.0 / (base + float(np.tanh(sharpness * (1.0 - threshold))))
        projected = (base + jnp.tanh(sharpness * (density - threshold))) * scale
        permittivity = jnp.where(inside, m0 + projected * (m1 - m0), background)
        out.append(jnp.where(in_grid, time_step / permittivity, 0.0))
    return out


def first_message(ref, at):
    return [jnp.concatenate([ref[at + 4 * c + i] for i in range(4)], axis=0) for c in range(2)]


def first_state(r, table, ee_ref, h1_ref, far_ref, near_ref, step):
    core = table[CORE]
    far, near = first_message(far_ref, COARSE + r * FIRST_TILES), first_message(near_ref, r * FIRST_TILES)
    trace_h = [jnp.where(table[WIDE] == 0, 0.0, x) for x in select(core == 0, far, near)]
    trace_e = [jnp.where(table[WIDE] == table[WIDE_COUNT] - 1, 0.0, x) for x in select(core == 1, far, near)]
    e = {p: [ee_ref[0, c, p] for c in range(3)] for p in range(PLANES)}
    h = {p: [h1_ref[0, c, p] for c in range(3)] for p in range(PLANES)}
    top = PLANES - 1
    h[top] = [h[top][0], h[top][1] + step * trace_e[1], h[top][2] - step * trace_e[0]]
    below = jnp.where(table[WIDE] == 0, 0.0, step)
    h[-1] = [None, trace_h[0] + below * e[0][2], trace_h[1] - below * e[0][1]]
    return e, h


def as_message(traces):
    rows = lax.broadcasted_iota(jnp.int32, (8, LANES), 0)
    tiles = []
    for n in range(3):
        for c in range(2):
            tiles += tiles_of(traces[n][c], 3)
    halo = [[traces[n][c][OWN:] for c in range(2)] for n in range(3)]
    for c in range(2):
        tiles.append(jnp.where((rows > 1) & (rows < 5), pltpu.roll(halo[1][c], 4, 0), halo[0][c]))
    tiles.append(jnp.where(rows == 3, pltpu.roll(halo[2][1], 4, 0), halo[2][0]))
    return tiles


def from_message(tile):
    traces = []
    for n in range(3):
        step = []
        for c in range(2):
            halo = tile(20) if n == 2 else tile(18 + c)
            halo = pltpu.roll(halo, 4, 0) if n == 1 or (n == 2 and c == 1) else halo
            step.append(jnp.concatenate([tile((n * 2 + c) * 3 + i) for i in range(3)] + [halo], axis=0))
        traces.append(step)
    return traces


def refine(table, mine_ref, far_ref, wz_ref, wy_ref, d_ref):
    last = table[WIDE] == table[WIDE_COUNT] - 1
    coarse = [mine_ref[q] + far_ref[q] for q in range(COARSE)]
    coarse[5] = jnp.where(last, coarse[4], coarse[5])
    along_z = jnp.dot(
        jnp.concatenate(coarse, axis=0),
        wz_ref[...],
        precision=lax.Precision.HIGHEST,
        preferred_element_type=jnp.float32,
    )
    strips = [
        jnp.concatenate([along_z[8 * q : 8 * q + 8, :LANES], along_z[8 * q : 8 * q + 8, LANES:]], axis=0)
        for q in range(COARSE)
    ]
    along_y = jnp.dot(
        wy_ref[...],
        jnp.concatenate(strips, axis=1),
        precision=lax.Precision.HIGHEST,
        preferred_element_type=jnp.float32,
    )
    for q in range(COARSE):
        d_ref[q] = along_y[:, LANES * q : LANES * (q + 1)]


def plane_coefficients(p, mask, table, levels, d_ref, c_ref):
    q = 1 + p // 2
    density = d_ref[q] if p % 2 == 0 else 0.5 * (d_ref[q] + d_ref[q + 1])
    values = coefficients_of(density, mask, table[WIDE] * PLANES + p, table, levels, lane_ids())
    for r in range(3):
        c_ref[r, p + 1] = values[r]


def trace_kernel(
    table, levels, mine_ref, wz_ref, wy_ref, mm_ref, far_ref, near_ref, ee_ref, h1_ref, jj_ref,
    far_out, near_out, c_ref, d_ref,
):
    r = pl.program_id(0)

    @pl.when(r == 0)
    def _():
        refine(table, mine_ref, far_ref, wz_ref, wy_ref, d_ref)
        for p in (0, 1, 2, 5, 6, 7):
            plane_coefficients(p, mm_ref[p], table, levels, d_ref, c_ref)

    lanes = lane_ids()
    step = step_of_rows(table[NARROW])
    core = table[CORE]
    zero = jnp.zeros((ROWS, LANES), jnp.float32)
    e, h = first_state(r, table, ee_ref, h1_ref, far_ref, near_ref, step)

    def electric(p):
        current = [jj_ref[c, p] for c in range(3)]
        e[p] = next_electric(e[p], h[p], (h[p - 1][1], h[p - 1][2]), c_ref[r, p + 1], current, lanes)

    def magnetic(p):
        h[p] = next_magnetic(h[p], e[p], (e[p + 1][1], e[p + 1][2]), step, lanes)

    for p in (0, 1, 2, 5, 6, 7):
        electric(p)
    h[-1] = [zero] * 3
    e[8] = [zero] * 3
    upward, downward = [], [(e[0][1], e[0][2])]
    for first in (5, 6, 7):
        for p in range(first, 8):
            magnetic(p)
        upward.append((h[7][1], h[7][2]))
        for p in range(first + 1, 8):
            electric(p)
    for last_plane in (1, 0):
        for p in range(last_plane + 1):
            magnetic(p)
        for p in range(last_plane + 1):
            electric(p)
        downward.append((e[0][1], e[0][2]))
    for i, (a, b) in enumerate(zip(as_message(upward), as_message(downward), strict=True)):
        far_out[r * TILES + i] = jnp.where(core == 1, a, b)
        near_out[r * TILES + i] = jnp.where(core == 1, b, a)


def inner_kernel(
    table, levels, mine_ref, wz_ref, wy_ref, mm_ref, far_ref, near_ref, ee_ref, h1_ref, jj_ref,
    eo_ref, ho_ref, c_ref, d_ref,
):
    r = pl.program_id(0)

    @pl.when(r == 0)
    def _():
        refine(table, mine_ref, far_ref, wz_ref, wy_ref, d_ref)
        core = table[CORE]
        far = jnp.concatenate([far_ref[COARSE + 3 * FIRST_TILES + i] for i in range(4)], axis=0)
        near = jnp.concatenate([near_ref[3 * FIRST_TILES + i] for i in range(4)], axis=0)
        for p in range(-1, PLANES + 1):
            if p < 0:
                mask = jnp.where(core == 0, far, near)
            else:
                mask = mm_ref[p] if p < PLANES else jnp.where(core == 1, far, near)
            plane_coefficients(p, mask, table, levels, d_ref, c_ref)

    lanes = lane_ids()
    step = step_of_rows(table[NARROW])
    e, h = first_state(r, table, ee_ref, h1_ref, far_ref, near_ref, step)

    def electric(first, last):
        for p in range(first, last + 1):
            current = [jj_ref[c, p] for c in range(3)]
            e[p] = next_electric(e[p], h[p], (h[p - 1][1], h[p - 1][2]), c_ref[r, p + 1], current, lanes)

    def magnetic(first, last):
        for p in range(first, last + 1):
            h[p] = next_magnetic(h[p], e[p], (e[p + 1][1], e[p + 1][2]), step, lanes)

    electric(0, 7)
    magnetic(0, 6)
    electric(1, 6)
    magnetic(1, 5)
    electric(2, 5)
    magnetic(2, 4)
    electric(3, 4)
    for p in range(PLANES):
        for c in range(3):
            eo_ref[0, c, p] = e[p][c]
            ho_ref[0, c, p] = h[p][c]


def window_kernel(table, c_ref, far_ref, near_ref, ee_ref, hh_ref, jj_ref, eo_ref, ho_ref):
    r = pl.program_id(0)
    lanes = lane_ids()
    core = table[CORE]
    step = step_of_rows(table[NARROW])
    below = jnp.where(table[WIDE] == 0, 0.0, step)
    zero = jnp.zeros((ROWS, LANES), jnp.float32)

    def tile_from_below(i):
        return jnp.where(core == 0, far_ref[r * TILES + i], near_ref[r * TILES + i])

    def tile_from_above(i):
        return jnp.where(core == 1, far_ref[r * TILES + i], near_ref[r * TILES + i])

    trace_h = from_message(tile_from_below)
    trace_e = from_message(tile_from_above)
    e = {p: [zero] * 3 for p in (-2, -1, 8, 9)}
    h = {p: [zero] * 3 for p in (-2, -1, 8)}
    for p in range(PLANES):
        e[p] = [ee_ref[0, c, p] for c in range(3)]
        h[p] = [hh_ref[0, c, p] for c in range(3)]

    def magnetic(planes, n):
        for p in planes:
            up = [e[p + 1][1], e[p + 1][2]]
            if p == 7:
                up = [up[0] + trace_e[n - 2][0], up[1] + trace_e[n - 2][1]]
            h[p] = next_magnetic(h[p], e[p], up, below if p < 0 else step, lanes)

    def electric(planes, n):
        for p in planes:
            down = [h[p - 1][1], h[p - 1][2]]
            if p == 0:
                down = [down[0] + trace_h[n - 2][0], down[1] + trace_h[n - 2][1]]
            current = [jj_ref[c, p] for c in range(3)] if 0 <= p < PLANES else None
            e[p] = next_electric(e[p], h[p], down, c_ref[0, p + 1], current, lanes)

    magnetic((-1, 7), 2)
    electric((0, 7, 8), 2)
    e[-1] = next_electric(e[-1], h[-1], (zero, zero), c_ref[0, 0], None, lanes)
    magnetic((-2, -1, 0, 6, 7, 8), 3)
    electric((-1, 0, 1, 6, 7, 8), 3)
    magnetic((-1, 0, 1, 5, 6, 7), 4)
    electric((0, 1, 2, 5, 6, 7), 4)
    for p in range(PLANES):
        for c in range(3):
            eo_ref[0, c, p] = e[p][c][:OWN]
            ho_ref[0, c, p] = h[p][c][:OWN]


def refine_weights():
    along_z = np.zeros((64, LANES), np.float32)
    for cell in range(LANES):
        along_z[cell // 2, cell] += 0.5
        along_z[min((cell + 1) // 2, 63), cell] += 0.5
    both = np.zeros((LANES, 2 * LANES), np.float32)
    both[:64, :LANES] = along_z
    both[64:, LANES:] = along_z
    along_y = np.zeros((ROWS, 16), np.float32)
    for row in range(ROWS):
        y = row if row < OWN + HALO else row - ROWS
        along_y[row, y // 2 + 2] += 0.5
        along_y[row, min((y + 1) // 2 + 2, 15)] += 0.5
    return both, along_y


def run(kernel, scalars, operands, outs, flops, scratch=(), steps=3, limit=60):
    def spec(shape, block):
        rank = len(shape)
        if block is None:
            return pl.BlockSpec(tuple(shape), lambda r: (0,) * rank)
        if block is True:
            return pl.BlockSpec((1, *shape[1:]), lambda r: (r,) + (0,) * (rank - 1))
        block_shape, place = block
        return pl.BlockSpec(block_shape, lambda r: place)

    moved = sum(4 * int(np.prod(x.shape)) for x, _ in operands) + sum(4 * int(np.prod(x)) for x, _ in outs)
    return pl.pallas_call(
        kernel,
        grid=(steps,),
        in_specs=[pl.BlockSpec(memory_space=pltpu.SMEM)] * len(scalars)
        + [spec(x.shape, block) for x, block in operands],
        out_specs=[spec(shape, block) for shape, block in outs],
        out_shape=[jax.ShapeDtypeStruct(shape, jnp.float32) for shape, _ in outs],
        scratch_shapes=list(scratch),
        compiler_params=pltpu.CompilerParams(
            dimension_semantics=("arbitrary",), vmem_limit_bytes=limit * 1024 * 1024
        ),
        cost_estimate=pl.CostEstimate(flops=flops, bytes_accessed=moved, transcendentals=0),
        interpret=INTERPRET,
        name=kernel.__name__,
    )(*scalars, *[x for x, _ in operands])


def body(
    electric,
    magnetic,
    current,
    density_tiles,
    tile_slabs,
    design_box,
    material_mask,
    material_levels,
):
    wide_count = lax.axis_size("wide")
    wide_place = lax.axis_index("wide")
    narrow_count = lax.axis_size("narrow")
    narrow_place = lax.axis_index("narrow")
    core = wide_place % 2
    half = wide_count // 2

    near_pairs = [(w, w ^ 1) for w in range(wide_count)]
    partner = [(w + 1) % wide_count if w % 2 else (w - 1) % wide_count for w in range(wide_count)]
    far_ring = [(w, partner[w]) for w in range(wide_count)]
    far_pairs = [(w, partner[w]) for w in range(1, wide_count - 1)]
    up = [(n, n + 1) for n in range(narrow_count - 1)]
    down = [(n + 1, n) for n in range(narrow_count - 1)]
    groups = [[w for w in range(wide_count) if (w // 2) % 2 == side] for side in range(2)]

    mate = jnp.where(wide_place % 2 == 1, wide_place + 1, wide_place - 1 + wide_count) % wide_count
    slabs = jnp.stack([wide_place, mate])[:, None] + jnp.arange(-1, 2, dtype=jnp.int32)[None, :]
    slabs = jnp.clip(slabs, 0, wide_count - 1)
    ids = jnp.arange(wide_count, dtype=jnp.int32)
    at = jnp.sum(jnp.where(tile_slabs[None, None, :] == slabs[:, :, None], ids, 0), axis=2)
    here = ((at // 2) % 2 == (wide_place // 2) % 2).astype(jnp.int32)
    place = (at // 4) * 2 + at % 2
    table = jnp.concatenate(
        [
            jnp.stack([wide_place, narrow_place, core, jnp.int32(wide_count), jnp.int32(narrow_count)]),
            design_box,
            jnp.stack([place, here], axis=1).reshape(12),
        ]
    ).astype(jnp.int32)

    stack = [
        electric.reshape(72, OWN, LANES),
        magnetic.reshape(72, OWN, LANES),
        current.reshape(24, OWN, LANES),
        material_mask,
    ]
    ends = [(x, ((x.shape[0], 8, LANES), (0, row, 0))) for x in stack for row in (0, 2)]
    halo = (HALO_PLANES, HALO, LANES)
    first_rows, last_rows = run(pack_kernel, (), ends, [(halo, None), (halo, None)], 1_000_000, steps=1)
    tile = jnp.transpose(density_tiles, (1, 0, 2))
    tile_first, tile_last = run(
        tile_rows_kernel, (), [(tile, None)], [((4, LANES), None), ((4, LANES), None)], 1000, steps=1, limit=8
    )
    tile_lo = lax.ppermute(tile_last, "narrow", up)
    tile_hi = lax.ppermute(tile_first, "narrow", down)
    early, first_rows, last_rows = lax.optimization_barrier((table, first_rows, last_rows))
    (spread,) = run(
        tile_kernel,
        (early,),
        [(tile, None), (tile_lo, None), (tile_hi, None)],
        [((half, 4, 8, LANES), None)],
        1_000_000,
        steps=1,
        limit=8,
    )
    gathered = lax.all_to_all(spread, "wide", 0, 0, axis_index_groups=groups, tiled=True)
    gathered = gathered.reshape(half * 4, 8, LANES)

    low = lax.ppermute(last_rows, "narrow", up)
    high = lax.ppermute(first_rows, "narrow", down)

    extended = (3, 3, PLANES, ROWS, LANES)
    planes = (PLANES, ROWS, LANES)
    message = (3 * FIRST_TILES + 4, 8, LANES)
    e_ext, h_one, j_ext, m_ext, far, near = run(
        extend_kernel,
        (table,),
        [(electric, True), (magnetic, True), (current, None), (material_mask, None), (low, None), (high, None)],
        [(extended, True), (extended, True), ((3, *planes), None), (planes, None), (message, None), (message, None)],
        10_000_000,
    )
    near = lax.ppermute(near, "wide", near_pairs)

    mine, far = run(
        select_kernel,
        (table,),
        [(gathered, None), (far, None)],
        [((COARSE, 8, LANES), None), ((COARSE + message[0], 8, LANES), None)],
        1_000_000,
        steps=1,
        limit=8,
    )
    far = lax.ppermute(far, "wide", far_ring)
    fields = [(e_ext, True), (h_one, True), (j_ext, None)]

    weights_z, weights_y = refine_weights()
    message = (3 * TILES, 8, LANES)
    coefficients = (3, PLANES + 2, ROWS, LANES)
    strips = pltpu.VMEM((COARSE, ROWS, LANES), jnp.float32)
    inputs = [(x, None) for x in (mine, weights_z, weights_y, m_ext, far, near)] + fields
    far_end, near_end = run(
        trace_kernel,
        (table, material_levels),
        inputs,
        [(message, None), (message, None)],
        10_000_000,
        [pltpu.VMEM(coefficients, jnp.float32), strips],
    )
    near_end = lax.ppermute(near_end, "wide", near_pairs)
    far_end = lax.ppermute(far_end, "wide", far_pairs)

    e_in, h_in, coefficient = run(
        inner_kernel,
        (table, material_levels),
        inputs,
        [(extended, True), (extended, True), (coefficients, None)],
        10_000_000,
        [strips],
        limit=24,
    )
    own = (3, 3, PLANES, OWN, LANES)
    return tuple(
        run(
            window_kernel,
            (table,),
            [(coefficient, True), (far_end, None), (near_end, None), (e_in, True), (h_in, True), (j_ext, None)],
            [(own, True), (own, True)],
            10_000_000,
            limit=24,
        )
    )


def solution(mesh):
    return jax.shard_map(
        body,
        mesh=mesh,
        in_specs=(
            P(None, None, "wide", "narrow", None),
            P(None, None, "wide", "narrow", None),
            P(None, "wide", "narrow", None),
            P("wide", "narrow", None),
            P(),
            P(),
            P("wide", "narrow", None),
            P(),
        ),
        out_specs=(P(None, None, "wide", "narrow", None), P(None, None, "wide", "narrow", None)),
        check_vma=False,
    )
```

time: 129 us -> 112 us (0.87)
  local copies, waits for them, and re-layouts: 25.6 us -> 6.38 us
  starting transfers between devices: 56.4 us -> 45.5 us
  Pallas kernels: 9.93 us -> 20 us
  waiting for transfers between devices: 34.8 us -> 37.7 us
    unnamed x56 -> x46, local copies, waits for them, and re-layouts: 18.5 us -> 5.47 us
    ppermute x6 -> x5, starting transfers between devices: 41.7 us -> 29.3 us  [the longest x1 11.9 us: body(): far = lax.ppermute(far, 'wide', far_ring)]
    pallas_call x4 -> x8, Pallas kernels: 9.93 us -> 20 us  [run(): pl.pallas_call(kernel, grid=(steps,), in_specs=[pl.BlockSpec(memory_space...]
    slice x7 -> x0, local copies, waits for them, and re-layouts: 3.74 us -> none  [the longest x3 2.32 us: body(): first_rows = jnp.concatenate([x[:, :HALO] for x in stack], axis=0)]
    ppermute x1, waiting for transfers between devices: 3.09 us -> 6.02 us  [body(): low = lax.ppermute(last_rows, 'narrow', up)]
    ppermute x6 -> x5, waiting for transfers between devices: 27 us -> 24.8 us  [the longest x1 12.7 us: body(): far_end = lax.ppermute(far_end, 'wide', far_pairs)]
    all_to_all x1, starting transfers between devices: 5.65 us -> 7.61 us  [body(): lax.all_to_all(spread, 'wide', 0, 0, axis_index_groups=groups, tiled=True)]
    ppermute x1, waiting for transfers between devices: 0.01 us -> 1.5 us  [body(): near = lax.ppermute(near, 'wide', near_pairs)]
  transfers between devices with their start and end apart: 10 -> 9, of which waited for: 4 -> 6; matrix products, arithmetic and copies ran while one was open for 4% -> 2% of each run, Pallas kernels for 1% -> 9%
where the time goes in v2:
time: 112 us
  starting transfers between devices  45.5 us (41%)
  waiting for transfers between devices  37.7 us (34%)
  Pallas kernels  20 us (18%)
  local copies, waits for them, and re-layouts  6.38 us (6%)
    pallas_call x8, Pallas kernels, run(): pl.pallas_call(kernel, grid=(steps,), in_specs=[pl.BlockSpec(memory_space...  20 us
    ppermute x1, waiting for transfers between devices, body(): far_end = lax.ppermute(far_end, 'wide', far_pairs)  12.7 us
    ppermute x1, starting transfers between devices, body(): far = lax.ppermute(far, 'wide', far_ring)  11.9 us
    ppermute x1, waiting for transfers between devices, body(): far = lax.ppermute(far, 'wide', far_ring)  11.8 us
    ppermute x1, starting transfers between devices, body(): far_end = lax.ppermute(far_end, 'wide', far_pairs)  8.49 us
    all_to_all x1, starting transfers between devices, body(): lax.all_to_all(spread, 'wide', 0, 0, axis_index_groups=groups, tiled=True)  7.61 us
    ppermute x1, waiting for transfers between devices, body(): low = lax.ppermute(last_rows, 'narrow', up)  6.02 us
    unnamed x46, local copies, waits for them, and re-layouts  5.47 us
  transfers between devices with their start and end apart: 9, of which 6 were waited for; matrix products, arithmetic and copies ran while one was open for 2% of the time, Pallas kernels for 9%

profile of v2, /device:TPU:102, one launch (start us, length us, event | category | flops | bytes accessed | tf_op | source)
XLA Modules:
  0.0 111.6 jit_solution(6978982321915695671)
XLA Ops:
  0.6 0.0 copy-start.12
  0.6 0.7 copy-done.12
  1.4 0.1 tile_rows_kernel.1
  1.4 5.0 %collective-permute-start = (f32[4,128]{1,0:T(4,128)S(1)}, f32[4,128]{1,0:T(4,128)S(1)}, u32[]{:S(2)}, u32[]{:S(2)}) collective-permute-start(f32[4,128]{1,0:T(4,128)S(1)} %get-tuple-element.25), channel_id=1, source_target_pairs={{0,1},{1,2},{2,3},{3,4},{4,5},{5,6},{6,7},{8,9},{9,10},{10,11},{11... | collective-permute-start | bytes 6152 | tf_op jit(solution)/shard_map/ppermute | solution.py:513
  6.5 1.9 %collective-permute-start.1 = (f32[4,128]{1,0:T(4,128)S(1)}, f32[4,128]{1,0:T(4,128)S(1)}, u32[]{:S(2)}, u32[]{:S(2)}) collective-permute-start(f32[4,128]{1,0:T(4,128)S(1)} %get-tuple-element.26), channel_id=1, source_target_pairs={{1,0},{2,1},{3,2},{4,3},{5,4},{6,5},{7,6},{9,8},{10,9},{11,10},{12... | collective-permute-start | bytes 6152 | tf_op jit(solution)/shard_map/ppermute | solution.py:514
  8.5 0.1 pad_add_fusion.1
  8.5 0.1 add_clamp_fusion
  8.6 0.9 fusion
  9.5 0.1 copy.13
  9.7 0.1 reshape.200
  9.7 0.7 concatenate.3.table
  10.5 2.3 %pack_kernel.1 = (f32[176,4,128]{2,1,0:T(4,128)}, f32[176,4,128]{2,1,0:T(4,128)}) custom-call(f32[72,24,128]{2,1,0:T(8,128)} %bitcast.30, f32[72,24,128]{2,1,0:T(8,128)} %bitcast.31, f32[72,24,128]{2,1,0:T(8,128)} %bitcast.32, f32[72,24,128]{2,1,0:T(8,128)} %bitcast.33, f32[24,24,128]{2,1,0:T(8,128)} %bitcast.34, f32[24,24,128]{2,1,0:T(8,128)} %bitcast.35, ...), custom_call_target="tpu_custom_call" | custom-call | flops 1000000 | bytes 5046272 | tf_op jit(solution)/shard_map/pack_kernel/pallas_call | solution.py:443
  12.8 0.0 collective-permute-done.lo_ref
  12.8 0.4 collective-permute-done.1.hi_ref
  13.2 0.0 copy-done.15
  13.2 0.0 copy-done.13
  13.2 1.5 %tile_kernel.1 = f32[32,4,8,128]{3,2,1,0:T(8,128)} custom-call(s32[23]{0:T(128)S(1)} %concatenate.3.table, f32[12,4,64]{2,1,0:T(4,128)S(1)} %bitcast.29, f32[4,128]{1,0:T(4,128)S(1)} %collective-permute-done.lo_ref, f32[4,128]{1,0:T(4,128)S(1)} %collective-permute-done.1.hi_ref), custom_call_target="tpu_custom_call" | custom-call | flops 1000000 | bytes 540672 | tf_op jit(solution)/shard_map/tile_kernel/pallas_call | solution.py:443
  14.7 7.6 %all-to-all-start = ((f32[32,4,8,128]{3,2,1,0:T(8,128)}), f32[32,4,8,128]{3,2,1,0:T(8,128)S(1)}, u32[]{:S(2)}, u32[]{:S(2)}) async-start(f32[32,4,8,128]{3,2,1,0:T(8,128)} %tile_kernel.1), calls=%async_computation | async-start | bytes 1048576 | tf_op jit(solution)/shard_map/all_to_all | solution.py:525
  22.3 0.0 copy-done.22
  22.3 0.0 copy-start.16
  22.3 4.8 %collective-permute-start.2 = (f32[176,4,128]{2,1,0:T(4,128)S(1)}, f32[176,4,128]{2,1,0:T(4,128)S(1)}, u32[]{:S(2)}, u32[]{:S(2)}) collective-permute-start(f32[176,4,128]{2,1,0:T(4,128)S(1)} %copy-done.22), channel_id=1, source_target_pairs={{0,1},{1,2},{2,3},{3,4},{4,5},{5,6},{6,7},{8,9},{9,10},{10,11},{11... | collective-permute-start | bytes 1081352 | tf_op jit(solution)/shard_map/ppermute | solution.py:528
  27.1 0.0 copy-done.21
  27.1 1.9 %collective-permute-start.3 = (f32[176,4,128]{2,1,0:T(4,128)S(1)}, f32[176,4,128]{2,1,0:T(4,128)S(1)}, u32[]{:S(2)}, u32[]{:S(2)}) collective-permute-start(f32[176,4,128]{2,1,0:T(4,128)S(1)} %copy-done.21), channel_id=1, source_target_pairs={{1,0},{2,1},{3,2},{4,3},{5,4},{6,5},{7,6},{9,8},{10,9},{11,10},{12... | collective-permute-start | bytes 1081352 | tf_op jit(solution)/shard_map/ppermute | solution.py:529
  29.1 6.0 %collective-permute-done.2.lo_ref = f32[176,4,128]{2,1,0:T(4,128)S(1)} collective-permute-done((f32[176,4,128]{2,1,0:T(4,128)S(1)}, f32[176,4,128]{2,1,0:T(4,128)S(1)}, u32[]{:S(2)}, u32[]{:S(2)}) %collective-permute-start.2) | collective-permute-done | bytes 360480 | tf_op jit(solution)/shard_map/ppermute | solution.py:528
  35.1 5.3 %collective-permute-done.3.hi_ref = f32[176,4,128]{2,1,0:T(4,128)S(1)} collective-permute-done((f32[176,4,128]{2,1,0:T(4,128)S(1)}, f32[176,4,128]{2,1,0:T(4,128)S(1)}, u32[]{:S(2)}, u32[]{:S(2)}) %collective-permute-start.3) | collective-permute-done | bytes 360480 | tf_op jit(solution)/shard_map/ppermute | solution.py:529
  40.4 0.0 copy-done.19
  40.4 0.7 copy-done.20
  41.2 4.4 %extend_kernel.1 = (f32[3,3,8,32,128]{4,3,2,1,0:T(8,128)}, f32[3,3,8,32,128]{4,3,2,1,0:T(8,128)}, f32[3,8,32,128]{3,2,1,0:T(8,128)}, f32[8,32,128]{2,1,0:T(8,128...) custom-call(s32[23]{0:T(128)} %copy-done.15, f32[3,3,8,24,128]{4,3,2,1,0:T(8,128)} %e_ref.1, ...), custom_call_target="tpu_custom_call" | custom-call | flops 10000000 | bytes 5996544 | tf_op jit(solution)/shard_map/extend_kernel/pallas_call | solution.py:443
  45.5 0.0 all-to-all-done
  45.6 0.0 copy-done.16
  45.6 0.0 copy-start.9
  45.6 0.9 copy-done.9
  46.5 0.6 select_kernel.1
  47.0 0.0 copy-start.10
  47.0 0.6 copy-done.10
  47.6 11.9 %collective-permute-start.4 = (f32[34,8,128]{2,1,0:T(8,128)S(1)}, f32[34,8,128]{2,1,0:T(8,128)S(1)}, u32[]{:S(2)}, u32[]{:S(2)}) collective-permute-start(f32[34,8,128]{2,1,0:T(8,128)S(1)} %get-tuple-element.32), channel_id=1, source_target_pairs={{0,504},{8,16},{16,8},{24,32},{32,24},{40,48},{48,40},{56,64},{64,... | collective-permute-start | bytes 417800 | tf_op jit(solution)/shard_map/ppermute | solution.py:552
  59.5 1.9 %collective-permute-start.5 = (f32[28,8,128]{2,1,0:T(8,128)}, f32[28,8,128]{2,1,0:T(8,128)S(1)}, u32[]{:S(2)}, u32[]{:S(2)}) collective-permute-start(f32[28,8,128]{2,1,0:T(8,128)} %get-tuple-element.33), channel_id=1, source_target_pairs={{0,8},{8,0},{16,24},{24,16},{32,40},{40,32},{48,56},{56,48},{64,72... | collective-permute-start | bytes 344072 | tf_op jit(solution)/shard_map/ppermute | solution.py:541
  61.5 1.5 %collective-permute-done.5.near_ref = f32[28,8,128]{2,1,0:T(8,128)S(1)} collective-permute-done((f32[28,8,128]{2,1,0:T(8,128)}, f32[28,8,128]{2,1,0:T(8,128)S(1)}, u32[]{:S(2)}, u32[]{:S(2)}) %collective-permute-start.5) | collective-permute-done | bytes 114720 | tf_op jit(solution)/shard_map/ppermute | solution.py:541
  63.0 11.8 %collective-permute-done.4.far_ref = f32[34,8,128]{2,1,0:T(8,128)S(1)} collective-permute-done((f32[34,8,128]{2,1,0:T(8,128)S(1)}, f32[34,8,128]{2,1,0:T(8,128)S(1)}, u32[]{:S(2)}, u32[]{:S(2)}) %collective-permute-start.4) | collective-permute-done | bytes 139296 | tf_op jit(solution)/shard_map/ppermute | solution.py:552
  74.7 0.0 copy-done.7
  74.7 0.6 copy-done.3
  75.4 0.0 copy-start.6
  75.4 0.0 copy-start.11
  75.4 0.0 copy-start.14
  75.4 0.0 copy-start.17
  75.4 0.0 copy-start.18
  75.4 5.0 %trace_kernel.1 = (f32[63,8,128]{2,1,0:T(8,128)}, f32[63,8,128]{2,1,0:T(8,128)}) custom-call(s32[23]{0:T(128)} %copy-done.15, f32[2]{0:T(128)} %levels.3, f32[6,8,128]{2,1,0:T(8,128)} %copy-done.10, f32[128,256]{1,0:T(8,128)} %constant.96.clone.wz_ref, f32[32,16]{1,0:T(8,128)} %constant.97.clone.wy_ref, f32[8,32,128]{2,1,0:T(8,128)} %get-tuple-element.31.mm_ref, ...), custom_call_target="tpu_custom_call" | custom-call | flops 10000000 | bytes 3811328 | tf_op jit(solution)/shard_map/trace_kernel/pallas_call | solution.py:443
  80.5 8.5 %collective-permute-start.6 = (f32[63,8,128]{2,1,0:T(8,128)}, f32[63,8,128]{2,1,0:T(8,128)S(1)}, u32[]{:S(2)}, u32[]{:S(2)}) collective-permute-start(f32[63,8,128]{2,1,0:T(8,128)} %get-tuple-element.38), channel_id=1, source_target_pairs={{8,16},{16,8},{24,32},{32,24},{40,48},{48,40},{56,64},{64,56},{72,... | collective-permute-start | bytes 774152 | tf_op jit(solution)/shard_map/ppermute | solution.py:569
  89.0 1.9 %collective-permute-start.7 = (f32[63,8,128]{2,1,0:T(8,128)}, f32[63,8,128]{2,1,0:T(8,128)S(1)}, u32[]{:S(2)}, u32[]{:S(2)}) collective-permute-start(f32[63,8,128]{2,1,0:T(8,128)} %get-tuple-element.39), channel_id=1, source_target_pairs={{0,8},{8,0},{16,24},{24,16},{32,40},{40,32},{48,56},{56,48},{64,72... | collective-permute-start | bytes 774152 | tf_op jit(solution)/shard_map/ppermute | solution.py:568
  90.9 0.0 copy-done
  90.9 0.0 copy-done.1
  90.9 0.0 copy-done.2
  90.9 0.0 copy-done.5
  90.9 0.0 copy-done.6
  90.9 0.0 copy-done.11
  91.0 0.0 copy-done.14
  91.0 0.0 copy-done.17
  91.0 0.0 copy-done.18
  91.0 0.9 copy-done.4
  91.9 0.9 copy-done.8
  92.8 3.1 %inner_kernel.1 = (f32[3,3,8,32,128]{4,3,2,1,0:T(8,128)S(1)}, f32[3,3,8,32,128]{4,3,2,1,0:T(8,128)S(1)}, f32[3,10,32,128]{3,2,1,0:T(8,128)S(1)}) custom-call(s32[23]{0:T(128)S(1)} %copy-done.17, f32[2]{0:T(128)S(1)} %copy-done.18, f32[6,8,128]{2,1,0:T(8,128)S(1)} %copy-done.11, f32[128,256]{1,0:T(8,128)S(1)} %copy-done.5, f32[32,16]{1,0:T(8,128)S(1)} %copy-done.14, ...), custom_call_target="tpu_custom_call" | custom-call | flops 10000000 | bytes 6146048 | tf_op jit(solution)/shard_map/inner_kernel/pallas_call | solution.py:443
  95.9 12.7 %collective-permute-done.6.far_ref = f32[63,8,128]{2,1,0:T(8,128)S(1)} collective-permute-done((f32[63,8,128]{2,1,0:T(8,128)}, f32[63,8,128]{2,1,0:T(8,128)S(1)}, u32[]{:S(2)}, u32[]{:S(2)}) %collective-permute-start.6) | collective-permute-done | bytes 258080 | tf_op jit(solution)/shard_map/ppermute | solution.py:569
  108.5 0.0 collective-permute-done.7.near_ref
  108.5 3.1 %window_kernel.1 = (f32[3,3,8,24,128]{4,3,2,1,0:T(8,128)}, f32[3,3,8,24,128]{4,3,2,1,0:T(8,128)}) custom-call(s32[23]{0:T(128)S(1)} %copy-done.17, f32[3,10,32,128]{3,2,1,0:T(8,128)S(1)} %get-tuple-element.37.c_ref, f32[63,8,128]{2,1,0:T(8,128)S(1)} %collective-permute-done.6.far_ref, f32[63,8,128]{2,1,0:T(8,128)S(1)} %collective-permute-done.7.near_ref, ...), custom_call_target="tpu_custom_call" | custom-call | flops 10000000 | bytes 5529600 | tf_op jit(solution)/shard_map/window_kernel/pallas_call | solution.py:443
  (19 shorter events, 0.1 us)
Async XLA Ops:
  0.6 0.7 copy-start.12
  1.4 11.3 %collective-permute-start = (f32[4,128]{1,0:T(4,128)S(1)}, f32[4,128]{1,0:T(4,128)S(1)}, u32[]{:S(2)}, u32[]{:S(2)}) collective-permute-start(f32[4,128]{1,0:T(4,128)S(1)} %get-tuple-element.25), channel_id=1, source_target_pairs={{0,1},{1,2},{2,3},{3,4},{4,5},{5,6},{6,7},{8,9},{9,10},{10,11},{11... | collective-permute-start | bytes 6152 | tf_op jit(solution)/shard_map/ppermute | solution.py:513
  6.5 6.7 %collective-permute-start.1 = (f32[4,128]{1,0:T(4,128)S(1)}, f32[4,128]{1,0:T(4,128)S(1)}, u32[]{:S(2)}, u32[]{:S(2)}) collective-permute-start(f32[4,128]{1,0:T(4,128)S(1)} %get-tuple-element.26), channel_id=1, source_target_pairs={{1,0},{2,1},{3,2},{4,3},{5,4},{6,5},{7,6},{9,8},{10,9},{11,10},{12... | collective-permute-start | bytes 6152 | tf_op jit(solution)/shard_map/ppermute | solution.py:514
  10.5 2.7 %copy-start.15 = (s32[23]{0:T(128)}, s32[23]{0:T(128)S(1)}, u32[]{:S(2)}) copy-start(s32[23]{0:T(128)S(1)} %concatenate.3.table) | copy-start | bytes 280
  10.5 2.7 %copy-start.13 = (f32[4,12,64]{2,0,1:T(4,128)S(1)}, f32[4,12,64]{2,0,1:T(4,128)}, u32[]{:S(2)}) copy-start(f32[4,12,64]{2,0,1:T(4,128)} %param.13) | copy-start | bytes 36868
  12.8 9.6 %copy-start.22 = (f32[176,4,128]{2,1,0:T(4,128)S(1)}, f32[176,4,128]{2,1,0:T(4,128)}, u32[]{:S(2)}) copy-start(f32[176,4,128]{2,1,0:T(4,128)} %get-tuple-element.27) | copy-start | bytes 1081348
  12.8 14.3 %copy-start.21 = (f32[176,4,128]{2,1,0:T(4,128)S(1)}, f32[176,4,128]{2,1,0:T(4,128)}, u32[]{:S(2)}) copy-start(f32[176,4,128]{2,1,0:T(4,128)} %get-tuple-element.28) | copy-start | bytes 1081348
  14.7 30.8 %all-to-all-start = ((f32[32,4,8,128]{3,2,1,0:T(8,128)}), f32[32,4,8,128]{3,2,1,0:T(8,128)S(1)}, u32[]{:S(2)}, u32[]{:S(2)}) async-start(f32[32,4,8,128]{3,2,1,0:T(8,128)} %tile_kernel.1), calls=%async_computation | async-start | bytes 1048576 | tf_op jit(solution)/shard_map/all_to_all | solution.py:525
  22.3 23.2 %copy-start.16 = (s32[23]{0:T(128)S(1)}, s32[23]{0:T(128)}, u32[]{:S(2)}) copy-start(s32[23]{0:T(128)} %copy-done.15) | copy-start | bytes 280
  22.3 12.7 %collective-permute-start.2 = (f32[176,4,128]{2,1,0:T(4,128)S(1)}, f32[176,4,128]{2,1,0:T(4,128)S(1)}, u32[]{:S(2)}, u32[]{:S(2)}) collective-permute-start(f32[176,4,128]{2,1,0:T(4,128)S(1)} %copy-done.22), channel_id=1, source_target_pairs={{0,1},{1,2},{2,3},{3,4},{4,5},{5,6},{6,7},{8,9},{9,10},{10,11},{11... | collective-permute-start | bytes 1081352 | tf_op jit(solution)/shard_map/ppermute | solution.py:528
  27.1 13.3 %collective-permute-start.3 = (f32[176,4,128]{2,1,0:T(4,128)S(1)}, f32[176,4,128]{2,1,0:T(4,128)S(1)}, u32[]{:S(2)}, u32[]{:S(2)}) collective-permute-start(f32[176,4,128]{2,1,0:T(4,128)S(1)} %copy-done.21), channel_id=1, source_target_pairs={{1,0},{2,1},{3,2},{4,3},{5,4},{6,5},{7,6},{9,8},{10,9},{11,10},{12... | collective-permute-start | bytes 1081352 | tf_op jit(solution)/shard_map/ppermute | solution.py:529
  35.1 5.3 %copy-start.19 = (f32[176,4,128]{2,1,0:T(4,128)}, f32[176,4,128]{2,1,0:T(4,128)S(1)}, u32[]{:S(2)}) copy-start(f32[176,4,128]{2,1,0:T(4,128)S(1)} %collective-permute-done.2.lo_ref) | copy-start | bytes 1081348
  40.4 0.7 copy-start.20
  45.6 0.9 copy-start.9
  47.0 0.6 copy-start.10
  47.6 27.1 %collective-permute-start.4 = (f32[34,8,128]{2,1,0:T(8,128)S(1)}, f32[34,8,128]{2,1,0:T(8,128)S(1)}, u32[]{:S(2)}, u32[]{:S(2)}) collective-permute-start(f32[34,8,128]{2,1,0:T(8,128)S(1)} %get-tuple-element.32), channel_id=1, source_target_pairs={{0,504},{8,16},{16,8},{24,32},{32,24},{40,48},{48,40},{56,64},{64,... | collective-permute-start | bytes 417800 | tf_op jit(solution)/shard_map/ppermute | solution.py:552
  59.5 3.4 %collective-permute-start.5 = (f32[28,8,128]{2,1,0:T(8,128)}, f32[28,8,128]{2,1,0:T(8,128)S(1)}, u32[]{:S(2)}, u32[]{:S(2)}) collective-permute-start(f32[28,8,128]{2,1,0:T(8,128)} %get-tuple-element.33), channel_id=1, source_target_pairs={{0,8},{8,0},{16,24},{24,16},{32,40},{40,32},{48,56},{56,48},{64,72... | collective-permute-start | bytes 344072 | tf_op jit(solution)/shard_map/ppermute | solution.py:541
  63.0 11.8 %copy-start.7 = (f32[28,8,128]{2,1,0:T(8,128)}, f32[28,8,128]{2,1,0:T(8,128)S(1)}, u32[]{:S(2)}) copy-start(f32[28,8,128]{2,1,0:T(8,128)S(1)} %collective-permute-done.5.near_ref) | copy-start | bytes 344068
  74.7 0.7 copy-start.3
  75.4 15.5 %copy-start = (f32[3,3,8,32,128]{4,3,2,1,0:T(8,128)S(1)}, f32[3,3,8,32,128]{4,3,2,1,0:T(8,128)}, u32[]{:S(2)}) copy-start(f32[3,3,8,32,128]{4,3,2,1,0:T(8,128)} %get-tuple-element.34.ee_ref) | copy-start | bytes 3538948
  75.4 15.5 %copy-start.1 = (f32[3,3,8,32,128]{4,3,2,1,0:T(8,128)S(1)}, f32[3,3,8,32,128]{4,3,2,1,0:T(8,128)}, u32[]{:S(2)}) copy-start(f32[3,3,8,32,128]{4,3,2,1,0:T(8,128)} %get-tuple-element.35.h1_ref) | copy-start | bytes 3538948
  75.4 15.5 %copy-start.2 = (f32[3,8,32,128]{3,2,1,0:T(8,128)S(1)}, f32[3,8,32,128]{3,2,1,0:T(8,128)}, u32[]{:S(2)}) copy-start(f32[3,8,32,128]{3,2,1,0:T(8,128)} %get-tuple-element.36.jj_ref) | copy-start | bytes 1179652
  75.4 15.5 %copy-start.5 = (f32[128,256]{1,0:T(8,128)S(1)}, f32[128,256]{1,0:T(8,128)}, u32[]{:S(2)}) copy-start(f32[128,256]{1,0:T(8,128)} %constant.96.clone.wz_ref) | copy-start | bytes 393220
  75.4 15.6 %copy-start.6 = (f32[8,32,128]{2,1,0:T(8,128)S(1)}, f32[8,32,128]{2,1,0:T(8,128)}, u32[]{:S(2)}) copy-start(f32[8,32,128]{2,1,0:T(8,128)} %get-tuple-element.31.mm_ref) | copy-start | bytes 393220
  75.4 15.6 %copy-start.11 = (f32[6,8,128]{2,1,0:T(8,128)S(1)}, f32[6,8,128]{2,1,0:T(8,128)}, u32[]{:S(2)}) copy-start(f32[6,8,128]{2,1,0:T(8,128)} %copy-done.10) | copy-start | bytes 73732
  75.4 15.6 %copy-start.14 = (f32[32,16]{1,0:T(8,128)S(1)}, f32[32,16]{1,0:T(8,128)}, u32[]{:S(2)}) copy-start(f32[32,16]{1,0:T(8,128)} %constant.97.clone.wy_ref) | copy-start | bytes 6148
  75.4 15.6 %copy-start.17 = (s32[23]{0:T(128)S(1)}, s32[23]{0:T(128)}, u32[]{:S(2)}) copy-start(s32[23]{0:T(128)} %copy-done.15) | copy-start | bytes 280
  75.4 15.6 %copy-start.18 = (f32[2]{0:T(128)S(1)}, f32[2]{0:T(128)}, u32[]{:S(2)}) copy-start(f32[2]{0:T(128)} %levels.3) | copy-start | bytes 28
  80.5 28.1 %collective-permute-start.6 = (f32[63,8,128]{2,1,0:T(8,128)}, f32[63,8,128]{2,1,0:T(8,128)S(1)}, u32[]{:S(2)}, u32[]{:S(2)}) collective-permute-start(f32[63,8,128]{2,1,0:T(8,128)} %get-tuple-element.38), channel_id=1, source_target_pairs={{8,16},{16,8},{24,32},{32,24},{40,48},{48,40},{56,64},{64,56},{72,... | collective-permute-start | bytes 774152 | tf_op jit(solution)/shard_map/ppermute | solution.py:569
  89.0 19.6 %collective-permute-start.7 = (f32[63,8,128]{2,1,0:T(8,128)}, f32[63,8,128]{2,1,0:T(8,128)S(1)}, u32[]{:S(2)}, u32[]{:S(2)}) collective-permute-start(f32[63,8,128]{2,1,0:T(8,128)} %get-tuple-element.39), channel_id=1, source_target_pairs={{0,8},{8,0},{16,24},{24,16},{32,40},{40,32},{48,56},{56,48},{64,72... | collective-permute-start | bytes 774152 | tf_op jit(solution)/shard_map/ppermute | solution.py:568
  91.0 0.9 copy-start.4
  91.9 0.9 copy-start.8

commit v3 on v2

--- a/solution.py
+++ b/solution.py
@@ -114,13 +114,14 @@
             spread_ref[i, q] = packed
 
 
-def select_kernel(table, g_ref, message_ref, mine_ref, far_ref):
+def select_kernel(table, g_ref, message_ref, mine_ref, far_ref, sem):
+    copy = pltpu.make_async_copy(message_ref, far_ref.at[pl.ds(COARSE, 3 * FIRST_TILES + 4)], sem)
+    copy.start()
     for at, ref in ((MINE, mine_ref), (THEIRS, far_ref)):
         for i, (which, q) in enumerate(((0, 3), (1, 0), (1, 1), (1, 2), (1, 3), (2, 0))):
             held = g_ref[table[at + which] * 4 + q]
             ref[i] = jnp.where(table[at + 3 + which] == 1, held, 0.0)
-    for i in range(3 * FIRST_TILES + 4):
-        far_ref[COARSE + i] = message_ref[i]
+    copy.wait()
 
 
 def extend_kernel(
@@ -200,13 +201,13 @@
     return [jnp.concatenate([ref[at + 4 * c + i] for i in range(4)], axis=0) for c in range(2)]
 
 
-def first_state(r, table, ee_ref, h1_ref, far_ref, near_ref, step):
+def first_state(r, block, table, ee_ref, h1_ref, far_ref, near_ref, step):
     core = table[CORE]
     far, near = first_message(far_ref, COARSE + r * FIRST_TILES), first_message(near_ref, r * FIRST_TILES)
     trace_h = [jnp.where(table[WIDE] == 0, 0.0, x) for x in select(core == 0, far, near)]
     trace_e = [jnp.where(table[WIDE] == table[WIDE_COUNT] - 1, 0.0, x) for x in select(core == 1, far, near)]
-    e = {p: [ee_ref[0, c, p] for c in range(3)] for p in range(PLANES)}
-    h = {p: [h1_ref[0, c, p] for c in range(3)] for p in range(PLANES)}
+    e = {p: [ee_ref[block, c, p] for c in range(3)] for p in range(PLANES)}
+    h = {p: [h1_ref[block, c, p] for c in range(3)] for p in range(PLANES)}
     top = PLANES - 1
     h[top] = [h[top][0], h[top][1] + step * trace_e[1], h[top][2] - step * trace_e[0]]
     below = jnp.where(table[WIDE] == 0, 0.0, step)
@@ -275,47 +276,52 @@
     table, levels, mine_ref, wz_ref, wy_ref, mm_ref, far_ref, near_ref, ee_ref, h1_ref, jj_ref,
     far_out, near_out, c_ref, d_ref,
 ):
-    r = pl.program_id(0)
-
-    @pl.when(r == 0)
-    def _():
-        refine(table, mine_ref, far_ref, wz_ref, wy_ref, d_ref)
-        for p in (0, 1, 2, 5, 6, 7):
-            plane_coefficients(p, mm_ref[p], table, levels, d_ref, c_ref)
-
+    refine(table, mine_ref, far_ref, wz_ref, wy_ref, d_ref)
+    for p in (0, 1, 2, 5, 6, 7):
+        plane_coefficients(p, mm_ref[p], table, levels, d_ref, c_ref)
     lanes = lane_ids()
     step = step_of_rows(table[NARROW])
     core = table[CORE]
     zero = jnp.zeros((ROWS, LANES), jnp.float32)
-    e, h = first_state(r, table, ee_ref, h1_ref, far_ref, near_ref, step)
-
-    def electric(p):
-        current = [jj_ref[c, p] for c in range(3)]
-        e[p] = next_electric(e[p], h[p], (h[p - 1][1], h[p - 1][2]), c_ref[r, p + 1], current, lanes)
-
-    def magnetic(p):
-        h[p] = next_magnetic(h[p], e[p], (e[p + 1][1], e[p + 1][2]), step, lanes)
-
-    for p in (0, 1, 2, 5, 6, 7):
-        electric(p)
-    h[-1] = [zero] * 3
-    e[8] = [zero] * 3
-    upward, downward = [], [(e[0][1], e[0][2])]
-    for first in (5, 6, 7):
-        for p in range(first, 8):
-            magnetic(p)
-        upward.append((h[7][1], h[7][2]))
-        for p in range(first + 1, 8):
+
+    def per_real(r, carry):
+        e, h = first_state(r, r, table, ee_ref, h1_ref, far_ref, near_ref, step)
+
+        def electric(p):
+            current = [jj_ref[c, p] for c in range(3)]
+            e[p] = next_electric(e[p], h[p], (h[p - 1][1], h[p - 1][2]), c_ref[r, p + 1], current, lanes)
+
+        def magnetic(p):
+            h[p] = next_magnetic(h[p], e[p], (e[p + 1][1], e[p + 1][2]), step, lanes)
+
+        for p in (0, 1, 2, 5, 6, 7):
             electric(p)
-    for last_plane in (1, 0):
-        for p in range(last_plane + 1):
-            magnetic(p)
-        for p in range(last_plane + 1):
-            electric(p)
-        downward.append((e[0][1], e[0][2]))
-    for i, (a, b) in enumerate(zip(as_message(upward), as_message(downward), strict=True)):
-        far_out[r * TILES + i] = jnp.where(core == 1, a, b)
-        near_out[r * TILES + i] = jnp.where(core == 1, b, a)
+        h[-1] = [zero] * 3
+        e[8] = [zero] * 3
+        upward, downward = [], [(e[0][1], e[0][2])]
+        for first in (5, 6, 7):
+            for p in range(first, 8):
+                magnetic(p)
+            upward.append((h[7][1], h[7][2]))
+            for p in range(first + 1, 8):
+                electric(p)
+        for last_plane in (1, 0):
+            for p in range(last_plane + 1):
+                magnetic(p)
+            for p in range(last_plane + 1):
+                electric(p)
+            downward.append((e[0][1], e[0][2]))
+        for i, (a, b) in enumerate(zip(as_message(upward), as_message(downward), strict=True)):
+            far_out[r * TILES + i] = jnp.where(core == 1, a, b)
+            near_out[r * TILES + i] = jnp.where(core == 1, b, a)
+        return carry
+
+    lax.fori_loop(0, 3, per_real, 0)
+
+
+def stage_kernel(*refs):
+    for source, copied in zip(refs[: len(refs) // 2], refs[len(refs) // 2 :], strict=True):
+        copied[...] = source[...]
 
 
 def inner_kernel(
@@ -339,7 +345,7 @@
 
     lanes = lane_ids()
     step = step_of_rows(table[NARROW])
-    e, h = first_state(r, table, ee_ref, h1_ref, far_ref, near_ref, step)
+    e, h = first_state(r, 0, table, ee_ref, h1_ref, far_ref, near_ref, step)
 
     def electric(first, last):
         for p in range(first, last + 1):
@@ -432,6 +438,8 @@
 def run(kernel, scalars, operands, outs, flops, scratch=(), steps=3, limit=60):
     def spec(shape, block):
         rank = len(shape)
+        if block is pl.ANY:
+            return pl.BlockSpec(memory_space=pl.ANY)
         if block is None:
             return pl.BlockSpec(tuple(shape), lambda r: (0,) * rank)
         if block is True:
@@ -512,10 +520,12 @@
     )
     tile_lo = lax.ppermute(tile_last, "narrow", up)
     tile_hi = lax.ppermute(tile_first, "narrow", down)
-    early, first_rows, last_rows = lax.optimization_barrier((table, first_rows, last_rows))
+    tile_lo, first_rows, last_rows = lax.optimization_barrier((tile_lo, first_rows, last_rows))
+    low = lax.ppermute(last_rows, "narrow", up)
+    high = lax.ppermute(first_rows, "narrow", down)
     (spread,) = run(
         tile_kernel,
-        (early,),
+        (table,),
         [(tile, None), (tile_lo, None), (tile_hi, None)],
         [((half, 4, 8, LANES), None)],
         1_000_000,
@@ -524,9 +534,6 @@
     )
     gathered = lax.all_to_all(spread, "wide", 0, 0, axis_index_groups=groups, tiled=True)
     gathered = gathered.reshape(half * 4, 8, LANES)
-
-    low = lax.ppermute(last_rows, "narrow", up)
-    high = lax.ppermute(first_rows, "narrow", down)
 
     extended = (3, 3, PLANES, ROWS, LANES)
     planes = (PLANES, ROWS, LANES)
@@ -536,16 +543,17 @@
         (table,),
         [(electric, True), (magnetic, True), (current, None), (material_mask, None), (low, None), (high, None)],
         [(extended, True), (extended, True), ((3, *planes), None), (planes, None), (message, None), (message, None)],
-        10_000_000,
+        100_000_000_000,
     )
     near = lax.ppermute(near, "wide", near_pairs)
 
     mine, far = run(
         select_kernel,
         (table,),
-        [(gathered, None), (far, None)],
+        [(gathered, None), (far, pl.ANY)],
         [((COARSE, 8, LANES), None), ((COARSE + message[0], 8, LANES), None)],
         1_000_000,
+        [pltpu.SemaphoreType.DMA],
         steps=1,
         limit=8,
     )
@@ -556,15 +564,26 @@
     message = (3 * TILES, 8, LANES)
     coefficients = (3, PLANES + 2, ROWS, LANES)
     strips = pltpu.VMEM((COARSE, ROWS, LANES), jnp.float32)
-    inputs = [(x, None) for x in (mine, weights_z, weights_y, m_ext, far, near)] + fields
+    still = (e_ext, h_one, j_ext, m_ext, weights_z, weights_y)
+    e_on, h_on, j_on, m_on, z_on, y_on = run(
+        stage_kernel,
+        (),
+        [(x, i < 2 or None) for i, x in enumerate(still)],
+        [(x.shape, i < 2 or None) for i, x in enumerate(still)],
+        1_000_000_000,
+        limit=10,
+    )
     far_end, near_end = run(
         trace_kernel,
         (table, material_levels),
-        inputs,
+        [(x, None) for x in (mine, z_on, y_on, m_on, far, near)] + [(e_on, None), (h_on, None), (j_on, None)],
         [(message, None), (message, None)],
         10_000_000,
         [pltpu.VMEM(coefficients, jnp.float32), strips],
-    )
+        steps=1,
+        limit=24,
+    )
+    inputs = [(x, None) for x in (mine, weights_z, weights_y, m_ext, far, near)] + fields
     near_end = lax.ppermute(near_end, "wide", near_pairs)
     far_end = lax.ppermute(far_end, "wide", far_pairs)
 

time: 112 us -> 109 us (0.973)
  the two profiles are of different devices: /device:TPU:102 before, /device:TPU:36 now
where the time goes in v3:
time: 109 us; the launch traced here: 108 us
  starting transfers between devices  55 us (50%)
  waiting for transfers between devices  24.8 us (23%)
  Pallas kernels  18.2 us (17%)
  local copies, waits for them, and re-layouts  7.77 us (7%)
    pallas_call x9, Pallas kernels, run(): pl.pallas_call(kernel, grid=(steps,), in_specs=[pl.BlockSpec(memory_space...  18.2 us
    ppermute x1, starting transfers between devices, body(): far = lax.ppermute(far, 'wide', far_ring)  16.4 us
    ppermute x1, waiting for transfers between devices, body(): far_end = lax.ppermute(far_end, 'wide', far_pairs)  15.7 us
    ppermute x1, starting transfers between devices, body(): far_end = lax.ppermute(far_end, 'wide', far_pairs)  15.5 us
    all_to_all x1, starting transfers between devices, body(): lax.all_to_all(spread, 'wide', 0, 0, axis_index_groups=groups, tiled=True)  7.6 us
    unnamed x40, local copies, waits for them, and re-layouts  7.5 us
    ppermute x1, waiting for transfers between devices, body(): far = lax.ppermute(far, 'wide', far_ring)  4.71 us
    ppermute x1, starting transfers between devices, body(): low = lax.ppermute(last_rows, 'narrow', up)  3.82 us
  transfers between devices with their start and end apart: 9, of which 4 were waited for; matrix products, arithmetic and copies ran while one was open for 1% of the time, Pallas kernels for 11%

profile of v3, /device:TPU:36, one launch (start us, length us, event | category | flops | bytes accessed | tf_op | source)
XLA Modules:
  0.0 107.8 jit_solution(1625364876992731176)
XLA Ops:
  0.6 0.0 copy-start.10
  0.6 0.7 copy-done.10
  1.4 0.1 tile_rows_kernel.1
  1.4 3.8 %collective-permute-start = (f32[4,128]{1,0:T(4,128)S(1)}, f32[4,128]{1,0:T(4,128)S(1)}, u32[]{:S(2)}, u32[]{:S(2)}) collective-permute-start(f32[4,128]{1,0:T(4,128)S(1)} %get-tuple-element.28), channel_id=1, source_target_pairs={{0,1},{1,2},{2,3},{3,4},{4,5},{5,6},{6,7},{8,9},{9,10},{10,11},{11... | collective-permute-start | bytes 6152 | tf_op jit(solution)/shard_map/ppermute | solution.py:521
  5.3 2.0 %collective-permute-start.1 = (f32[4,128]{1,0:T(4,128)S(1)}, f32[4,128]{1,0:T(4,128)S(1)}, u32[]{:S(2)}, u32[]{:S(2)}) collective-permute-start(f32[4,128]{1,0:T(4,128)S(1)} %get-tuple-element.32), channel_id=1, source_target_pairs={{1,0},{2,1},{3,2},{4,3},{5,4},{6,5},{7,6},{9,8},{10,9},{11,10},{12... | collective-permute-start | bytes 6152 | tf_op jit(solution)/shard_map/ppermute | solution.py:522
  7.3 0.1 pad_add_fusion.1
  7.4 0.1 add_clamp_fusion
  7.5 0.9 fusion
  8.3 0.1 copy.13
  8.4 0.0 copy-start.17
  8.4 0.0 copy-start.11
  8.4 2.3 %pack_kernel.1 = (f32[176,4,128]{2,1,0:T(4,128)}, f32[176,4,128]{2,1,0:T(4,128)}) custom-call(f32[72,24,128]{2,1,0:T(8,128)} %bitcast.30, f32[72,24,128]{2,1,0:T(8,128)} %bitcast.31, f32[72,24,128]{2,1,0:T(8,128)} %bitcast.32, f32[72,24,128]{2,1,0:T(8,128)} %bitcast.33, f32[24,24,128]{2,1,0:T(8,128)} %bitcast.34, f32[24,24,128]{2,1,0:T(8,128)} %bitcast.35, ...), custom_call_target="tpu_custom_call" | custom-call | flops 1000000 | bytes 5046272 | tf_op jit(solution)/shard_map/pack_kernel/pallas_call | solution.py:451
  10.8 0.0 collective-permute-done.lo_ref
  10.8 3.8 %collective-permute-start.2 = (f32[176,4,128]{2,1,0:T(4,128)}, f32[176,4,128]{2,1,0:T(4,128)S(1)}, u32[]{:S(2)}, u32[]{:S(2)}) collective-permute-start(f32[176,4,128]{2,1,0:T(4,128)} %get-tuple-element.33), channel_id=1, source_target_pairs={{0,1},{1,2},{2,3},{3,4},{4,5},{5,6},{6,7},{8,9},{9,10},{10,11},{11... | collective-permute-start | bytes 1081352 | tf_op jit(solution)/shard_map/ppermute | solution.py:524
  14.6 2.0 %collective-permute-start.3 = (f32[176,4,128]{2,1,0:T(4,128)}, f32[176,4,128]{2,1,0:T(4,128)S(1)}, u32[]{:S(2)}, u32[]{:S(2)}) collective-permute-start(f32[176,4,128]{2,1,0:T(4,128)} %get-tuple-element.34), channel_id=1, source_target_pairs={{1,0},{2,1},{3,2},{4,3},{5,4},{6,5},{7,6},{9,8},{10,9},{11,10},{12... | collective-permute-start | bytes 1081352 | tf_op jit(solution)/shard_map/ppermute | solution.py:525
  16.7 0.1 reshape.200
  16.8 0.0 copy-done.17
  16.8 0.1 concatenate.3.table
  16.9 0.0 copy-start.12
  16.9 0.0 collective-permute-done.1.hi_ref
  16.9 0.0 copy-done.11
  16.9 1.5 %tile_kernel.1 = f32[32,4,8,128]{3,2,1,0:T(8,128)} custom-call(s32[23]{0:T(128)S(1)} %concatenate.3.table, f32[12,4,64]{2,1,0:T(4,128)S(1)} %bitcast.29, f32[4,128]{1,0:T(4,128)S(1)} %collective-permute-done.lo_ref, f32[4,128]{1,0:T(4,128)S(1)} %collective-permute-done.1.hi_ref), custom_call_target="tpu_custom_call" | custom-call | flops 1000000 | bytes 540672 | tf_op jit(solution)/shard_map/tile_kernel/pallas_call | solution.py:451
  18.4 7.6 %all-to-all-start = ((f32[32,4,8,128]{3,2,1,0:T(8,128)}), f32[32,4,8,128]{3,2,1,0:T(8,128)S(1)}, u32[]{:S(2)}, u32[]{:S(2)}) async-start(f32[32,4,8,128]{3,2,1,0:T(8,128)} %tile_kernel.1), calls=%async_computation | async-start | bytes 1048576 | tf_op jit(solution)/shard_map/all_to_all | solution.py:535
  26.1 0.0 copy-start.6
  26.1 0.0 copy-start.15
  26.1 0.0 collective-permute-done.2.lo_ref
  26.1 0.0 copy-start.18
  26.1 1.5 %collective-permute-done.3.hi_ref = f32[176,4,128]{2,1,0:T(4,128)S(1)} collective-permute-done((f32[176,4,128]{2,1,0:T(4,128)}, f32[176,4,128]{2,1,0:T(4,128)S(1)}, u32[]{:S(2)}, u32[]{:S(2)}) %collective-permute-start.3) | collective-permute-done | bytes 360480 | tf_op jit(solution)/shard_map/ppermute | solution.py:525
  27.6 0.0 copy-done.12
  27.6 0.0 copy-done.18
  27.6 0.0 copy-start.19
  27.6 0.7 copy-done.19
  28.3 4.4 %extend_kernel.1 = (f32[3,3,8,32,128]{4,3,2,1,0:T(8,128)}, f32[3,3,8,32,128]{4,3,2,1,0:T(8,128)}, f32[3,8,32,128]{3,2,1,0:T(8,128)}, f32[8,32,128]{2,1,0:T(8,128...) custom-call(s32[23]{0:T(128)} %copy-done.12, f32[3,3,8,24,128]{4,3,2,1,0:T(8,128)} %e_ref.1, ...), custom_call_target="tpu_custom_call" | custom-call | flops 99999997952 | bytes 5996544 | tf_op jit(solution)/shard_map/extend_kernel/pallas_call | solution.py:451
  32.7 2.9 %all-to-all-done = f32[32,4,8,128]{3,2,1,0:T(8,128)S(1)} async-done(((f32[32,4,8,128]{3,2,1,0:T(8,128)}), f32[32,4,8,128]{3,2,1,0:T(8,128)S(1)}, u32[]{:S(2)}, u32[]{:S(2)}) %all-to-all-start) | async-done | bytes 524320 | tf_op jit(solution)/shard_map/all_to_all | solution.py:535
  35.6 0.9 copy-done.9
  36.5 0.7 copy-done.13
  37.2 0.7 select_kernel.1
  37.9 16.4 %collective-permute-start.4 = (f32[34,8,128]{2,1,0:T(8,128)S(1)}, f32[34,8,128]{2,1,0:T(8,128)S(1)}, u32[]{:S(2)}, u32[]{:S(2)}) collective-permute-start(f32[34,8,128]{2,1,0:T(8,128)S(1)} %get-tuple-element.38), channel_id=1, source_target_pairs={{0,504},{8,16},{16,8},{24,32},{32,24},{40,48},{48,40},{56,64},{64,... | collective-permute-start | bytes 417800 | tf_op jit(solution)/shard_map/ppermute | solution.py:560
  54.2 1.9 %collective-permute-start.5 = (f32[28,8,128]{2,1,0:T(8,128)}, f32[28,8,128]{2,1,0:T(8,128)S(1)}, u32[]{:S(2)}, u32[]{:S(2)}) collective-permute-start(f32[28,8,128]{2,1,0:T(8,128)} %get-tuple-element.39), channel_id=1, source_target_pairs={{0,8},{8,0},{16,24},{24,16},{32,40},{40,32},{48,56},{56,48},{64,72... | collective-permute-start | bytes 344072 | tf_op jit(solution)/shard_map/ppermute | solution.py:548
  56.2 0.0 copy-done.6
  56.2 0.0 copy-done.15
  56.2 0.0 copy-start
  56.2 1.0 copy-done
  57.2 1.3 %copy-done.2 = f32[3,3,8,32,128]{4,3,2,1,0:T(8,128)S(1)} copy-done((f32[3,3,8,32,128]{4,3,2,1,0:T(8,128)S(1)}, f32[3,3,8,32,128]{4,3,2,1,0:T(8,128)}, u32[]{:S(2)}) %copy-start.2) | copy-done | bytes 1179672
  58.5 1.3 %copy-done.4 = f32[3,3,8,32,128]{4,3,2,1,0:T(8,128)S(1)} copy-done((f32[3,3,8,32,128]{4,3,2,1,0:T(8,128)S(1)}, f32[3,3,8,32,128]{4,3,2,1,0:T(8,128)}, u32[]{:S(2)}) %copy-start.4) | copy-done | bytes 1179672
  59.7 0.9 copy-done.7
  60.6 0.3 stage_kernel.1
  61.0 0.0 collective-permute-done.5.near_ref
  61.0 4.7 %collective-permute-done.4.far_ref = f32[34,8,128]{2,1,0:T(8,128)S(1)} collective-permute-done((f32[34,8,128]{2,1,0:T(8,128)S(1)}, f32[34,8,128]{2,1,0:T(8,128)S(1)}, u32[]{:S(2)}, u32[]{:S(2)}) %collective-permute-start.4) | collective-permute-done | bytes 139296 | tf_op jit(solution)/shard_map/ppermute | solution.py:560
  65.7 0.0 copy-done.14
  65.7 0.0 copy-done.16
  65.7 0.0 copy-start.5
  65.7 0.0 copy-start.8
  65.7 2.6 %trace_kernel.1 = (f32[63,8,128]{2,1,0:T(8,128)S(1)}, f32[63,8,128]{2,1,0:T(8,128)S(1)}) custom-call(s32[23]{0:T(128)S(1)} %copy-done.14, f32[2]{0:T(128)S(1)} %copy-done.16, f32[6,8,128]{2,1,0:T(8,128)S(1)} %get-tuple-element.36.mine_ref, f32[128,256]{1,0:T(8,128)S(1)} %get-tuple-element.44.wz_ref, f32[32,16]{1,0:T(8,128)S(1)} %get-tuple-element.45.wy_ref, ...), custom_call_target="tpu_custom_call" | custom-call | flops 10000000 | bytes 3811328 | tf_op jit(solution)/shard_map/trace_kernel/pallas_call | solution.py:451
  68.3 15.5 %collective-permute-start.6 = (f32[63,8,128]{2,1,0:T(8,128)S(1)}, f32[63,8,128]{2,1,0:T(8,128)S(1)}, u32[]{:S(2)}, u32[]{:S(2)}) collective-permute-start(f32[63,8,128]{2,1,0:T(8,128)S(1)} %get-tuple-element.50), channel_id=1, source_target_pairs={{8,16},{16,8},{24,32},{32,24},{40,48},{48,40},{56,64},{64,56},{72,... | collective-permute-start | bytes 774152 | tf_op jit(solution)/shard_map/ppermute | solution.py:588
  83.8 1.9 %collective-permute-start.7 = (f32[63,8,128]{2,1,0:T(8,128)S(1)}, f32[63,8,128]{2,1,0:T(8,128)S(1)}, u32[]{:S(2)}, u32[]{:S(2)}) collective-permute-start(f32[63,8,128]{2,1,0:T(8,128)S(1)} %get-tuple-element.51), channel_id=1, source_target_pairs={{0,8},{8,0},{16,24},{24,16},{32,40},{40,32},{48,56},{56,48},{64,72... | collective-permute-start | bytes 774152 | tf_op jit(solution)/shard_map/ppermute | solution.py:587
  85.7 0.0 copy-done.1
  85.7 0.0 copy-done.3
  85.8 0.0 copy-done.5
  85.8 0.0 copy-done.8
  85.8 3.2 %inner_kernel.1 = (f32[3,3,8,32,128]{4,3,2,1,0:T(8,128)S(1)}, f32[3,3,8,32,128]{4,3,2,1,0:T(8,128)S(1)}, f32[3,10,32,128]{3,2,1,0:T(8,128)S(1)}) custom-call(s32[23]{0:T(128)S(1)} %copy-done.14, f32[2]{0:T(128)S(1)} %copy-done.16, f32[6,8,128]{2,1,0:T(8,128)S(1)} %get-tuple-element.36.mine_ref, f32[128,256]{1,0:T(8,128)S(1)} %copy-done.6, ...), custom_call_target="tpu_custom_call" | custom-call | flops 10000000 | bytes 6146048 | tf_op jit(solution)/shard_map/inner_kernel/pallas_call | solution.py:451
  89.0 15.7 %collective-permute-done.6.far_ref = f32[63,8,128]{2,1,0:T(8,128)S(1)} collective-permute-done((f32[63,8,128]{2,1,0:T(8,128)S(1)}, f32[63,8,128]{2,1,0:T(8,128)S(1)}, u32[]{:S(2)}, u32[]{:S(2)}) %collective-permute-start.6) | collective-permute-done | bytes 258080 | tf_op jit(solution)/shard_map/ppermute | solution.py:588
  104.7 0.0 collective-permute-done.7.near_ref
  104.7 3.1 %window_kernel.1 = (f32[3,3,8,24,128]{4,3,2,1,0:T(8,128)}, f32[3,3,8,24,128]{4,3,2,1,0:T(8,128)}) custom-call(s32[23]{0:T(128)S(1)} %copy-done.14, f32[3,10,32,128]{3,2,1,0:T(8,128)S(1)} %get-tuple-element.43.c_ref, f32[63,8,128]{2,1,0:T(8,128)S(1)} %collective-permute-done.6.far_ref, f32[63,8,128]{2,1,0:T(8,128)S(1)} %collective-permute-done.7.near_ref, ...), custom_call_target="tpu_custom_call" | custom-call | flops 10000000 | bytes 5529600 | tf_op jit(solution)/shard_map/window_kernel/pallas_call | solution.py:451
  (14 shorter events, 0.1 us)
Async XLA Ops:
  0.6 0.7 copy-start.10
  1.4 9.3 %collective-permute-start = (f32[4,128]{1,0:T(4,128)S(1)}, f32[4,128]{1,0:T(4,128)S(1)}, u32[]{:S(2)}, u32[]{:S(2)}) collective-permute-start(f32[4,128]{1,0:T(4,128)S(1)} %get-tuple-element.28), channel_id=1, source_target_pairs={{0,1},{1,2},{2,3},{3,4},{4,5},{5,6},{6,7},{8,9},{9,10},{10,11},{11... | collective-permute-start | bytes 6152 | tf_op jit(solution)/shard_map/ppermute | solution.py:521
  5.3 11.6 %collective-permute-start.1 = (f32[4,128]{1,0:T(4,128)S(1)}, f32[4,128]{1,0:T(4,128)S(1)}, u32[]{:S(2)}, u32[]{:S(2)}) collective-permute-start(f32[4,128]{1,0:T(4,128)S(1)} %get-tuple-element.32), channel_id=1, source_target_pairs={{1,0},{2,1},{3,2},{4,3},{5,4},{6,5},{7,6},{9,8},{10,9},{11,10},{12... | collective-permute-start | bytes 6152 | tf_op jit(solution)/shard_map/ppermute | solution.py:522
  8.4 8.4 %copy-start.17 = (s32[6]{0:T(128)S(1)}, s32[6]{0:T(128)}, u32[]{:S(2)}) copy-start(s32[6]{0:T(128)} %param.15) | copy-start | bytes 76
  8.4 8.5 %copy-start.11 = (f32[4,12,64]{2,0,1:T(4,128)S(1)}, f32[4,12,64]{2,0,1:T(4,128)}, u32[]{:S(2)}) copy-start(f32[4,12,64]{2,0,1:T(4,128)} %param.13) | copy-start | bytes 36868
  10.8 15.3 %collective-permute-start.2 = (f32[176,4,128]{2,1,0:T(4,128)}, f32[176,4,128]{2,1,0:T(4,128)S(1)}, u32[]{:S(2)}, u32[]{:S(2)}) collective-permute-start(f32[176,4,128]{2,1,0:T(4,128)} %get-tuple-element.33), channel_id=1, source_target_pairs={{0,1},{1,2},{2,3},{3,4},{4,5},{5,6},{6,7},{8,9},{9,10},{10,11},{11... | collective-permute-start | bytes 1081352 | tf_op jit(solution)/shard_map/ppermute | solution.py:524
  14.6 13.0 %collective-permute-start.3 = (f32[176,4,128]{2,1,0:T(4,128)}, f32[176,4,128]{2,1,0:T(4,128)S(1)}, u32[]{:S(2)}, u32[]{:S(2)}) collective-permute-start(f32[176,4,128]{2,1,0:T(4,128)} %get-tuple-element.34), channel_id=1, source_target_pairs={{1,0},{2,1},{3,2},{4,3},{5,4},{6,5},{7,6},{9,8},{10,9},{11,10},{12... | collective-permute-start | bytes 1081352 | tf_op jit(solution)/shard_map/ppermute | solution.py:525
  16.9 10.7 %copy-start.12 = (s32[23]{0:T(128)}, s32[23]{0:T(128)S(1)}, u32[]{:S(2)}) copy-start(s32[23]{0:T(128)S(1)} %concatenate.3.table) | copy-start | bytes 280
  18.4 17.2 %all-to-all-start = ((f32[32,4,8,128]{3,2,1,0:T(8,128)}), f32[32,4,8,128]{3,2,1,0:T(8,128)S(1)}, u32[]{:S(2)}, u32[]{:S(2)}) async-start(f32[32,4,8,128]{3,2,1,0:T(8,128)} %tile_kernel.1), calls=%async_computation | async-start | bytes 1048576 | tf_op jit(solution)/shard_map/all_to_all | solution.py:535
  26.1 30.1 %copy-start.6 = (f32[128,256]{1,0:T(8,128)S(1)}, f32[128,256]{1,0:T(8,128)}, u32[]{:S(2)}) copy-start(f32[128,256]{1,0:T(8,128)} %constant.96.clone.wz_ref.refs_4_) | copy-start | bytes 393220
  26.1 30.1 %copy-start.15 = (f32[32,16]{1,0:T(8,128)S(1)}, f32[32,16]{1,0:T(8,128)}, u32[]{:S(2)}) copy-start(f32[32,16]{1,0:T(8,128)} %constant.97.clone.wy_ref.refs_5_) | copy-start | bytes 6148
  26.1 1.5 %copy-start.18 = (f32[176,4,128]{2,1,0:T(4,128)}, f32[176,4,128]{2,1,0:T(4,128)S(1)}, u32[]{:S(2)}) copy-start(f32[176,4,128]{2,1,0:T(4,128)S(1)} %collective-permute-done.2.lo_ref) | copy-start | bytes 1081348
  27.6 0.7 copy-start.19
  35.6 0.9 copy-start.9
  36.5 0.7 copy-start.13
  37.9 27.8 %collective-permute-start.4 = (f32[34,8,128]{2,1,0:T(8,128)S(1)}, f32[34,8,128]{2,1,0:T(8,128)S(1)}, u32[]{:S(2)}, u32[]{:S(2)}) collective-permute-start(f32[34,8,128]{2,1,0:T(8,128)S(1)} %get-tuple-element.38), channel_id=1, source_target_pairs={{0,504},{8,16},{16,8},{24,32},{32,24},{40,48},{48,40},{56,64},{64,... | collective-permute-start | bytes 417800 | tf_op jit(solution)/shard_map/ppermute | solution.py:560
  54.2 6.7 %collective-permute-start.5 = (f32[28,8,128]{2,1,0:T(8,128)}, f32[28,8,128]{2,1,0:T(8,128)S(1)}, u32[]{:S(2)}, u32[]{:S(2)}) collective-permute-start(f32[28,8,128]{2,1,0:T(8,128)} %get-tuple-element.39), channel_id=1, source_target_pairs={{0,8},{8,0},{16,24},{24,16},{32,40},{40,32},{48,56},{56,48},{64,72... | collective-permute-start | bytes 344072 | tf_op jit(solution)/shard_map/ppermute | solution.py:548
  56.2 1.0 copy-start
  57.2 1.3 %copy-start.2 = (f32[3,3,8,32,128]{4,3,2,1,0:T(8,128)S(1)}, f32[3,3,8,32,128]{4,3,2,1,0:T(8,128)}, u32[]{:S(2)}) copy-start(f32[3,3,8,32,128]{4,3,2,1,0:T(8,128)} %get-tuple-element.40.ee_ref.refs_0_) | copy-start | bytes 3538948
  58.5 1.3 %copy-start.4 = (f32[3,3,8,32,128]{4,3,2,1,0:T(8,128)S(1)}, f32[3,3,8,32,128]{4,3,2,1,0:T(8,128)}, u32[]{:S(2)}) copy-start(f32[3,3,8,32,128]{4,3,2,1,0:T(8,128)} %get-tuple-element.41.h1_ref.refs_1_) | copy-start | bytes 3538948
  59.7 0.9 copy-start.7
  60.6 5.0 %copy-start.14 = (s32[23]{0:T(128)S(1)}, s32[23]{0:T(128)}, u32[]{:S(2)}) copy-start(s32[23]{0:T(128)} %copy-done.12) | copy-start | bytes 280
  60.6 5.0 %copy-start.16 = (f32[2]{0:T(128)S(1)}, f32[2]{0:T(128)}, u32[]{:S(2)}) copy-start(f32[2]{0:T(128)} %levels.3) | copy-start | bytes 28
  65.7 20.0 %copy-start.1 = (f32[3,8,32,128]{3,2,1,0:T(8,128)S(1)}, f32[3,8,32,128]{3,2,1,0:T(8,128)}, u32[]{:S(2)}) copy-start(f32[3,8,32,128]{3,2,1,0:T(8,128)} %get-tuple-element.42.jj_ref.refs_2_) | copy-start | bytes 1179652
  65.7 20.0 %copy-start.3 = (f32[3,3,8,32,128]{4,3,2,1,0:T(8,128)S(1)}, f32[3,3,8,32,128]{4,3,2,1,0:T(8,128)}, u32[]{:S(2)}) copy-start(f32[3,3,8,32,128]{4,3,2,1,0:T(8,128)} %get-tuple-element.40.ee_ref.refs_0_) | copy-start | bytes 3538948
  65.7 20.1 %copy-start.5 = (f32[3,3,8,32,128]{4,3,2,1,0:T(8,128)S(1)}, f32[3,3,8,32,128]{4,3,2,1,0:T(8,128)}, u32[]{:S(2)}) copy-start(f32[3,3,8,32,128]{4,3,2,1,0:T(8,128)} %get-tuple-element.41.h1_ref.refs_1_) | copy-start | bytes 3538948
  65.7 20.1 %copy-start.8 = (f32[8,32,128]{2,1,0:T(8,128)S(1)}, f32[8,32,128]{2,1,0:T(8,128)}, u32[]{:S(2)}) copy-start(f32[8,32,128]{2,1,0:T(8,128)} %get-tuple-element.37.mm_ref.refs_3_) | copy-start | bytes 393220
  68.3 36.4 %collective-permute-start.6 = (f32[63,8,128]{2,1,0:T(8,128)S(1)}, f32[63,8,128]{2,1,0:T(8,128)S(1)}, u32[]{:S(2)}, u32[]{:S(2)}) collective-permute-start(f32[63,8,128]{2,1,0:T(8,128)S(1)} %get-tuple-element.50), channel_id=1, source_target_pairs={{8,16},{16,8},{24,32},{32,24},{40,48},{48,40},{56,64},{64,56},{72,... | collective-permute-start | bytes 774152 | tf_op jit(solution)/shard_map/ppermute | solution.py:588
  83.8 20.9 %collective-permute-start.7 = (f32[63,8,128]{2,1,0:T(8,128)S(1)}, f32[63,8,128]{2,1,0:T(8,128)S(1)}, u32[]{:S(2)}, u32[]{:S(2)}) collective-permute-start(f32[63,8,128]{2,1,0:T(8,128)S(1)} %get-tuple-element.51), channel_id=1, source_target_pairs={{0,8},{8,0},{16,24},{24,16},{32,40},{40,32},{48,56},{56,48},{64,72... | collective-permute-start | bytes 774152 | tf_op jit(solution)/shard_map/ppermute | solution.py:587

commit v4 on v3

--- a/solution.py
+++ b/solution.py
@@ -84,12 +84,12 @@
     return [jnp.where(condition, a, b) for a, b in zip(yes, no, strict=True)]
 
 
-def tile_rows_kernel(tile_ref, first_ref, last_ref):
-    first_ref[...] = jnp.concatenate([tile_ref[0], tile_ref[1]], axis=1)
-    last_ref[...] = jnp.concatenate([tile_ref[10], tile_ref[11]], axis=1)
-
-
-def pack_kernel(e_first, e_last, h_first, h_last, j_first, j_last, m_first, m_last, first_ref, last_ref):
+def pack_kernel(
+    e_first, e_last, h_first, h_last, j_first, j_last, m_first, m_last, tile_ref,
+    first_ref, last_ref, tile_first, tile_last,
+):
+    tile_first[...] = jnp.concatenate([tile_ref[0], tile_ref[1]], axis=1)
+    tile_last[...] = jnp.concatenate([tile_ref[10], tile_ref[11]], axis=1)
     for at, count, first, last in (
         (E_AT, 72, e_first, e_last),
         (H_AT, 72, h_first, h_last),
@@ -369,54 +369,68 @@
             ho_ref[0, c, p] = h[p][c]
 
 
-def window_kernel(table, c_ref, far_ref, near_ref, ee_ref, hh_ref, jj_ref, eo_ref, ho_ref):
-    r = pl.program_id(0)
+def window_kernel(table, c_ref, far_ref, near_ref, ee_ref, hh_ref, jj_ref, eo_hbm, ho_hbm, eo_ref, ho_ref, sems):
     lanes = lane_ids()
     core = table[CORE]
     step = step_of_rows(table[NARROW])
     below = jnp.where(table[WIDE] == 0, 0.0, step)
     zero = jnp.zeros((ROWS, LANES), jnp.float32)
 
-    def tile_from_below(i):
-        return jnp.where(core == 0, far_ref[r * TILES + i], near_ref[r * TILES + i])
-
-    def tile_from_above(i):
-        return jnp.where(core == 1, far_ref[r * TILES + i], near_ref[r * TILES + i])
-
-    trace_h = from_message(tile_from_below)
-    trace_e = from_message(tile_from_above)
-    e = {p: [zero] * 3 for p in (-2, -1, 8, 9)}
-    h = {p: [zero] * 3 for p in (-2, -1, 8)}
-    for p in range(PLANES):
-        e[p] = [ee_ref[0, c, p] for c in range(3)]
-        h[p] = [hh_ref[0, c, p] for c in range(3)]
-
-    def magnetic(planes, n):
-        for p in planes:
-            up = [e[p + 1][1], e[p + 1][2]]
-            if p == 7:
-                up = [up[0] + trace_e[n - 2][0], up[1] + trace_e[n - 2][1]]
-            h[p] = next_magnetic(h[p], e[p], up, below if p < 0 else step, lanes)
-
-    def electric(planes, n):
-        for p in planes:
-            down = [h[p - 1][1], h[p - 1][2]]
-            if p == 0:
-                down = [down[0] + trace_h[n - 2][0], down[1] + trace_h[n - 2][1]]
-            current = [jj_ref[c, p] for c in range(3)] if 0 <= p < PLANES else None
-            e[p] = next_electric(e[p], h[p], down, c_ref[0, p + 1], current, lanes)
-
-    magnetic((-1, 7), 2)
-    electric((0, 7, 8), 2)
-    e[-1] = next_electric(e[-1], h[-1], (zero, zero), c_ref[0, 0], None, lanes)
-    magnetic((-2, -1, 0, 6, 7, 8), 3)
-    electric((-1, 0, 1, 6, 7, 8), 3)
-    magnetic((-1, 0, 1, 5, 6, 7), 4)
-    electric((0, 1, 2, 5, 6, 7), 4)
-    for p in range(PLANES):
-        for c in range(3):
-            eo_ref[0, c, p] = e[p][c][:OWN]
-            ho_ref[0, c, p] = h[p][c][:OWN]
+    def written(r):
+        return [
+            pltpu.make_async_copy(eo_ref.at[r], eo_hbm.at[r], sems.at[0, r]),
+            pltpu.make_async_copy(ho_ref.at[r], ho_hbm.at[r], sems.at[1, r]),
+        ]
+
+    def per_real(r, carry):
+        def tile_from_below(i):
+            return jnp.where(core == 0, far_ref[r * TILES + i], near_ref[r * TILES + i])
+
+        def tile_from_above(i):
+            return jnp.where(core == 1, far_ref[r * TILES + i], near_ref[r * TILES + i])
+
+        trace_h = from_message(tile_from_below)
+        trace_e = from_message(tile_from_above)
+        e = {p: [zero] * 3 for p in (-2, -1, 8, 9)}
+        h = {p: [zero] * 3 for p in (-2, -1, 8)}
+        for p in range(PLANES):
+            e[p] = [ee_ref[r, c, p] for c in range(3)]
+            h[p] = [hh_ref[r, c, p] for c in range(3)]
+
+        def magnetic(planes, n):
+            for p in planes:
+                up = [e[p + 1][1], e[p + 1][2]]
+                if p == 7:
+                    up = [up[0] + trace_e[n - 2][0], up[1] + trace_e[n - 2][1]]
+                h[p] = next_magnetic(h[p], e[p], up, below if p < 0 else step, lanes)
+
+        def electric(planes, n):
+            for p in planes:
+                down = [h[p - 1][1], h[p - 1][2]]
+                if p == 0:
+                    down = [down[0] + trace_h[n - 2][0], down[1] + trace_h[n - 2][1]]
+                current = [jj_ref[c, p] for c in range(3)] if 0 <= p < PLANES else None
+                e[p] = next_electric(e[p], h[p], down, c_ref[r, p + 1], current, lanes)
+
+        magnetic((-1, 7), 2)
+        electric((0, 7, 8), 2)
+        e[-1] = next_electric(e[-1], h[-1], (zero, zero), c_ref[r, 0], None, lanes)
+        magnetic((-2, -1, 0, 6, 7, 8), 3)
+        electric((-1, 0, 1, 6, 7, 8), 3)
+        magnetic((-1, 0, 1, 5, 6, 7), 4)
+        electric((0, 1, 2, 5, 6, 7), 4)
+        for p in range(PLANES):
+            for c in range(3):
+                eo_ref[r, c, p] = e[p][c][:OWN]
+                ho_ref[r, c, p] = h[p][c][:OWN]
+        for copy in written(r):
+            copy.start()
+        return carry
+
+    lax.fori_loop(0, 3, per_real, 0)
+    for r in range(3):
+        for copy in written(r):
+            copy.wait()
 
 
 def refine_weights():
@@ -465,6 +479,21 @@
     )(*scalars, *[x for x, _ in operands])
 
 
+def run_in_place(kernel, scalars, operands, outs, scratch, out_space, limit):
+    return pl.pallas_call(
+        kernel,
+        in_specs=[pl.BlockSpec(memory_space=pltpu.SMEM)] * len(scalars)
+        + [pl.BlockSpec(memory_space=pltpu.VMEM)] * len(operands),
+        out_specs=[pl.BlockSpec(memory_space=out_space)] * len(outs),
+        out_shape=[jax.ShapeDtypeStruct(shape, jnp.float32) for shape in outs],
+        scratch_shapes=list(scratch),
+        compiler_params=pltpu.CompilerParams(vmem_limit_bytes=limit * 1024 * 1024),
+        cost_estimate=pl.CostEstimate(flops=10_000_000, bytes_accessed=10_000_000, transcendentals=0),
+        interpret=INTERPRET,
+        name=kernel.__name__,
+    )(*scalars, *operands)
+
+
 def body(
     electric,
     magnetic,
@@ -513,10 +542,14 @@
     ]
     ends = [(x, ((x.shape[0], 8, LANES), (0, row, 0))) for x in stack for row in (0, 2)]
     halo = (HALO_PLANES, HALO, LANES)
-    first_rows, last_rows = run(pack_kernel, (), ends, [(halo, None), (halo, None)], 1_000_000, steps=1)
     tile = jnp.transpose(density_tiles, (1, 0, 2))
-    tile_first, tile_last = run(
-        tile_rows_kernel, (), [(tile, None)], [((4, LANES), None), ((4, LANES), None)], 1000, steps=1, limit=8
+    first_rows, last_rows, tile_first, tile_last = run(
+        pack_kernel,
+        (),
+        ends + [(tile, None)],
+        [(halo, None), (halo, None), ((4, LANES), None), ((4, LANES), None)],
+        1_000_000,
+        steps=1,
     )
     tile_lo = lax.ppermute(tile_last, "narrow", up)
     tile_hi = lax.ppermute(tile_first, "narrow", down)
@@ -573,15 +606,14 @@
         1_000_000_000,
         limit=10,
     )
-    far_end, near_end = run(
+    far_end, near_end = run_in_place(
         trace_kernel,
         (table, material_levels),
-        [(x, None) for x in (mine, z_on, y_on, m_on, far, near)] + [(e_on, None), (h_on, None), (j_on, None)],
-        [(message, None), (message, None)],
-        10_000_000,
+        (mine, z_on, y_on, m_on, far, near, e_on, h_on, j_on),
+        [message, message],
         [pltpu.VMEM(coefficients, jnp.float32), strips],
-        steps=1,
-        limit=24,
+        pltpu.VMEM,
+        16,
     )
     inputs = [(x, None) for x in (mine, weights_z, weights_y, m_ext, far, near)] + fields
     near_end = lax.ppermute(near_end, "wide", near_pairs)
@@ -598,13 +630,14 @@
     )
     own = (3, 3, PLANES, OWN, LANES)
     return tuple(
-        run(
+        run_in_place(
             window_kernel,
             (table,),
-            [(coefficient, True), (far_end, None), (near_end, None), (e_in, True), (h_in, True), (j_ext, None)],
-            [(own, True), (own, True)],
-            10_000_000,
-            limit=24,
+            (coefficient, far_end, near_end, e_in, h_in, j_ext),
+            [own, own],
+            [pltpu.VMEM(own, jnp.float32), pltpu.VMEM(own, jnp.float32), pltpu.SemaphoreType.DMA((2, 3))],
+            pltpu.HBM,
+            16,
         )
     )
 

time: 109 us -> 107 us (0.982)
    pallas_call x9 -> x6, Pallas kernels: 18.2 us -> 12.4 us  [run(): pl.pallas_call(kernel, grid=(steps,), in_specs=[pl.BlockSpec(memory_space...]
    pallas_call x0 -> x2, Pallas kernels: none -> 5.56 us  [run_in_place(): pl.pallas_call(kernel, in_specs=[pl.BlockSpec(memory_space=pltpu.SMEM)] *...]
  transfers between devices with their start and end apart: 9 -> 9, of which waited for: 4 -> 4; matrix products, arithmetic and copies ran while one was open for 1% -> 1% of each run, Pallas kernels for 11% -> 9%
where the time goes in v4:
time: 107 us; the launch traced here: 106 us
  starting transfers between devices  55 us (51%)
  waiting for transfers between devices  24.8 us (23%)
  Pallas kernels  18 us (17%)
  local copies, waits for them, and re-layouts  6.99 us (7%)
    ppermute x1, starting transfers between devices, body(): far = lax.ppermute(far, 'wide', far_ring)  16.4 us
    ppermute x1, waiting for transfers between devices, body(): far_end = lax.ppermute(far_end, 'wide', far_pairs)  15.7 us
    ppermute x1, starting transfers between devices, body(): far_end = lax.ppermute(far_end, 'wide', far_pairs)  15.5 us
    pallas_call x6, Pallas kernels, run(): pl.pallas_call(kernel, grid=(steps,), in_specs=[pl.BlockSpec(memory_space...  12.4 us
    all_to_all x1, starting transfers between devices, body(): lax.all_to_all(spread, 'wide', 0, 0, axis_index_groups=groups, tiled=True)  7.6 us
    unnamed x40, local copies, waits for them, and re-layouts  6.72 us
    pallas_call x2, Pallas kernels, run_in_place(): pl.pallas_call(kernel, in_specs=[pl.BlockSpec(memory_space=pltpu.SMEM)] *...  5.56 us
    ppermute x1, waiting for transfers between devices, body(): far = lax.ppermute(far, 'wide', far_ring)  4.71 us
  transfers between devices with their start and end apart: 9, of which 4 were waited for; matrix products, arithmetic and copies ran while one was open for 1% of the time, Pallas kernels for 9%

profile of v4, /device:TPU:36, one launch (start us, length us, event | category | flops | bytes accessed | tf_op | source)
XLA Modules:
  0.0 106.2 jit_solution(5792941968826052428)
XLA Ops:
  0.6 0.0 copy-start.16
  0.6 0.0 copy-start.17
  0.7 0.0 copy-start.10
  0.7 2.3 %pack_kernel.1 = (f32[176,4,128]{2,1,0:T(4,128)}, f32[176,4,128]{2,1,0:T(4,128)}, f32[4,128]{1,0:T(4,128)}, f32[4,128]{1,0:T(4,128)}) custom-call(f32[72,24,128]{2,1,0:T(8,128)} %bitcast.30, f32[72,24,128]{2,1,0:T(8,128)} %bitcast.31, f32[72,24,128]{2,1,0:T(8,128)} %bitcast.32, f32[72,24,128]{2,1,0:T(8,128)} %bitcast.33, f32[24,24,128]{2,1,0:T(8,128)} %bitcast.34, ...), custom_call_target="tpu_custom_call" | custom-call | flops 1000000 | bytes 5062656 | tf_op jit(solution)/shard_map/pack_kernel/pallas_call | solution.py:465
  2.9 3.8 %collective-permute-start = (f32[4,128]{1,0:T(4,128)}, f32[4,128]{1,0:T(4,128)S(1)}, u32[]{:S(2)}, u32[]{:S(2)}) collective-permute-start(f32[4,128]{1,0:T(4,128)} %get-tuple-element.28), channel_id=1, source_target_pairs={{0,1},{1,2},{2,3},{3,4},{4,5},{5,6},{6,7},{8,9},{9,10},{10,11},{11... | collective-permute-start | bytes 6152 | tf_op jit(solution)/shard_map/ppermute | solution.py:554
  6.7 2.0 %collective-permute-start.1 = (f32[4,128]{1,0:T(4,128)}, f32[4,128]{1,0:T(4,128)S(1)}, u32[]{:S(2)}, u32[]{:S(2)}) collective-permute-start(f32[4,128]{1,0:T(4,128)} %get-tuple-element.32), channel_id=1, source_target_pairs={{1,0},{2,1},{3,2},{4,3},{5,4},{6,5},{7,6},{9,8},{10,9},{11,10},{12... | collective-permute-start | bytes 6152 | tf_op jit(solution)/shard_map/ppermute | solution.py:555
  8.8 0.1 pad_add_fusion.1
  8.9 0.1 add_clamp_fusion
  9.0 0.0 copy-done.16
  9.0 0.2 fusion
  9.2 0.1 copy.13
  9.3 0.0 collective-permute-done.lo_ref
  9.3 3.8 %collective-permute-start.2 = (f32[176,4,128]{2,1,0:T(4,128)}, f32[176,4,128]{2,1,0:T(4,128)S(1)}, u32[]{:S(2)}, u32[]{:S(2)}) collective-permute-start(f32[176,4,128]{2,1,0:T(4,128)} %get-tuple-element.33), channel_id=1, source_target_pairs={{0,1},{1,2},{2,3},{3,4},{4,5},{5,6},{6,7},{8,9},{9,10},{10,11},{11... | collective-permute-start | bytes 1081352 | tf_op jit(solution)/shard_map/ppermute | solution.py:557
  13.1 2.0 %collective-permute-start.3 = (f32[176,4,128]{2,1,0:T(4,128)}, f32[176,4,128]{2,1,0:T(4,128)S(1)}, u32[]{:S(2)}, u32[]{:S(2)}) collective-permute-start(f32[176,4,128]{2,1,0:T(4,128)} %get-tuple-element.34), channel_id=1, source_target_pairs={{1,0},{2,1},{3,2},{4,3},{5,4},{6,5},{7,6},{9,8},{10,9},{11,10},{12... | collective-permute-start | bytes 1081352 | tf_op jit(solution)/shard_map/ppermute | solution.py:558
  15.2 0.1 reshape.200
  15.3 0.0 copy-done.17
  15.3 0.1 concatenate.3.table
  15.4 0.0 copy-start.11
  15.4 0.0 collective-permute-done.1.hi_ref
  15.4 0.0 copy-done.10
  15.4 1.5 %tile_kernel.1 = f32[32,4,8,128]{3,2,1,0:T(8,128)} custom-call(s32[23]{0:T(128)S(1)} %concatenate.3.table, f32[12,4,64]{2,1,0:T(4,128)S(1)} %bitcast.29, f32[4,128]{1,0:T(4,128)S(1)} %collective-permute-done.lo_ref, f32[4,128]{1,0:T(4,128)S(1)} %collective-permute-done.1.hi_ref), custom_call_target="tpu_custom_call" | custom-call | flops 1000000 | bytes 540672 | tf_op jit(solution)/shard_map/tile_kernel/pallas_call | solution.py:465
  17.0 7.6 %all-to-all-start = ((f32[32,4,8,128]{3,2,1,0:T(8,128)}), f32[32,4,8,128]{3,2,1,0:T(8,128)S(1)}, u32[]{:S(2)}, u32[]{:S(2)}) async-start(f32[32,4,8,128]{3,2,1,0:T(8,128)} %tile_kernel.1), calls=%async_computation | async-start | bytes 1048576 | tf_op jit(solution)/shard_map/all_to_all | solution.py:568
  24.6 0.0 copy-start.6
  24.6 0.0 copy-start.14
  24.6 0.0 collective-permute-done.2.lo_ref
  24.6 0.0 copy-start.18
  24.6 1.5 %collective-permute-done.3.hi_ref = f32[176,4,128]{2,1,0:T(4,128)S(1)} collective-permute-done((f32[176,4,128]{2,1,0:T(4,128)}, f32[176,4,128]{2,1,0:T(4,128)S(1)}, u32[]{:S(2)}, u32[]{:S(2)}) %collective-permute-start.3) | collective-permute-done | bytes 360480 | tf_op jit(solution)/shard_map/ppermute | solution.py:558
  26.1 0.0 copy-done.11
  26.1 0.0 copy-done.18
  26.1 0.0 copy-start.19
  26.1 0.7 copy-done.19
  26.8 4.4 %extend_kernel.1 = (f32[3,3,8,32,128]{4,3,2,1,0:T(8,128)}, f32[3,3,8,32,128]{4,3,2,1,0:T(8,128)}, f32[3,8,32,128]{3,2,1,0:T(8,128)}, f32[8,32,128]{2,1,0:T(8,128...) custom-call(s32[23]{0:T(128)} %copy-done.11, f32[3,3,8,24,128]{4,3,2,1,0:T(8,128)} %e_ref.1, ...), custom_call_target="tpu_custom_call" | custom-call | flops 99999997952 | bytes 5996544 | tf_op jit(solution)/shard_map/extend_kernel/pallas_call | solution.py:465
  31.2 2.9 %all-to-all-done = f32[32,4,8,128]{3,2,1,0:T(8,128)S(1)} async-done(((f32[32,4,8,128]{3,2,1,0:T(8,128)}), f32[32,4,8,128]{3,2,1,0:T(8,128)S(1)}, u32[]{:S(2)}, u32[]{:S(2)}) %all-to-all-start) | async-done | bytes 524320 | tf_op jit(solution)/shard_map/all_to_all | solution.py:568
  34.1 0.0 copy-start.9
  34.1 0.9 copy-done.9
  35.0 0.6 copy-done.12
  35.6 0.7 select_kernel.1
  36.3 16.4 %collective-permute-start.4 = (f32[34,8,128]{2,1,0:T(8,128)S(1)}, f32[34,8,128]{2,1,0:T(8,128)S(1)}, u32[]{:S(2)}, u32[]{:S(2)}) collective-permute-start(f32[34,8,128]{2,1,0:T(8,128)S(1)} %get-tuple-element.38), channel_id=1, source_target_pairs={{0,504},{8,16},{16,8},{24,32},{32,24},{40,48},{48,40},{56,64},{64,... | collective-permute-start | bytes 417800 | tf_op jit(solution)/shard_map/ppermute | solution.py:593
  52.7 1.9 %collective-permute-start.5 = (f32[28,8,128]{2,1,0:T(8,128)}, f32[28,8,128]{2,1,0:T(8,128)S(1)}, u32[]{:S(2)}, u32[]{:S(2)}) collective-permute-start(f32[28,8,128]{2,1,0:T(8,128)} %get-tuple-element.39), channel_id=1, source_target_pairs={{0,8},{8,0},{16,24},{24,16},{32,40},{40,32},{48,56},{56,48},{64,72... | collective-permute-start | bytes 344072 | tf_op jit(solution)/shard_map/ppermute | solution.py:581
  54.6 0.0 copy-done.6
  54.6 0.0 copy-done.14
  54.7 0.0 copy-start
  54.7 1.0 copy-done
  55.7 1.3 %copy-done.2 = f32[3,3,8,32,128]{4,3,2,1,0:T(8,128)S(1)} copy-done((f32[3,3,8,32,128]{4,3,2,1,0:T(8,128)S(1)}, f32[3,3,8,32,128]{4,3,2,1,0:T(8,128)}, u32[]{:S(2)}) %copy-start.2) | copy-done | bytes 1179672
  56.9 1.3 %copy-done.4 = f32[3,3,8,32,128]{4,3,2,1,0:T(8,128)S(1)} copy-done((f32[3,3,8,32,128]{4,3,2,1,0:T(8,128)S(1)}, f32[3,3,8,32,128]{4,3,2,1,0:T(8,128)}, u32[]{:S(2)}) %copy-start.4) | copy-done | bytes 1179672
  58.2 0.9 copy-done.7
  59.1 0.3 stage_kernel.1
  59.4 0.0 collective-permute-done.5.near_ref
  59.4 4.7 %collective-permute-done.4.far_ref = f32[34,8,128]{2,1,0:T(8,128)S(1)} collective-permute-done((f32[34,8,128]{2,1,0:T(8,128)S(1)}, f32[34,8,128]{2,1,0:T(8,128)S(1)}, u32[]{:S(2)}, u32[]{:S(2)}) %collective-permute-start.4) | collective-permute-done | bytes 139296 | tf_op jit(solution)/shard_map/ppermute | solution.py:593
  64.1 0.0 copy-done.13
  64.2 0.0 copy-done.15
  64.2 0.0 copy-start.5
  64.2 0.0 copy-start.8
  64.2 2.6 %trace_kernel.1 = (f32[63,8,128]{2,1,0:T(8,128)S(1)}, f32[63,8,128]{2,1,0:T(8,128)S(1)}) custom-call(s32[23]{0:T(128)S(1)} %copy-done.13, f32[2]{0:T(128)S(1)} %copy-done.15, f32[6,8,128]{2,1,0:T(8,128)S(1)} %get-tuple-element.36.mine_ref, f32[128,256]{1,0:T(8,128)S(1)} %get-tuple-element.44.wz_ref, f32[32,16]{1,0:T(8,128)S(1)} %get-tuple-element.45.wy_ref, ...), custom_call_target="tpu_custom_call" | custom-call | flops 10000000 | bytes 10000000 | tf_op jit(solution)/shard_map/trace_kernel/pallas_call | solution.py:483
  66.7 15.5 %collective-permute-start.6 = (f32[63,8,128]{2,1,0:T(8,128)S(1)}, f32[63,8,128]{2,1,0:T(8,128)S(1)}, u32[]{:S(2)}, u32[]{:S(2)}) collective-permute-start(f32[63,8,128]{2,1,0:T(8,128)S(1)} %get-tuple-element.50), channel_id=1, source_target_pairs={{8,16},{16,8},{24,32},{32,24},{40,48},{48,40},{56,64},{64,56},{72,... | collective-permute-start | bytes 774152 | tf_op jit(solution)/shard_map/ppermute | solution.py:620
  82.3 1.9 %collective-permute-start.7 = (f32[63,8,128]{2,1,0:T(8,128)S(1)}, f32[63,8,128]{2,1,0:T(8,128)S(1)}, u32[]{:S(2)}, u32[]{:S(2)}) collective-permute-start(f32[63,8,128]{2,1,0:T(8,128)S(1)} %get-tuple-element.51), channel_id=1, source_target_pairs={{0,8},{8,0},{16,24},{24,16},{32,40},{40,32},{48,56},{56,48},{64,72... | collective-permute-start | bytes 774152 | tf_op jit(solution)/shard_map/ppermute | solution.py:619
  84.2 0.0 copy-done.1
  84.2 0.0 copy-done.3
  84.2 0.0 copy-done.5
  84.2 0.0 copy-done.8
  84.2 3.2 %inner_kernel.1 = (f32[3,3,8,32,128]{4,3,2,1,0:T(8,128)S(1)}, f32[3,3,8,32,128]{4,3,2,1,0:T(8,128)S(1)}, f32[3,10,32,128]{3,2,1,0:T(8,128)S(1)}) custom-call(s32[23]{0:T(128)S(1)} %copy-done.13, f32[2]{0:T(128)S(1)} %copy-done.15, f32[6,8,128]{2,1,0:T(8,128)S(1)} %get-tuple-element.36.mine_ref, f32[128,256]{1,0:T(8,128)S(1)} %copy-done.6, ...), custom_call_target="tpu_custom_call" | custom-call | flops 10000000 | bytes 6146048 | tf_op jit(solution)/shard_map/inner_kernel/pallas_call | solution.py:465
  87.5 15.7 %collective-permute-done.6.far_ref = f32[63,8,128]{2,1,0:T(8,128)S(1)} collective-permute-done((f32[63,8,128]{2,1,0:T(8,128)S(1)}, f32[63,8,128]{2,1,0:T(8,128)S(1)}, u32[]{:S(2)}, u32[]{:S(2)}) %collective-permute-start.6) | collective-permute-done | bytes 258080 | tf_op jit(solution)/shard_map/ppermute | solution.py:620
  103.2 0.0 collective-permute-done.7.near_ref
  103.2 3.0 %window_kernel.1 = (f32[3,3,8,24,128]{4,3,2,1,0:T(8,128)}, f32[3,3,8,24,128]{4,3,2,1,0:T(8,128)}) custom-call(s32[23]{0:T(128)S(1)} %copy-done.13, f32[3,10,32,128]{3,2,1,0:T(8,128)S(1)} %get-tuple-element.43.c_ref, f32[63,8,128]{2,1,0:T(8,128)S(1)} %collective-permute-done.6.far_ref, f32[63,8,128]{2,1,0:T(8,128)S(1)} %collective-permute-done.7.near_ref, ...), custom_call_target="tpu_custom_call" | custom-call | flops 10000000 | bytes 10000000 | tf_op jit(solution)/shard_map/window_kernel/pallas_call | solution.py:483
  (13 shorter events, 0.1 us)
Async XLA Ops:
  0.6 8.3 %copy-start.16 = (s32[64]{0:T(128)S(1)}, s32[64]{0:T(128)}, u32[]{:S(2)}) copy-start(s32[64]{0:T(128)} %param.14) | copy-start | bytes 772
  0.6 14.7 %copy-start.17 = (s32[6]{0:T(128)S(1)}, s32[6]{0:T(128)}, u32[]{:S(2)}) copy-start(s32[6]{0:T(128)} %param.15) | copy-start | bytes 76
  0.7 14.8 %copy-start.10 = (f32[4,12,64]{2,0,1:T(4,128)S(1)}, f32[4,12,64]{2,0,1:T(4,128)}, u32[]{:S(2)}) copy-start(f32[4,12,64]{2,0,1:T(4,128)} %param.13) | copy-start | bytes 36868
  2.9 6.4 %collective-permute-start = (f32[4,128]{1,0:T(4,128)}, f32[4,128]{1,0:T(4,128)S(1)}, u32[]{:S(2)}, u32[]{:S(2)}) collective-permute-start(f32[4,128]{1,0:T(4,128)} %get-tuple-element.28), channel_id=1, source_target_pairs={{0,1},{1,2},{2,3},{3,4},{4,5},{5,6},{6,7},{8,9},{9,10},{10,11},{11... | collective-permute-start | bytes 6152 | tf_op jit(solution)/shard_map/ppermute | solution.py:554
  6.7 8.7 %collective-permute-start.1 = (f32[4,128]{1,0:T(4,128)}, f32[4,128]{1,0:T(4,128)S(1)}, u32[]{:S(2)}, u32[]{:S(2)}) collective-permute-start(f32[4,128]{1,0:T(4,128)} %get-tuple-element.32), channel_id=1, source_target_pairs={{1,0},{2,1},{3,2},{4,3},{5,4},{6,5},{7,6},{9,8},{10,9},{11,10},{12... | collective-permute-start | bytes 6152 | tf_op jit(solution)/shard_map/ppermute | solution.py:555
  9.3 15.3 %collective-permute-start.2 = (f32[176,4,128]{2,1,0:T(4,128)}, f32[176,4,128]{2,1,0:T(4,128)S(1)}, u32[]{:S(2)}, u32[]{:S(2)}) collective-permute-start(f32[176,4,128]{2,1,0:T(4,128)} %get-tuple-element.33), channel_id=1, source_target_pairs={{0,1},{1,2},{2,3},{3,4},{4,5},{5,6},{6,7},{8,9},{9,10},{10,11},{11... | collective-permute-start | bytes 1081352 | tf_op jit(solution)/shard_map/ppermute | solution.py:557
  13.1 13.0 %collective-permute-start.3 = (f32[176,4,128]{2,1,0:T(4,128)}, f32[176,4,128]{2,1,0:T(4,128)S(1)}, u32[]{:S(2)}, u32[]{:S(2)}) collective-permute-start(f32[176,4,128]{2,1,0:T(4,128)} %get-tuple-element.34), channel_id=1, source_target_pairs={{1,0},{2,1},{3,2},{4,3},{5,4},{6,5},{7,6},{9,8},{10,9},{11,10},{12... | collective-permute-start | bytes 1081352 | tf_op jit(solution)/shard_map/ppermute | solution.py:558
  15.4 10.7 %copy-start.11 = (s32[23]{0:T(128)}, s32[23]{0:T(128)S(1)}, u32[]{:S(2)}) copy-start(s32[23]{0:T(128)S(1)} %concatenate.3.table) | copy-start | bytes 280
  17.0 17.2 %all-to-all-start = ((f32[32,4,8,128]{3,2,1,0:T(8,128)}), f32[32,4,8,128]{3,2,1,0:T(8,128)S(1)}, u32[]{:S(2)}, u32[]{:S(2)}) async-start(f32[32,4,8,128]{3,2,1,0:T(8,128)} %tile_kernel.1), calls=%async_computation | async-start | bytes 1048576 | tf_op jit(solution)/shard_map/all_to_all | solution.py:568
  24.6 30.1 %copy-start.6 = (f32[128,256]{1,0:T(8,128)S(1)}, f32[128,256]{1,0:T(8,128)}, u32[]{:S(2)}) copy-start(f32[128,256]{1,0:T(8,128)} %constant.96.clone.wz_ref.refs_4_) | copy-start | bytes 393220
  24.6 30.1 %copy-start.14 = (f32[32,16]{1,0:T(8,128)S(1)}, f32[32,16]{1,0:T(8,128)}, u32[]{:S(2)}) copy-start(f32[32,16]{1,0:T(8,128)} %constant.97.clone.wy_ref.refs_5_) | copy-start | bytes 6148
  24.6 1.5 %copy-start.18 = (f32[176,4,128]{2,1,0:T(4,128)}, f32[176,4,128]{2,1,0:T(4,128)S(1)}, u32[]{:S(2)}) copy-start(f32[176,4,128]{2,1,0:T(4,128)S(1)} %collective-permute-done.2.lo_ref) | copy-start | bytes 1081348
  26.1 0.7 copy-start.19
  34.1 0.9 copy-start.9
  35.0 0.6 copy-start.12
  36.3 27.8 %collective-permute-start.4 = (f32[34,8,128]{2,1,0:T(8,128)S(1)}, f32[34,8,128]{2,1,0:T(8,128)S(1)}, u32[]{:S(2)}, u32[]{:S(2)}) collective-permute-start(f32[34,8,128]{2,1,0:T(8,128)S(1)} %get-tuple-element.38), channel_id=1, source_target_pairs={{0,504},{8,16},{16,8},{24,32},{32,24},{40,48},{48,40},{56,64},{64,... | collective-permute-start | bytes 417800 | tf_op jit(solution)/shard_map/ppermute | solution.py:593
  52.7 6.7 %collective-permute-start.5 = (f32[28,8,128]{2,1,0:T(8,128)}, f32[28,8,128]{2,1,0:T(8,128)S(1)}, u32[]{:S(2)}, u32[]{:S(2)}) collective-permute-start(f32[28,8,128]{2,1,0:T(8,128)} %get-tuple-element.39), channel_id=1, source_target_pairs={{0,8},{8,0},{16,24},{24,16},{32,40},{40,32},{48,56},{56,48},{64,72... | collective-permute-start | bytes 344072 | tf_op jit(solution)/shard_map/ppermute | solution.py:581
  54.7 1.0 copy-start
  55.7 1.3 %copy-start.2 = (f32[3,3,8,32,128]{4,3,2,1,0:T(8,128)S(1)}, f32[3,3,8,32,128]{4,3,2,1,0:T(8,128)}, u32[]{:S(2)}) copy-start(f32[3,3,8,32,128]{4,3,2,1,0:T(8,128)} %get-tuple-element.40.ee_ref.refs_0_) | copy-start | bytes 3538948
  56.9 1.3 %copy-start.4 = (f32[3,3,8,32,128]{4,3,2,1,0:T(8,128)S(1)}, f32[3,3,8,32,128]{4,3,2,1,0:T(8,128)}, u32[]{:S(2)}) copy-start(f32[3,3,8,32,128]{4,3,2,1,0:T(8,128)} %get-tuple-element.41.h1_ref.refs_1_) | copy-start | bytes 3538948
  58.2 0.9 copy-start.7
  59.1 5.0 %copy-start.13 = (s32[23]{0:T(128)S(1)}, s32[23]{0:T(128)}, u32[]{:S(2)}) copy-start(s32[23]{0:T(128)} %copy-done.11) | copy-start | bytes 280
  59.1 5.0 %copy-start.15 = (f32[2]{0:T(128)S(1)}, f32[2]{0:T(128)}, u32[]{:S(2)}) copy-start(f32[2]{0:T(128)} %levels.3) | copy-start | bytes 28
  64.2 20.0 %copy-start.1 = (f32[3,8,32,128]{3,2,1,0:T(8,128)S(1)}, f32[3,8,32,128]{3,2,1,0:T(8,128)}, u32[]{:S(2)}) copy-start(f32[3,8,32,128]{3,2,1,0:T(8,128)} %get-tuple-element.42.jj_ref.refs_2_) | copy-start | bytes 1179652
  64.2 20.0 %copy-start.3 = (f32[3,3,8,32,128]{4,3,2,1,0:T(8,128)S(1)}, f32[3,3,8,32,128]{4,3,2,1,0:T(8,128)}, u32[]{:S(2)}) copy-start(f32[3,3,8,32,128]{4,3,2,1,0:T(8,128)} %get-tuple-element.40.ee_ref.refs_0_) | copy-start | bytes 3538948
  64.2 20.1 %copy-start.5 = (f32[3,3,8,32,128]{4,3,2,1,0:T(8,128)S(1)}, f32[3,3,8,32,128]{4,3,2,1,0:T(8,128)}, u32[]{:S(2)}) copy-start(f32[3,3,8,32,128]{4,3,2,1,0:T(8,128)} %get-tuple-element.41.h1_ref.refs_1_) | copy-start | bytes 3538948
  64.2 20.1 %copy-start.8 = (f32[8,32,128]{2,1,0:T(8,128)S(1)}, f32[8,32,128]{2,1,0:T(8,128)}, u32[]{:S(2)}) copy-start(f32[8,32,128]{2,1,0:T(8,128)} %get-tuple-element.37.mm_ref.refs_3_) | copy-start | bytes 393220
  66.7 36.4 %collective-permute-start.6 = (f32[63,8,128]{2,1,0:T(8,128)S(1)}, f32[63,8,128]{2,1,0:T(8,128)S(1)}, u32[]{:S(2)}, u32[]{:S(2)}) collective-permute-start(f32[63,8,128]{2,1,0:T(8,128)S(1)} %get-tuple-element.50), channel_id=1, source_target_pairs={{8,16},{16,8},{24,32},{32,24},{40,48},{48,40},{56,64},{64,56},{72,... | collective-permute-start | bytes 774152 | tf_op jit(solution)/shard_map/ppermute | solution.py:620
  82.3 20.9 %collective-permute-start.7 = (f32[63,8,128]{2,1,0:T(8,128)S(1)}, f32[63,8,128]{2,1,0:T(8,128)S(1)}, u32[]{:S(2)}, u32[]{:S(2)}) collective-permute-start(f32[63,8,128]{2,1,0:T(8,128)S(1)} %get-tuple-element.51), channel_id=1, source_target_pairs={{0,8},{8,0},{16,24},{24,16},{32,40},{40,32},{48,56},{56,48},{64,72... | collective-permute-start | bytes 774152 | tf_op jit(solution)/shard_map/ppermute | solution.py:619

commit v5 on v4

--- a/solution.py
+++ b/solution.py
@@ -114,14 +114,11 @@
             spread_ref[i, q] = packed
 
 
-def select_kernel(table, g_ref, message_ref, mine_ref, far_ref, sem):
-    copy = pltpu.make_async_copy(message_ref, far_ref.at[pl.ds(COARSE, 3 * FIRST_TILES + 4)], sem)
-    copy.start()
-    for at, ref in ((MINE, mine_ref), (THEIRS, far_ref)):
+def select_kernel(table, g_ref, mine_ref, theirs_ref):
+    for at, ref in ((MINE, mine_ref), (THEIRS, theirs_ref)):
         for i, (which, q) in enumerate(((0, 3), (1, 0), (1, 1), (1, 2), (1, 3), (2, 0))):
             held = g_ref[table[at + which] * 4 + q]
             ref[i] = jnp.where(table[at + 3 + which] == 1, held, 0.0)
-    copy.wait()
 
 
 def extend_kernel(
@@ -153,7 +150,7 @@
         up = e
     far, near = select(core == 1, upward, downward), select(core == 1, downward, upward)
     for i in range(FIRST_TILES):
-        far_ref[r * FIRST_TILES + i] = far[i]
+        far_ref[COARSE + r * FIRST_TILES + i] = far[i]
         near_ref[r * FIRST_TILES + i] = near[i]
 
     @pl.when(r == 0)
@@ -165,7 +162,7 @@
         above, below = tiles_of(mm_ref[PLANES - 1]), tiles_of(mm_ref[0])
         far, near = select(core == 1, above, below), select(core == 1, below, above)
         for i in range(4):
-            far_ref[3 * FIRST_TILES + i] = far[i]
+            far_ref[COARSE + 3 * FIRST_TILES + i] = far[i]
             near_ref[3 * FIRST_TILES + i] = near[i]
 
 
@@ -575,21 +572,22 @@
         extend_kernel,
         (table,),
         [(electric, True), (magnetic, True), (current, None), (material_mask, None), (low, None), (high, None)],
-        [(extended, True), (extended, True), ((3, *planes), None), (planes, None), (message, None), (message, None)],
+        [(extended, True), (extended, True), ((3, *planes), None), (planes, None), ((COARSE + message[0], 8, LANES), None), (message, None)],
         100_000_000_000,
     )
     near = lax.ppermute(near, "wide", near_pairs)
 
-    mine, far = run(
+    coarse = (COARSE, 8, LANES)
+    mine, theirs = run(
         select_kernel,
         (table,),
-        [(gathered, None), (far, pl.ANY)],
-        [((COARSE, 8, LANES), None), ((COARSE + message[0], 8, LANES), None)],
+        [(gathered, None)],
+        [(coarse, None), (coarse, None)],
         1_000_000,
-        [pltpu.SemaphoreType.DMA],
         steps=1,
         limit=8,
     )
+    far = lax.dynamic_update_slice(far, theirs, (0, 0, 0))
     far = lax.ppermute(far, "wide", far_ring)
     fields = [(e_ext, True), (h_one, True), (j_ext, None)]
 

time: 107 us -> 107 us (level)
    unnamed x40 -> x38, local copies, waits for them, and re-layouts: 6.72 us -> 5.89 us
where the time goes in v5:
time: 107 us; the launch traced here: 106 us
  starting transfers between devices  54.9 us (51%)
  waiting for transfers between devices  25.1 us (23%)
  Pallas kernels  17.8 us (17%)
  local copies, waits for them, and re-layouts  6.76 us (6%)
    ppermute x1, starting transfers between devices, body(): far = lax.ppermute(far, 'wide', far_ring)  16.3 us
    ppermute x1, waiting for transfers between devices, body(): far_end = lax.ppermute(far_end, 'wide', far_pairs)  15.7 us
    ppermute x1, starting transfers between devices, body(): far_end = lax.ppermute(far_end, 'wide', far_pairs)  15.4 us
    pallas_call x6, Pallas kernels, run(): pl.pallas_call(kernel, grid=(steps,), in_specs=[pl.BlockSpec(memory_space...  12.3 us
    all_to_all x1, starting transfers between devices, body(): lax.all_to_all(spread, 'wide', 0, 0, axis_index_groups=groups, tiled=True)  7.6 us
    unnamed x38, local copies, waits for them, and re-layouts  5.89 us
    pallas_call x2, Pallas kernels, run_in_place(): pl.pallas_call(kernel, in_specs=[pl.BlockSpec(memory_space=pltpu.SMEM)] *...  5.54 us
    ppermute x1, waiting for transfers between devices, body(): far = lax.ppermute(far, 'wide', far_ring)  5.02 us
  transfers between devices with their start and end apart: 9, of which 4 were waited for; matrix products, arithmetic and copies ran while one was open for 1% of the time, Pallas kernels for 9%

profile of v5, /device:TPU:36, one launch (start us, length us, event | category | flops | bytes accessed | tf_op | source)
XLA Modules:
  0.0 105.9 jit_solution(14122952130856388013)
XLA Ops:
  0.6 0.0 copy-start.15
  0.6 0.0 copy-start.16
  0.7 0.0 copy-start.9
  0.7 2.3 %pack_kernel.1 = (f32[176,4,128]{2,1,0:T(4,128)}, f32[176,4,128]{2,1,0:T(4,128)}, f32[4,128]{1,0:T(4,128)}, f32[4,128]{1,0:T(4,128)}) custom-call(f32[72,24,128]{2,1,0:T(8,128)} %bitcast.30, f32[72,24,128]{2,1,0:T(8,128)} %bitcast.31, f32[72,24,128]{2,1,0:T(8,128)} %bitcast.32, f32[72,24,128]{2,1,0:T(8,128)} %bitcast.33, f32[24,24,128]{2,1,0:T(8,128)} %bitcast.34, ...), custom_call_target="tpu_custom_call" | custom-call | flops 1000000 | bytes 5062656 | tf_op jit(solution)/shard_map/pack_kernel/pallas_call | solution.py:462
  2.9 3.8 %collective-permute-start = (f32[4,128]{1,0:T(4,128)}, f32[4,128]{1,0:T(4,128)S(1)}, u32[]{:S(2)}, u32[]{:S(2)}) collective-permute-start(f32[4,128]{1,0:T(4,128)} %get-tuple-element.28), channel_id=1, source_target_pairs={{0,1},{1,2},{2,3},{3,4},{4,5},{5,6},{6,7},{8,9},{9,10},{10,11},{11... | collective-permute-start | bytes 6152 | tf_op jit(solution)/shard_map/ppermute | solution.py:551
  6.7 2.0 %collective-permute-start.1 = (f32[4,128]{1,0:T(4,128)}, f32[4,128]{1,0:T(4,128)S(1)}, u32[]{:S(2)}, u32[]{:S(2)}) collective-permute-start(f32[4,128]{1,0:T(4,128)} %get-tuple-element.32), channel_id=1, source_target_pairs={{1,0},{2,1},{3,2},{4,3},{5,4},{6,5},{7,6},{9,8},{10,9},{11,10},{12... | collective-permute-start | bytes 6152 | tf_op jit(solution)/shard_map/ppermute | solution.py:552
  8.8 0.1 pad_add_fusion.1
  8.9 0.1 add_clamp_fusion
  9.0 0.0 copy-done.15
  9.0 0.2 fusion
  9.2 0.1 copy.13
  9.3 0.0 collective-permute-done.lo_ref
  9.3 3.8 %collective-permute-start.2 = (f32[176,4,128]{2,1,0:T(4,128)}, f32[176,4,128]{2,1,0:T(4,128)S(1)}, u32[]{:S(2)}, u32[]{:S(2)}) collective-permute-start(f32[176,4,128]{2,1,0:T(4,128)} %get-tuple-element.34), channel_id=1, source_target_pairs={{0,1},{1,2},{2,3},{3,4},{4,5},{5,6},{6,7},{8,9},{9,10},{10,11},{11... | collective-permute-start | bytes 1081352 | tf_op jit(solution)/shard_map/ppermute | solution.py:554
  13.1 2.0 %collective-permute-start.3 = (f32[176,4,128]{2,1,0:T(4,128)}, f32[176,4,128]{2,1,0:T(4,128)S(1)}, u32[]{:S(2)}, u32[]{:S(2)}) collective-permute-start(f32[176,4,128]{2,1,0:T(4,128)} %get-tuple-element.35), channel_id=1, source_target_pairs={{1,0},{2,1},{3,2},{4,3},{5,4},{6,5},{7,6},{9,8},{10,9},{11,10},{12... | collective-permute-start | bytes 1081352 | tf_op jit(solution)/shard_map/ppermute | solution.py:555
  15.2 0.1 reshape.200
  15.3 0.0 copy-done.16
  15.3 0.1 concatenate.3.table
  15.4 0.0 copy-start.10
  15.4 0.0 collective-permute-done.1.hi_ref
  15.4 0.0 copy-done.9
  15.4 1.5 %tile_kernel.1 = f32[32,4,8,128]{3,2,1,0:T(8,128)} custom-call(s32[23]{0:T(128)S(1)} %concatenate.3.table, f32[12,4,64]{2,1,0:T(4,128)S(1)} %bitcast.29, f32[4,128]{1,0:T(4,128)S(1)} %collective-permute-done.lo_ref, f32[4,128]{1,0:T(4,128)S(1)} %collective-permute-done.1.hi_ref), custom_call_target="tpu_custom_call" | custom-call | flops 1000000 | bytes 540672 | tf_op jit(solution)/shard_map/tile_kernel/pallas_call | solution.py:462
  17.0 7.6 %all-to-all-start = ((f32[32,4,8,128]{3,2,1,0:T(8,128)}), f32[32,4,8,128]{3,2,1,0:T(8,128)S(1)}, u32[]{:S(2)}, u32[]{:S(2)}) async-start(f32[32,4,8,128]{3,2,1,0:T(8,128)} %tile_kernel.1), calls=%async_computation | async-start | bytes 1048576 | tf_op jit(solution)/shard_map/all_to_all | solution.py:565
  24.6 0.0 copy-start.6
  24.6 0.0 copy-start.13
  24.6 0.0 collective-permute-done.2.lo_ref
  24.6 0.0 copy-start.17
  24.6 1.5 %collective-permute-done.3.hi_ref = f32[176,4,128]{2,1,0:T(4,128)S(1)} collective-permute-done((f32[176,4,128]{2,1,0:T(4,128)}, f32[176,4,128]{2,1,0:T(4,128)S(1)}, u32[]{:S(2)}, u32[]{:S(2)}) %collective-permute-start.3) | collective-permute-done | bytes 360480 | tf_op jit(solution)/shard_map/ppermute | solution.py:555
  26.1 0.0 copy-done.10
  26.1 0.0 copy-done.17
  26.1 0.0 copy-start.18
  26.1 0.7 copy-done.18
  26.8 4.4 %extend_kernel.1 = (f32[3,3,8,32,128]{4,3,2,1,0:T(8,128)}, f32[3,3,8,32,128]{4,3,2,1,0:T(8,128)}, f32[3,8,32,128]{3,2,1,0:T(8,128)}, f32[8,32,128]{2,1,0:T(8,128...) custom-call(s32[23]{0:T(128)} %copy-done.10, f32[3,3,8,24,128]{4,3,2,1,0:T(8,128)} %e_ref.1, ...), custom_call_target="tpu_custom_call" | custom-call | flops 99999997952 | bytes 6021120 | tf_op jit(solution)/shard_map/extend_kernel/pallas_call | solution.py:462
  31.3 2.8 %all-to-all-done = f32[32,4,8,128]{3,2,1,0:T(8,128)S(1)} async-done(((f32[32,4,8,128]{3,2,1,0:T(8,128)}), f32[32,4,8,128]{3,2,1,0:T(8,128)S(1)}, u32[]{:S(2)}, u32[]{:S(2)}) %all-to-all-start) | async-done | bytes 524320 | tf_op jit(solution)/shard_map/all_to_all | solution.py:565
  34.1 0.0 copy-start.11
  34.1 0.7 copy-done.11
  34.8 0.6 select_kernel.1
  35.3 0.6 constant_dynamic-update-slice_fusion
  35.9 16.3 %collective-permute-start.4 = (f32[34,8,128]{2,1,0:T(8,128)}, f32[34,8,128]{2,1,0:T(8,128)S(1)}, u32[]{:S(2)}, u32[]{:S(2)}) collective-permute-start(f32[34,8,128]{2,1,0:T(8,128)} %constant_dynamic-update-slice_fusion), channel_id=1, source_target_pairs={{0,504},{8,16},{16,8},{24,32},{32,24},{40,48},{48,40},{56,64},{64,... | collective-permute-start | bytes 417800 | tf_op jit(solution)/shard_map/ppermute | solution.py:591
  52.3 1.9 %collective-permute-start.5 = (f32[28,8,128]{2,1,0:T(8,128)}, f32[28,8,128]{2,1,0:T(8,128)S(1)}, u32[]{:S(2)}, u32[]{:S(2)}) collective-permute-start(f32[28,8,128]{2,1,0:T(8,128)} %get-tuple-element.39), channel_id=1, source_target_pairs={{0,8},{8,0},{16,24},{24,16},{32,40},{40,32},{48,56},{56,48},{64,72... | collective-permute-start | bytes 344072 | tf_op jit(solution)/shard_map/ppermute | solution.py:578
  54.2 0.0 copy-done.6
  54.2 0.0 copy-done.13
  54.2 0.0 copy-start
  54.3 1.0 copy-done
  55.3 1.3 %copy-done.2 = f32[3,3,8,32,128]{4,3,2,1,0:T(8,128)S(1)} copy-done((f32[3,3,8,32,128]{4,3,2,1,0:T(8,128)S(1)}, f32[3,3,8,32,128]{4,3,2,1,0:T(8,128)}, u32[]{:S(2)}) %copy-start.2) | copy-done | bytes 1179672
  56.5 1.3 %copy-done.4 = f32[3,3,8,32,128]{4,3,2,1,0:T(8,128)S(1)} copy-done((f32[3,3,8,32,128]{4,3,2,1,0:T(8,128)S(1)}, f32[3,3,8,32,128]{4,3,2,1,0:T(8,128)}, u32[]{:S(2)}) %copy-start.4) | copy-done | bytes 1179672
  57.8 0.9 copy-done.7
  58.7 0.3 stage_kernel.1
  59.0 0.0 collective-permute-done.5.near_ref
  59.0 5.0 %collective-permute-done.4.far_ref = f32[34,8,128]{2,1,0:T(8,128)S(1)} collective-permute-done((f32[34,8,128]{2,1,0:T(8,128)}, f32[34,8,128]{2,1,0:T(8,128)S(1)}, u32[]{:S(2)}, u32[]{:S(2)}) %collective-permute-start.4) | collective-permute-done | bytes 139296 | tf_op jit(solution)/shard_map/ppermute | solution.py:591
  64.1 0.0 copy-done.12
  64.1 0.0 copy-done.14
  64.1 0.0 copy-start.5
  64.1 0.0 copy-start.8
  64.1 2.5 %trace_kernel.1 = (f32[63,8,128]{2,1,0:T(8,128)S(1)}, f32[63,8,128]{2,1,0:T(8,128)S(1)}) custom-call(s32[23]{0:T(128)S(1)} %copy-done.12, f32[2]{0:T(128)S(1)} %copy-done.14, f32[6,8,128]{2,1,0:T(8,128)S(1)} %get-tuple-element.33.mine_ref, f32[128,256]{1,0:T(8,128)S(1)} %get-tuple-element.44.wz_ref, f32[32,16]{1,0:T(8,128)S(1)} %get-tuple-element.45.wy_ref, ...), custom_call_target="tpu_custom_call" | custom-call | flops 10000000 | bytes 10000000 | tf_op jit(solution)/shard_map/trace_kernel/pallas_call | solution.py:480
  66.6 15.4 %collective-permute-start.6 = (f32[63,8,128]{2,1,0:T(8,128)S(1)}, f32[63,8,128]{2,1,0:T(8,128)S(1)}, u32[]{:S(2)}, u32[]{:S(2)}) collective-permute-start(f32[63,8,128]{2,1,0:T(8,128)S(1)} %get-tuple-element.50), channel_id=1, source_target_pairs={{8,16},{16,8},{24,32},{32,24},{40,48},{48,40},{56,64},{64,56},{72,... | collective-permute-start | bytes 774152 | tf_op jit(solution)/shard_map/ppermute | solution.py:618
  82.0 1.9 %collective-permute-start.7 = (f32[63,8,128]{2,1,0:T(8,128)S(1)}, f32[63,8,128]{2,1,0:T(8,128)S(1)}, u32[]{:S(2)}, u32[]{:S(2)}) collective-permute-start(f32[63,8,128]{2,1,0:T(8,128)S(1)} %get-tuple-element.51), channel_id=1, source_target_pairs={{0,8},{8,0},{16,24},{24,16},{32,40},{40,32},{48,56},{56,48},{64,72... | collective-permute-start | bytes 774152 | tf_op jit(solution)/shard_map/ppermute | solution.py:617
  84.0 0.0 copy-done.1
  84.0 0.0 copy-done.3
  84.0 0.0 copy-done.5
  84.0 0.0 copy-done.8
  84.0 3.2 %inner_kernel.1 = (f32[3,3,8,32,128]{4,3,2,1,0:T(8,128)S(1)}, f32[3,3,8,32,128]{4,3,2,1,0:T(8,128)S(1)}, f32[3,10,32,128]{3,2,1,0:T(8,128)S(1)}) custom-call(s32[23]{0:T(128)S(1)} %copy-done.12, f32[2]{0:T(128)S(1)} %copy-done.14, f32[6,8,128]{2,1,0:T(8,128)S(1)} %get-tuple-element.33.mine_ref, f32[128,256]{1,0:T(8,128)S(1)} %copy-done.6, ...), custom_call_target="tpu_custom_call" | custom-call | flops 10000000 | bytes 6146048 | tf_op jit(solution)/shard_map/inner_kernel/pallas_call | solution.py:462
  87.2 15.7 %collective-permute-done.6.far_ref = f32[63,8,128]{2,1,0:T(8,128)S(1)} collective-permute-done((f32[63,8,128]{2,1,0:T(8,128)S(1)}, f32[63,8,128]{2,1,0:T(8,128)S(1)}, u32[]{:S(2)}, u32[]{:S(2)}) %collective-permute-start.6) | collective-permute-done | bytes 258080 | tf_op jit(solution)/shard_map/ppermute | solution.py:618
  102.9 0.0 collective-permute-done.7.near_ref
  102.9 3.0 %window_kernel.1 = (f32[3,3,8,24,128]{4,3,2,1,0:T(8,128)}, f32[3,3,8,24,128]{4,3,2,1,0:T(8,128)}) custom-call(s32[23]{0:T(128)S(1)} %copy-done.12, f32[3,10,32,128]{3,2,1,0:T(8,128)S(1)} %get-tuple-element.43.c_ref, f32[63,8,128]{2,1,0:T(8,128)S(1)} %collective-permute-done.6.far_ref, f32[63,8,128]{2,1,0:T(8,128)S(1)} %collective-permute-done.7.near_ref, ...), custom_call_target="tpu_custom_call" | custom-call | flops 10000000 | bytes 10000000 | tf_op jit(solution)/shard_map/window_kernel/pallas_call | solution.py:480
  (12 shorter events, 0.1 us)
Async XLA Ops:
  0.6 8.3 %copy-start.15 = (s32[64]{0:T(128)S(1)}, s32[64]{0:T(128)}, u32[]{:S(2)}) copy-start(s32[64]{0:T(128)} %param.14) | copy-start | bytes 772
  0.6 14.7 %copy-start.16 = (s32[6]{0:T(128)S(1)}, s32[6]{0:T(128)}, u32[]{:S(2)}) copy-start(s32[6]{0:T(128)} %param.15) | copy-start | bytes 76
  0.7 14.8 %copy-start.9 = (f32[4,12,64]{2,0,1:T(4,128)S(1)}, f32[4,12,64]{2,0,1:T(4,128)}, u32[]{:S(2)}) copy-start(f32[4,12,64]{2,0,1:T(4,128)} %param.13) | copy-start | bytes 36868
  2.9 6.4 %collective-permute-start = (f32[4,128]{1,0:T(4,128)}, f32[4,128]{1,0:T(4,128)S(1)}, u32[]{:S(2)}, u32[]{:S(2)}) collective-permute-start(f32[4,128]{1,0:T(4,128)} %get-tuple-element.28), channel_id=1, source_target_pairs={{0,1},{1,2},{2,3},{3,4},{4,5},{5,6},{6,7},{8,9},{9,10},{10,11},{11... | collective-permute-start | bytes 6152 | tf_op jit(solution)/shard_map/ppermute | solution.py:551
  6.7 8.7 %collective-permute-start.1 = (f32[4,128]{1,0:T(4,128)}, f32[4,128]{1,0:T(4,128)S(1)}, u32[]{:S(2)}, u32[]{:S(2)}) collective-permute-start(f32[4,128]{1,0:T(4,128)} %get-tuple-element.32), channel_id=1, source_target_pairs={{1,0},{2,1},{3,2},{4,3},{5,4},{6,5},{7,6},{9,8},{10,9},{11,10},{12... | collective-permute-start | bytes 6152 | tf_op jit(solution)/shard_map/ppermute | solution.py:552
  9.3 15.3 %collective-permute-start.2 = (f32[176,4,128]{2,1,0:T(4,128)}, f32[176,4,128]{2,1,0:T(4,128)S(1)}, u32[]{:S(2)}, u32[]{:S(2)}) collective-permute-start(f32[176,4,128]{2,1,0:T(4,128)} %get-tuple-element.34), channel_id=1, source_target_pairs={{0,1},{1,2},{2,3},{3,4},{4,5},{5,6},{6,7},{8,9},{9,10},{10,11},{11... | collective-permute-start | bytes 1081352 | tf_op jit(solution)/shard_map/ppermute | solution.py:554
  13.1 13.0 %collective-permute-start.3 = (f32[176,4,128]{2,1,0:T(4,128)}, f32[176,4,128]{2,1,0:T(4,128)S(1)}, u32[]{:S(2)}, u32[]{:S(2)}) collective-permute-start(f32[176,4,128]{2,1,0:T(4,128)} %get-tuple-element.35), channel_id=1, source_target_pairs={{1,0},{2,1},{3,2},{4,3},{5,4},{6,5},{7,6},{9,8},{10,9},{11,10},{12... | collective-permute-start | bytes 1081352 | tf_op jit(solution)/shard_map/ppermute | solution.py:555
  15.4 10.7 %copy-start.10 = (s32[23]{0:T(128)}, s32[23]{0:T(128)S(1)}, u32[]{:S(2)}) copy-start(s32[23]{0:T(128)S(1)} %concatenate.3.table) | copy-start | bytes 280
  17.0 17.2 %all-to-all-start = ((f32[32,4,8,128]{3,2,1,0:T(8,128)}), f32[32,4,8,128]{3,2,1,0:T(8,128)S(1)}, u32[]{:S(2)}, u32[]{:S(2)}) async-start(f32[32,4,8,128]{3,2,1,0:T(8,128)} %tile_kernel.1), calls=%async_computation | async-start | bytes 1048576 | tf_op jit(solution)/shard_map/all_to_all | solution.py:565
  24.6 29.7 %copy-start.6 = (f32[128,256]{1,0:T(8,128)S(1)}, f32[128,256]{1,0:T(8,128)}, u32[]{:S(2)}) copy-start(f32[128,256]{1,0:T(8,128)} %constant.96.clone.wz_ref.refs_4_) | copy-start | bytes 393220
  24.6 29.7 %copy-start.13 = (f32[32,16]{1,0:T(8,128)S(1)}, f32[32,16]{1,0:T(8,128)}, u32[]{:S(2)}) copy-start(f32[32,16]{1,0:T(8,128)} %constant.97.clone.wy_ref.refs_5_) | copy-start | bytes 6148
  24.6 1.5 %copy-start.17 = (f32[176,4,128]{2,1,0:T(4,128)}, f32[176,4,128]{2,1,0:T(4,128)S(1)}, u32[]{:S(2)}) copy-start(f32[176,4,128]{2,1,0:T(4,128)S(1)} %collective-permute-done.2.lo_ref) | copy-start | bytes 1081348
  26.1 0.7 copy-start.18
  34.1 0.7 copy-start.11
  35.9 28.1 %collective-permute-start.4 = (f32[34,8,128]{2,1,0:T(8,128)}, f32[34,8,128]{2,1,0:T(8,128)S(1)}, u32[]{:S(2)}, u32[]{:S(2)}) collective-permute-start(f32[34,8,128]{2,1,0:T(8,128)} %constant_dynamic-update-slice_fusion), channel_id=1, source_target_pairs={{0,504},{8,16},{16,8},{24,32},{32,24},{40,48},{48,40},{56,64},{64,... | collective-permute-start | bytes 417800 | tf_op jit(solution)/shard_map/ppermute | solution.py:591
  52.3 6.7 %collective-permute-start.5 = (f32[28,8,128]{2,1,0:T(8,128)}, f32[28,8,128]{2,1,0:T(8,128)S(1)}, u32[]{:S(2)}, u32[]{:S(2)}) collective-permute-start(f32[28,8,128]{2,1,0:T(8,128)} %get-tuple-element.39), channel_id=1, source_target_pairs={{0,8},{8,0},{16,24},{24,16},{32,40},{40,32},{48,56},{56,48},{64,72... | collective-permute-start | bytes 344072 | tf_op jit(solution)/shard_map/ppermute | solution.py:578
  54.2 1.0 copy-start
  55.2 1.3 %copy-start.2 = (f32[3,3,8,32,128]{4,3,2,1,0:T(8,128)S(1)}, f32[3,3,8,32,128]{4,3,2,1,0:T(8,128)}, u32[]{:S(2)}) copy-start(f32[3,3,8,32,128]{4,3,2,1,0:T(8,128)} %get-tuple-element.40.ee_ref.refs_0_) | copy-start | bytes 3538948
  56.5 1.3 %copy-start.4 = (f32[3,3,8,32,128]{4,3,2,1,0:T(8,128)S(1)}, f32[3,3,8,32,128]{4,3,2,1,0:T(8,128)}, u32[]{:S(2)}) copy-start(f32[3,3,8,32,128]{4,3,2,1,0:T(8,128)} %get-tuple-element.41.h1_ref.refs_1_) | copy-start | bytes 3538948
  57.8 0.9 copy-start.7
  58.7 5.4 %copy-start.12 = (s32[23]{0:T(128)S(1)}, s32[23]{0:T(128)}, u32[]{:S(2)}) copy-start(s32[23]{0:T(128)} %copy-done.10) | copy-start | bytes 280
  58.7 5.4 %copy-start.14 = (f32[2]{0:T(128)S(1)}, f32[2]{0:T(128)}, u32[]{:S(2)}) copy-start(f32[2]{0:T(128)} %levels.3) | copy-start | bytes 28
  64.1 19.9 %copy-start.1 = (f32[3,8,32,128]{3,2,1,0:T(8,128)S(1)}, f32[3,8,32,128]{3,2,1,0:T(8,128)}, u32[]{:S(2)}) copy-start(f32[3,8,32,128]{3,2,1,0:T(8,128)} %get-tuple-element.42.jj_ref.refs_2_) | copy-start | bytes 1179652
  64.1 19.9 %copy-start.3 = (f32[3,3,8,32,128]{4,3,2,1,0:T(8,128)S(1)}, f32[3,3,8,32,128]{4,3,2,1,0:T(8,128)}, u32[]{:S(2)}) copy-start(f32[3,3,8,32,128]{4,3,2,1,0:T(8,128)} %get-tuple-element.40.ee_ref.refs_0_) | copy-start | bytes 3538948
  64.1 19.9 %copy-start.5 = (f32[3,3,8,32,128]{4,3,2,1,0:T(8,128)S(1)}, f32[3,3,8,32,128]{4,3,2,1,0:T(8,128)}, u32[]{:S(2)}) copy-start(f32[3,3,8,32,128]{4,3,2,1,0:T(8,128)} %get-tuple-element.41.h1_ref.refs_1_) | copy-start | bytes 3538948
  64.1 19.9 %copy-start.8 = (f32[8,32,128]{2,1,0:T(8,128)S(1)}, f32[8,32,128]{2,1,0:T(8,128)}, u32[]{:S(2)}) copy-start(f32[8,32,128]{2,1,0:T(8,128)} %get-tuple-element.36.mm_ref.refs_3_) | copy-start | bytes 393220
  66.6 36.3 %collective-permute-start.6 = (f32[63,8,128]{2,1,0:T(8,128)S(1)}, f32[63,8,128]{2,1,0:T(8,128)S(1)}, u32[]{:S(2)}, u32[]{:S(2)}) collective-permute-start(f32[63,8,128]{2,1,0:T(8,128)S(1)} %get-tuple-element.50), channel_id=1, source_target_pairs={{8,16},{16,8},{24,32},{32,24},{40,48},{48,40},{56,64},{64,56},{72,... | collective-permute-start | bytes 774152 | tf_op jit(solution)/shard_map/ppermute | solution.py:618
  82.0 20.9 %collective-permute-start.7 = (f32[63,8,128]{2,1,0:T(8,128)S(1)}, f32[63,8,128]{2,1,0:T(8,128)S(1)}, u32[]{:S(2)}, u32[]{:S(2)}) collective-permute-start(f32[63,8,128]{2,1,0:T(8,128)S(1)} %get-tuple-element.51), channel_id=1, source_target_pairs={{0,8},{8,0},{16,24},{24,16},{32,40},{40,32},{48,56},{56,48},{64,72... | collective-permute-start | bytes 774152 | tf_op jit(solution)/shard_map/ppermute | solution.py:617

commit v6 on v5

--- a/solution.py
+++ b/solution.py
@@ -451,6 +451,8 @@
         rank = len(shape)
         if block is pl.ANY:
             return pl.BlockSpec(memory_space=pl.ANY)
+        if block == 'halves':
+            return pl.BlockSpec((shape[0] // 2, *shape[1:]), lambda r: (r,) + (0,) * (rank - 1))
         if block is None:
             return pl.BlockSpec(tuple(shape), lambda r: (0,) * rank)
         if block is True:
@@ -557,9 +559,9 @@
         tile_kernel,
         (table,),
         [(tile, None), (tile_lo, None), (tile_hi, None)],
-        [((half, 4, 8, LANES), None)],
+        [((half, 4, 8, LANES), 'halves')],
         1_000_000,
-        steps=1,
+        steps=2,
         limit=8,
     )
     gathered = lax.all_to_all(spread, "wide", 0, 0, axis_index_groups=groups, tiled=True)

time: 107 us -> 107 us (level)
  no operation moved by 1% of the time
where the time goes in v6:
time: 107 us; the launch traced here: 106 us
  starting transfers between devices  54.9 us (51%)
  waiting for transfers between devices  25.1 us (23%)
  Pallas kernels  17.9 us (17%)
  local copies, waits for them, and re-layouts  6.76 us (6%)
    ppermute x1, starting transfers between devices, body(): far = lax.ppermute(far, 'wide', far_ring)  16.3 us
    ppermute x1, waiting for transfers between devices, body(): far_end = lax.ppermute(far_end, 'wide', far_pairs)  15.7 us
    ppermute x1, starting transfers between devices, body(): far_end = lax.ppermute(far_end, 'wide', far_pairs)  15.4 us
    pallas_call x6, Pallas kernels, run(): pl.pallas_call(kernel, grid=(steps,), in_specs=[pl.BlockSpec(memory_space...  12.4 us
    all_to_all x1, starting transfers between devices, body(): lax.all_to_all(spread, 'wide', 0, 0, axis_index_groups=groups, tiled=True)  7.6 us
    unnamed x38, local copies, waits for them, and re-layouts  5.89 us
    pallas_call x2, Pallas kernels, run_in_place(): pl.pallas_call(kernel, in_specs=[pl.BlockSpec(memory_space=pltpu.SMEM)] *...  5.54 us
    ppermute x1, waiting for transfers between devices, body(): far = lax.ppermute(far, 'wide', far_ring)  5.02 us
  transfers between devices with their start and end apart: 9, of which 4 were waited for; matrix products, arithmetic and copies ran while one was open for 1% of the time, Pallas kernels for 9%

profile of v6, /device:TPU:36, one launch (start us, length us, event | category | flops | bytes accessed | tf_op | source)
XLA Modules:
  0.0 106.0 jit_solution(10314080144872477475)
XLA Ops:
  0.6 0.0 copy-start.15
  0.6 0.0 copy-start.16
  0.7 0.0 copy-start.9
  0.7 2.3 %pack_kernel.1 = (f32[176,4,128]{2,1,0:T(4,128)}, f32[176,4,128]{2,1,0:T(4,128)}, f32[4,128]{1,0:T(4,128)}, f32[4,128]{1,0:T(4,128)}) custom-call(f32[72,24,128]{2,1,0:T(8,128)} %bitcast.30, f32[72,24,128]{2,1,0:T(8,128)} %bitcast.31, f32[72,24,128]{2,1,0:T(8,128)} %bitcast.32, f32[72,24,128]{2,1,0:T(8,128)} %bitcast.33, f32[24,24,128]{2,1,0:T(8,128)} %bitcast.34, ...), custom_call_target="tpu_custom_call" | custom-call | flops 1000000 | bytes 5062656 | tf_op jit(solution)/shard_map/pack_kernel/pallas_call | solution.py:464
  2.9 3.8 %collective-permute-start = (f32[4,128]{1,0:T(4,128)}, f32[4,128]{1,0:T(4,128)S(1)}, u32[]{:S(2)}, u32[]{:S(2)}) collective-permute-start(f32[4,128]{1,0:T(4,128)} %get-tuple-element.28), channel_id=1, source_target_pairs={{0,1},{1,2},{2,3},{3,4},{4,5},{5,6},{6,7},{8,9},{9,10},{10,11},{11... | collective-permute-start | bytes 6152 | tf_op jit(solution)/shard_map/ppermute | solution.py:553
  6.7 2.0 %collective-permute-start.1 = (f32[4,128]{1,0:T(4,128)}, f32[4,128]{1,0:T(4,128)S(1)}, u32[]{:S(2)}, u32[]{:S(2)}) collective-permute-start(f32[4,128]{1,0:T(4,128)} %get-tuple-element.32), channel_id=1, source_target_pairs={{1,0},{2,1},{3,2},{4,3},{5,4},{6,5},{7,6},{9,8},{10,9},{11,10},{12... | collective-permute-start | bytes 6152 | tf_op jit(solution)/shard_map/ppermute | solution.py:554
  8.8 0.1 pad_add_fusion.1
  8.9 0.1 add_clamp_fusion
  9.0 0.0 copy-done.15
  9.0 0.2 fusion
  9.2 0.1 copy.13
  9.3 0.0 collective-permute-done.lo_ref
  9.3 3.8 %collective-permute-start.2 = (f32[176,4,128]{2,1,0:T(4,128)}, f32[176,4,128]{2,1,0:T(4,128)S(1)}, u32[]{:S(2)}, u32[]{:S(2)}) collective-permute-start(f32[176,4,128]{2,1,0:T(4,128)} %get-tuple-element.34), channel_id=1, source_target_pairs={{0,1},{1,2},{2,3},{3,4},{4,5},{5,6},{6,7},{8,9},{9,10},{10,11},{11... | collective-permute-start | bytes 1081352 | tf_op jit(solution)/shard_map/ppermute | solution.py:556
  13.1 2.0 %collective-permute-start.3 = (f32[176,4,128]{2,1,0:T(4,128)}, f32[176,4,128]{2,1,0:T(4,128)S(1)}, u32[]{:S(2)}, u32[]{:S(2)}) collective-permute-start(f32[176,4,128]{2,1,0:T(4,128)} %get-tuple-element.35), channel_id=1, source_target_pairs={{1,0},{2,1},{3,2},{4,3},{5,4},{6,5},{7,6},{9,8},{10,9},{11,10},{12... | collective-permute-start | bytes 1081352 | tf_op jit(solution)/shard_map/ppermute | solution.py:557
  15.2 0.1 reshape.200
  15.3 0.0 copy-done.16
  15.3 0.1 concatenate.3.table
  15.4 0.0 copy-start.10
  15.4 0.0 collective-permute-done.1.hi_ref
  15.4 0.0 copy-done.9
  15.4 1.6 %tile_kernel.1 = f32[32,4,8,128]{3,2,1,0:T(8,128)} custom-call(s32[23]{0:T(128)S(1)} %concatenate.3.table, f32[12,4,64]{2,1,0:T(4,128)S(1)} %bitcast.29, f32[4,128]{1,0:T(4,128)S(1)} %collective-permute-done.lo_ref, f32[4,128]{1,0:T(4,128)S(1)} %collective-permute-done.1.hi_ref), custom_call_target="tpu_custom_call" | custom-call | flops 1000000 | bytes 540672 | tf_op jit(solution)/shard_map/tile_kernel/pallas_call | solution.py:464
  17.0 7.6 %all-to-all-start = ((f32[32,4,8,128]{3,2,1,0:T(8,128)}), f32[32,4,8,128]{3,2,1,0:T(8,128)S(1)}, u32[]{:S(2)}, u32[]{:S(2)}) async-start(f32[32,4,8,128]{3,2,1,0:T(8,128)} %tile_kernel.1), calls=%async_computation | async-start | bytes 1048576 | tf_op jit(solution)/shard_map/all_to_all | solution.py:567
  24.6 0.0 copy-start.6
  24.7 0.0 copy-start.13
  24.7 0.0 collective-permute-done.2.lo_ref
  24.7 0.0 copy-start.17
  24.7 1.4 %collective-permute-done.3.hi_ref = f32[176,4,128]{2,1,0:T(4,128)S(1)} collective-permute-done((f32[176,4,128]{2,1,0:T(4,128)}, f32[176,4,128]{2,1,0:T(4,128)S(1)}, u32[]{:S(2)}, u32[]{:S(2)}) %collective-permute-start.3) | collective-permute-done | bytes 360480 | tf_op jit(solution)/shard_map/ppermute | solution.py:557
  26.1 0.0 copy-done.10
  26.1 0.0 copy-done.17
  26.1 0.0 copy-start.18
  26.1 0.7 copy-done.18
  26.8 4.4 %extend_kernel.1 = (f32[3,3,8,32,128]{4,3,2,1,0:T(8,128)}, f32[3,3,8,32,128]{4,3,2,1,0:T(8,128)}, f32[3,8,32,128]{3,2,1,0:T(8,128)}, f32[8,32,128]{2,1,0:T(8,128...) custom-call(s32[23]{0:T(128)} %copy-done.10, f32[3,3,8,24,128]{4,3,2,1,0:T(8,128)} %e_ref.1, ...), custom_call_target="tpu_custom_call" | custom-call | flops 99999997952 | bytes 6021120 | tf_op jit(solution)/shard_map/extend_kernel/pallas_call | solution.py:464
  31.3 2.9 %all-to-all-done = f32[32,4,8,128]{3,2,1,0:T(8,128)S(1)} async-done(((f32[32,4,8,128]{3,2,1,0:T(8,128)}), f32[32,4,8,128]{3,2,1,0:T(8,128)S(1)}, u32[]{:S(2)}, u32[]{:S(2)}) %all-to-all-start) | async-done | bytes 524320 | tf_op jit(solution)/shard_map/all_to_all | solution.py:567
  34.2 0.0 copy-start.11
  34.2 0.7 copy-done.11
  34.9 0.6 select_kernel.1
  35.4 0.6 constant_dynamic-update-slice_fusion
  36.0 16.3 %collective-permute-start.4 = (f32[34,8,128]{2,1,0:T(8,128)}, f32[34,8,128]{2,1,0:T(8,128)S(1)}, u32[]{:S(2)}, u32[]{:S(2)}) collective-permute-start(f32[34,8,128]{2,1,0:T(8,128)} %constant_dynamic-update-slice_fusion), channel_id=1, source_target_pairs={{0,504},{8,16},{16,8},{24,32},{32,24},{40,48},{48,40},{56,64},{64,... | collective-permute-start | bytes 417800 | tf_op jit(solution)/shard_map/ppermute | solution.py:593
  52.4 1.9 %collective-permute-start.5 = (f32[28,8,128]{2,1,0:T(8,128)}, f32[28,8,128]{2,1,0:T(8,128)S(1)}, u32[]{:S(2)}, u32[]{:S(2)}) collective-permute-start(f32[28,8,128]{2,1,0:T(8,128)} %get-tuple-element.39), channel_id=1, source_target_pairs={{0,8},{8,0},{16,24},{24,16},{32,40},{40,32},{48,56},{56,48},{64,72... | collective-permute-start | bytes 344072 | tf_op jit(solution)/shard_map/ppermute | solution.py:580
  54.3 0.0 copy-done.6
  54.3 0.0 copy-done.13
  54.3 0.0 copy-start
  54.3 1.0 copy-done
  55.3 1.3 %copy-done.2 = f32[3,3,8,32,128]{4,3,2,1,0:T(8,128)S(1)} copy-done((f32[3,3,8,32,128]{4,3,2,1,0:T(8,128)S(1)}, f32[3,3,8,32,128]{4,3,2,1,0:T(8,128)}, u32[]{:S(2)}) %copy-start.2) | copy-done | bytes 1179672
  56.6 1.3 %copy-done.4 = f32[3,3,8,32,128]{4,3,2,1,0:T(8,128)S(1)} copy-done((f32[3,3,8,32,128]{4,3,2,1,0:T(8,128)S(1)}, f32[3,3,8,32,128]{4,3,2,1,0:T(8,128)}, u32[]{:S(2)}) %copy-start.4) | copy-done | bytes 1179672
  57.9 0.9 copy-done.7
  58.8 0.3 stage_kernel.1
  59.1 0.0 collective-permute-done.5.near_ref
  59.1 5.0 %collective-permute-done.4.far_ref = f32[34,8,128]{2,1,0:T(8,128)S(1)} collective-permute-done((f32[34,8,128]{2,1,0:T(8,128)}, f32[34,8,128]{2,1,0:T(8,128)S(1)}, u32[]{:S(2)}, u32[]{:S(2)}) %collective-permute-start.4) | collective-permute-done | bytes 139296 | tf_op jit(solution)/shard_map/ppermute | solution.py:593
  64.1 0.0 copy-done.12
  64.1 0.0 copy-done.14
  64.2 0.0 copy-start.5
  64.2 0.0 copy-start.8
  64.2 2.5 %trace_kernel.1 = (f32[63,8,128]{2,1,0:T(8,128)S(1)}, f32[63,8,128]{2,1,0:T(8,128)S(1)}) custom-call(s32[23]{0:T(128)S(1)} %copy-done.12, f32[2]{0:T(128)S(1)} %copy-done.14, f32[6,8,128]{2,1,0:T(8,128)S(1)} %get-tuple-element.33.mine_ref, f32[128,256]{1,0:T(8,128)S(1)} %get-tuple-element.44.wz_ref, f32[32,16]{1,0:T(8,128)S(1)} %get-tuple-element.45.wy_ref, ...), custom_call_target="tpu_custom_call" | custom-call | flops 10000000 | bytes 10000000 | tf_op jit(solution)/shard_map/trace_kernel/pallas_call | solution.py:482
  66.7 15.4 %collective-permute-start.6 = (f32[63,8,128]{2,1,0:T(8,128)S(1)}, f32[63,8,128]{2,1,0:T(8,128)S(1)}, u32[]{:S(2)}, u32[]{:S(2)}) collective-permute-start(f32[63,8,128]{2,1,0:T(8,128)S(1)} %get-tuple-element.50), channel_id=1, source_target_pairs={{8,16},{16,8},{24,32},{32,24},{40,48},{48,40},{56,64},{64,56},{72,... | collective-permute-start | bytes 774152 | tf_op jit(solution)/shard_map/ppermute | solution.py:620
  82.1 1.9 %collective-permute-start.7 = (f32[63,8,128]{2,1,0:T(8,128)S(1)}, f32[63,8,128]{2,1,0:T(8,128)S(1)}, u32[]{:S(2)}, u32[]{:S(2)}) collective-permute-start(f32[63,8,128]{2,1,0:T(8,128)S(1)} %get-tuple-element.51), channel_id=1, source_target_pairs={{0,8},{8,0},{16,24},{24,16},{32,40},{40,32},{48,56},{56,48},{64,72... | collective-permute-start | bytes 774152 | tf_op jit(solution)/shard_map/ppermute | solution.py:619
  84.1 0.0 copy-done.1
  84.1 0.0 copy-done.3
  84.1 0.0 copy-done.5
  84.1 0.0 copy-done.8
  84.1 3.2 %inner_kernel.1 = (f32[3,3,8,32,128]{4,3,2,1,0:T(8,128)S(1)}, f32[3,3,8,32,128]{4,3,2,1,0:T(8,128)S(1)}, f32[3,10,32,128]{3,2,1,0:T(8,128)S(1)}) custom-call(s32[23]{0:T(128)S(1)} %copy-done.12, f32[2]{0:T(128)S(1)} %copy-done.14, f32[6,8,128]{2,1,0:T(8,128)S(1)} %get-tuple-element.33.mine_ref, f32[128,256]{1,0:T(8,128)S(1)} %copy-done.6, ...), custom_call_target="tpu_custom_call" | custom-call | flops 10000000 | bytes 6146048 | tf_op jit(solution)/shard_map/inner_kernel/pallas_call | solution.py:464
  87.3 15.7 %collective-permute-done.6.far_ref = f32[63,8,128]{2,1,0:T(8,128)S(1)} collective-permute-done((f32[63,8,128]{2,1,0:T(8,128)S(1)}, f32[63,8,128]{2,1,0:T(8,128)S(1)}, u32[]{:S(2)}, u32[]{:S(2)}) %collective-permute-start.6) | collective-permute-done | bytes 258080 | tf_op jit(solution)/shard_map/ppermute | solution.py:620
  103.0 0.0 collective-permute-done.7.near_ref
  103.0 3.0 %window_kernel.1 = (f32[3,3,8,24,128]{4,3,2,1,0:T(8,128)}, f32[3,3,8,24,128]{4,3,2,1,0:T(8,128)}) custom-call(s32[23]{0:T(128)S(1)} %copy-done.12, f32[3,10,32,128]{3,2,1,0:T(8,128)S(1)} %get-tuple-element.43.c_ref, f32[63,8,128]{2,1,0:T(8,128)S(1)} %collective-permute-done.6.far_ref, f32[63,8,128]{2,1,0:T(8,128)S(1)} %collective-permute-done.7.near_ref, ...), custom_call_target="tpu_custom_call" | custom-call | flops 10000000 | bytes 10000000 | tf_op jit(solution)/shard_map/window_kernel/pallas_call | solution.py:482
  (12 shorter events, 0.1 us)
Async XLA Ops:
  0.6 8.3 %copy-start.15 = (s32[64]{0:T(128)S(1)}, s32[64]{0:T(128)}, u32[]{:S(2)}) copy-start(s32[64]{0:T(128)} %param.14) | copy-start | bytes 772
  0.6 14.7 %copy-start.16 = (s32[6]{0:T(128)S(1)}, s32[6]{0:T(128)}, u32[]{:S(2)}) copy-start(s32[6]{0:T(128)} %param.15) | copy-start | bytes 76
  0.7 14.8 %copy-start.9 = (f32[4,12,64]{2,0,1:T(4,128)S(1)}, f32[4,12,64]{2,0,1:T(4,128)}, u32[]{:S(2)}) copy-start(f32[4,12,64]{2,0,1:T(4,128)} %param.13) | copy-start | bytes 36868
  2.9 6.4 %collective-permute-start = (f32[4,128]{1,0:T(4,128)}, f32[4,128]{1,0:T(4,128)S(1)}, u32[]{:S(2)}, u32[]{:S(2)}) collective-permute-start(f32[4,128]{1,0:T(4,128)} %get-tuple-element.28), channel_id=1, source_target_pairs={{0,1},{1,2},{2,3},{3,4},{4,5},{5,6},{6,7},{8,9},{9,10},{10,11},{11... | collective-permute-start | bytes 6152 | tf_op jit(solution)/shard_map/ppermute | solution.py:553
  6.7 8.7 %collective-permute-start.1 = (f32[4,128]{1,0:T(4,128)}, f32[4,128]{1,0:T(4,128)S(1)}, u32[]{:S(2)}, u32[]{:S(2)}) collective-permute-start(f32[4,128]{1,0:T(4,128)} %get-tuple-element.32), channel_id=1, source_target_pairs={{1,0},{2,1},{3,2},{4,3},{5,4},{6,5},{7,6},{9,8},{10,9},{11,10},{12... | collective-permute-start | bytes 6152 | tf_op jit(solution)/shard_map/ppermute | solution.py:554
  9.3 15.4 %collective-permute-start.2 = (f32[176,4,128]{2,1,0:T(4,128)}, f32[176,4,128]{2,1,0:T(4,128)S(1)}, u32[]{:S(2)}, u32[]{:S(2)}) collective-permute-start(f32[176,4,128]{2,1,0:T(4,128)} %get-tuple-element.34), channel_id=1, source_target_pairs={{0,1},{1,2},{2,3},{3,4},{4,5},{5,6},{6,7},{8,9},{9,10},{10,11},{11... | collective-permute-start | bytes 1081352 | tf_op jit(solution)/shard_map/ppermute | solution.py:556
  13.1 13.0 %collective-permute-start.3 = (f32[176,4,128]{2,1,0:T(4,128)}, f32[176,4,128]{2,1,0:T(4,128)S(1)}, u32[]{:S(2)}, u32[]{:S(2)}) collective-permute-start(f32[176,4,128]{2,1,0:T(4,128)} %get-tuple-element.35), channel_id=1, source_target_pairs={{1,0},{2,1},{3,2},{4,3},{5,4},{6,5},{7,6},{9,8},{10,9},{11,10},{12... | collective-permute-start | bytes 1081352 | tf_op jit(solution)/shard_map/ppermute | solution.py:557
  15.4 10.7 %copy-start.10 = (s32[23]{0:T(128)}, s32[23]{0:T(128)S(1)}, u32[]{:S(2)}) copy-start(s32[23]{0:T(128)S(1)} %concatenate.3.table) | copy-start | bytes 280
  17.0 17.2 %all-to-all-start = ((f32[32,4,8,128]{3,2,1,0:T(8,128)}), f32[32,4,8,128]{3,2,1,0:T(8,128)S(1)}, u32[]{:S(2)}, u32[]{:S(2)}) async-start(f32[32,4,8,128]{3,2,1,0:T(8,128)} %tile_kernel.1), calls=%async_computation | async-start | bytes 1048576 | tf_op jit(solution)/shard_map/all_to_all | solution.py:567
  24.6 29.7 %copy-start.6 = (f32[128,256]{1,0:T(8,128)S(1)}, f32[128,256]{1,0:T(8,128)}, u32[]{:S(2)}) copy-start(f32[128,256]{1,0:T(8,128)} %constant.96.clone.wz_ref.refs_4_) | copy-start | bytes 393220
  24.7 29.7 %copy-start.13 = (f32[32,16]{1,0:T(8,128)S(1)}, f32[32,16]{1,0:T(8,128)}, u32[]{:S(2)}) copy-start(f32[32,16]{1,0:T(8,128)} %constant.97.clone.wy_ref.refs_5_) | copy-start | bytes 6148
  24.7 1.4 %copy-start.17 = (f32[176,4,128]{2,1,0:T(4,128)}, f32[176,4,128]{2,1,0:T(4,128)S(1)}, u32[]{:S(2)}) copy-start(f32[176,4,128]{2,1,0:T(4,128)S(1)} %collective-permute-done.2.lo_ref) | copy-start | bytes 1081348
  26.1 0.7 copy-start.18
  34.2 0.7 copy-start.11
  36.0 28.1 %collective-permute-start.4 = (f32[34,8,128]{2,1,0:T(8,128)}, f32[34,8,128]{2,1,0:T(8,128)S(1)}, u32[]{:S(2)}, u32[]{:S(2)}) collective-permute-start(f32[34,8,128]{2,1,0:T(8,128)} %constant_dynamic-update-slice_fusion), channel_id=1, source_target_pairs={{0,504},{8,16},{16,8},{24,32},{32,24},{40,48},{48,40},{56,64},{64,... | collective-permute-start | bytes 417800 | tf_op jit(solution)/shard_map/ppermute | solution.py:593
  52.4 6.7 %collective-permute-start.5 = (f32[28,8,128]{2,1,0:T(8,128)}, f32[28,8,128]{2,1,0:T(8,128)S(1)}, u32[]{:S(2)}, u32[]{:S(2)}) collective-permute-start(f32[28,8,128]{2,1,0:T(8,128)} %get-tuple-element.39), channel_id=1, source_target_pairs={{0,8},{8,0},{16,24},{24,16},{32,40},{40,32},{48,56},{56,48},{64,72... | collective-permute-start | bytes 344072 | tf_op jit(solution)/shard_map/ppermute | solution.py:580
  54.3 1.0 copy-start
  55.3 1.3 %copy-start.2 = (f32[3,3,8,32,128]{4,3,2,1,0:T(8,128)S(1)}, f32[3,3,8,32,128]{4,3,2,1,0:T(8,128)}, u32[]{:S(2)}) copy-start(f32[3,3,8,32,128]{4,3,2,1,0:T(8,128)} %get-tuple-element.40.ee_ref.refs_0_) | copy-start | bytes 3538948
  56.6 1.3 %copy-start.4 = (f32[3,3,8,32,128]{4,3,2,1,0:T(8,128)S(1)}, f32[3,3,8,32,128]{4,3,2,1,0:T(8,128)}, u32[]{:S(2)}) copy-start(f32[3,3,8,32,128]{4,3,2,1,0:T(8,128)} %get-tuple-element.41.h1_ref.refs_1_) | copy-start | bytes 3538948
  57.9 0.9 copy-start.7
  58.8 5.4 %copy-start.12 = (s32[23]{0:T(128)S(1)}, s32[23]{0:T(128)}, u32[]{:S(2)}) copy-start(s32[23]{0:T(128)} %copy-done.10) | copy-start | bytes 280
  58.8 5.4 %copy-start.14 = (f32[2]{0:T(128)S(1)}, f32[2]{0:T(128)}, u32[]{:S(2)}) copy-start(f32[2]{0:T(128)} %levels.3) | copy-start | bytes 28
  64.1 19.9 %copy-start.1 = (f32[3,8,32,128]{3,2,1,0:T(8,128)S(1)}, f32[3,8,32,128]{3,2,1,0:T(8,128)}, u32[]{:S(2)}) copy-start(f32[3,8,32,128]{3,2,1,0:T(8,128)} %get-tuple-element.42.jj_ref.refs_2_) | copy-start | bytes 1179652
  64.1 19.9 %copy-start.3 = (f32[3,3,8,32,128]{4,3,2,1,0:T(8,128)S(1)}, f32[3,3,8,32,128]{4,3,2,1,0:T(8,128)}, u32[]{:S(2)}) copy-start(f32[3,3,8,32,128]{4,3,2,1,0:T(8,128)} %get-tuple-element.40.ee_ref.refs_0_) | copy-start | bytes 3538948
  64.2 19.9 %copy-start.5 = (f32[3,3,8,32,128]{4,3,2,1,0:T(8,128)S(1)}, f32[3,3,8,32,128]{4,3,2,1,0:T(8,128)}, u32[]{:S(2)}) copy-start(f32[3,3,8,32,128]{4,3,2,1,0:T(8,128)} %get-tuple-element.41.h1_ref.refs_1_) | copy-start | bytes 3538948
  64.2 19.9 %copy-start.8 = (f32[8,32,128]{2,1,0:T(8,128)S(1)}, f32[8,32,128]{2,1,0:T(8,128)}, u32[]{:S(2)}) copy-start(f32[8,32,128]{2,1,0:T(8,128)} %get-tuple-element.36.mm_ref.refs_3_) | copy-start | bytes 393220
  66.7 36.3 %collective-permute-start.6 = (f32[63,8,128]{2,1,0:T(8,128)S(1)}, f32[63,8,128]{2,1,0:T(8,128)S(1)}, u32[]{:S(2)}, u32[]{:S(2)}) collective-permute-start(f32[63,8,128]{2,1,0:T(8,128)S(1)} %get-tuple-element.50), channel_id=1, source_target_pairs={{8,16},{16,8},{24,32},{32,24},{40,48},{48,40},{56,64},{64,56},{72,... | collective-permute-start | bytes 774152 | tf_op jit(solution)/shard_map/ppermute | solution.py:620
  82.1 20.9 %collective-permute-start.7 = (f32[63,8,128]{2,1,0:T(8,128)S(1)}, f32[63,8,128]{2,1,0:T(8,128)S(1)}, u32[]{:S(2)}, u32[]{:S(2)}) collective-permute-start(f32[63,8,128]{2,1,0:T(8,128)S(1)} %get-tuple-element.51), channel_id=1, source_target_pairs={{0,8},{8,0},{16,24},{24,16},{32,40},{40,32},{48,56},{56,48},{64,72... | collective-permute-start | bytes 774152 | tf_op jit(solution)/shard_map/ppermute | solution.py:619
